TPU v7x, 32 devices: a whole 2x2x4 slice. The times are simulated.
32 devices in a mesh: dp: 4 (over y, core), mp: 8 (over z, x).
Axes of the slice: x: 2, y: 2, z: 4, core: 2. Of those that a mesh axis runs over, the one named last changes fastest.
Arguments:
- char_ids: int32 [8960, 50], P(('dp', 'mp')), may hold values from 0 to 261
- doc_lengths: int32 [40], replicated, may hold values from 1040 to 1620, as said below
- window_doc: int32 [448], P('dp'), may hold values from 0 to 39, as said below
- window_offset: int32 [448], P('dp'), may hold values from 1000 to 1619, as said below
- char_table: float32 [262, 16], replicated, may hold values from -6 to 6
- conv_weight: float32 [7, 16, 2048], P(None, None, 'dp'), may hold values from -0.5 to 0.5
- conv_bias: float32 [2048], replicated, may hold values from -3 to 3
- highway_weight: float32 [2, 2048, 4096], P(None, 'dp'), may hold values from -0.125 to 0.125
- highway_bias: float32 [2, 4096], replicated, may hold values from -3 to 3
- proj_weight: float32 [2048, 512], P('dp'), may hold values from -0.125 to 0.125
- proj_bias: float32 [512], replicated, may hold values from -3 to 3
- lstm_input_weight: float32 [2, 512, 16384], P(None, 'dp', 'mp'), may hold values from -0.25 to 0.25
- lstm_state_weight: float32 [2, 512, 16384], P(None, 'dp', 'mp'), may hold values from -0.25 to 0.25
- lstm_bias: float32 [2, 16384], P(None, 'mp'), may hold values from -3 to 3
- lstm_proj: float32 [2, 4096, 512], P(None, 'mp', 'dp'), may hold values from -0.25 to 0.25
- init_cell: float32 [2, 448, 4096], P(None, 'dp', 'mp'), may hold values from -6 to 6
- init_hidden: bfloat16 [2, 448, 512], P(None, 'dp'), may hold values from -3 to 3
- cotangent: bfloat16 [448, 20, 1024], P('dp'), may hold values from -6 to 6
Outputs:
- hidden: bfloat16 [448, 20, 1024], P('dp')
- grad_char_table: float32 [262, 16], replicated
- grad_conv_weight: float32 [7, 16, 2048], P(None, None, 'dp')
- grad_conv_bias: float32 [2048], replicated
- grad_highway_weight: float32 [2, 2048, 4096], P(None, 'dp')
- grad_highway_bias: float32 [2, 4096], replicated
- grad_proj_weight: float32 [2048, 512], P('dp')
- grad_proj_bias: float32 [512], replicated
- grad_lstm_input: float32 [2, 512, 16384], P(None, 'dp', 'mp')
- grad_lstm_state: float32 [2, 512, 16384], P(None, 'dp', 'mp')
- grad_lstm_bias: float32 [2, 16384], P(None, 'mp')
- grad_lstm_proj: float32 [2, 4096, 512], P(None, 'mp', 'dp')
Inputs may be any that keep to these rules, and one draw needn't show every extreme that they name: `doc_lengths`: one document of each draw has length 1040 and one has length 1620. `window_doc`: a document number below 40. doc_lengths[window_doc] - window_offset lies between 1 and 40, and both ends occur in every draw.
All inputs are finite; a program needn't handle non-finite values.
Results may differ from a plain program's by a relative error of at most 0.025.
Values may be sent and summed in bfloat16 or wider, within the bound.
A program may use at most 448 MiB of HBM per device.

v0:
```python
import math

import jax
import jax.numpy as jnp
from jax import lax
from jax.sharding import PartitionSpec as P

VOCAB = 262
CHARS = 50
CDIM = 16
TAPS = 7
FILTERS = 2048
PROJ = 512
UNIT_BLOCK = 128
WIN = 20
GATES = 16384


CLIP = 3.0


def filter_widths(count):
    unit_size = count // 64
    index_row = jnp.arange(count)
    widths = jnp.ones((count,), jnp.int32)
    for exponent in range(6):
        widths = widths + (index_row >= unit_size * (1 << exponent)).astype(jnp.int32)
    return widths


def split_gates(pre_act, unit_count):
    leading = pre_act.shape[:-1]
    shaped = pre_act.reshape(leading + (unit_count // UNIT_BLOCK, 4, UNIT_BLOCK))
    return [shaped[..., gate_index, :].reshape(leading + (unit_count,)) for gate_index in range(4)]


def join_gates(gate_parts, unit_count):
    leading = gate_parts[0].shape[:-1]
    stacked = jnp.stack(
        [
            part_value.reshape(leading + (unit_count // UNIT_BLOCK, UNIT_BLOCK))
            for part_value in gate_parts
        ],
        axis=-2,
    )
    return stacked.reshape(leading + (4 * unit_count,))


def silu_slope(value):
    sigma = jax.nn.sigmoid(value)
    return sigma * (1.0 + value * (1.0 - sigma))


def char_columns(id_block, table_low):
    flat_ids = id_block.reshape(-1)
    one_hot = flat_ids[:, None] == jnp.arange(VOCAB)[None, :]
    char_vecs = jnp.dot(
        one_hot.astype(jnp.bfloat16), table_low, preferred_element_type=jnp.float32
    ).astype(jnp.bfloat16)
    char_vecs = char_vecs.reshape(id_block.shape[0], CHARS, CDIM)
    padded = jnp.pad(char_vecs, ((0, 0), (0, TAPS - 1), (0, 0)))
    columns = jnp.concatenate(
        [padded[:, tap_index : tap_index + CHARS, :] for tap_index in range(TAPS)], axis=2
    )
    return (one_hot, columns.reshape(-1, TAPS * CDIM))


def shards(
    char_ids,
    doc_lengths,
    window_doc,
    window_offset,
    char_table,
    conv_weight,
    conv_bias,
    highway_weight,
    highway_bias,
    proj_weight,
    proj_bias,
    lstm_input_weight,
    lstm_state_weight,
    lstm_bias,
    lstm_proj,
    init_cell,
    init_hidden,
    cotangent,
):
    tok_share = char_ids.shape[0]
    row_count = window_doc.shape[0]
    group_tokens = row_count * WIN
    cell_local = init_cell.shape[2]
    gate_local = lstm_bias.shape[1]
    mp_index = lax.axis_index("mp")
    dp_index = lax.axis_index("dp")
    dp_width = conv_weight.shape[2]
    token_start = mp_index * tok_share
    high_low = highway_weight.astype(jnp.bfloat16)
    conv_full, high_full, proj_full = (
        lax.all_gather(conv_weight.astype(jnp.bfloat16), "dp", axis=2, tiled=True),
        lax.all_gather(high_low, "dp", axis=1, tiled=True),
        lax.all_gather(proj_weight.astype(jnp.bfloat16), "dp", axis=0, tiled=True),
    )
    input_full, state_full, lproj_full = (
        lax.all_gather(lstm_input_weight.astype(jnp.bfloat16), "dp", axis=1, tiled=True),
        lax.all_gather(lstm_state_weight.astype(jnp.bfloat16), "dp", axis=1, tiled=True),
        lax.all_gather(lstm_proj.astype(jnp.bfloat16), "dp", axis=2, tiled=True),
    )
    widths = filter_widths(FILTERS)
    tap_mask = jnp.arange(TAPS)[:, None] < widths[None, :]
    conv_matrix = (conv_full * tap_mask[:, None, :].astype(jnp.bfloat16)).reshape(
        TAPS * CDIM, FILTERS
    )
    valid_mask = (jnp.arange(CHARS)[:, None] <= CHARS - widths[None, :]).astype(jnp.float32)
    counts = (CHARS + 1 - widths).astype(jnp.float32)
    table_low = char_table.astype(jnp.bfloat16)
    block_size = math.gcd(tok_share, WIN)
    id_blocks = char_ids.reshape(tok_share // block_size, block_size, CHARS)

    def pool_block(id_block):
        one_hot, columns = char_columns(id_block, table_low)
        conv_out = jnp.dot(columns, conv_matrix, preferred_element_type=jnp.float32).reshape(
            block_size, CHARS, FILTERS
        )
        exp_total = jnp.sum(jnp.exp(conv_out) * valid_mask, axis=1)
        return jnp.log(exp_total / counts)

    pooled = lax.map(pool_block, id_blocks).reshape(tok_share, FILTERS)
    pre_pool = pooled + conv_bias
    layer_value = jax.nn.silu(pre_pool)
    kept_inputs = []
    kept_mixed = []
    for layer_index in range(2):
        mixed = (
            jnp.dot(
                layer_value.astype(jnp.bfloat16),
                high_full[layer_index],
                preferred_element_type=jnp.float32,
            )
            + highway_bias[layer_index]
        )
        kept_inputs.append(layer_value)
        kept_mixed.append(mixed)
        gate_value = jax.nn.sigmoid(mixed[:, FILTERS:])
        layer_value = gate_value * layer_value + (1.0 - gate_value) * jax.nn.silu(
            mixed[:, :FILTERS]
        )
    top_low = layer_value.astype(jnp.bfloat16)
    embed_local = jnp.dot(top_low, proj_full, preferred_element_type=jnp.float32) + proj_bias
    embed_term = lax.dynamic_update_slice_in_dim(
        jnp.zeros((group_tokens, PROJ), jnp.float32), embed_local, token_start, 0
    )
    embed_sum = lax.psum(embed_term.astype(jnp.bfloat16), "mp")
    input_pre = (
        jnp.einsum("np,dpg->dng", embed_sum, input_full, preferred_element_type=jnp.float32)
        + lstm_bias[:, None, :]
    )
    input_pre = input_pre.reshape(2, row_count, WIN, gate_local)
    scan_input = jnp.transpose(jnp.stack([input_pre[0], input_pre[1][:, ::-1]]), (2, 0, 1, 3))
    doc_index = jnp.arange(doc_lengths.shape[0])
    chosen_len = jnp.sum(
        jnp.where(window_doc[:, None] == doc_index[None, :], doc_lengths[None, :], 0), axis=1
    )
    reset_at = chosen_len - window_offset
    step_ids = jnp.arange(WIN)
    keep_fwd = (step_ids[None, :] != reset_at[:, None]).astype(jnp.float32)
    keep_bwd = (step_ids[None, :] != reset_at[:, None] - 1).astype(jnp.float32)[:, ::-1]
    keep_masks = jnp.transpose(jnp.stack([keep_fwd, keep_bwd]), (2, 0, 1))

    def forward_step(carry, inputs):
        cell_state, hidden_state = carry
        step_pre, keep_now = inputs
        keep_cols = keep_now[:, :, None]
        cell_prev = cell_state * keep_cols
        hidden_prev = hidden_state * keep_cols.astype(jnp.bfloat16)
        pre_act = step_pre + jnp.einsum(
            "drp,dpg->drg", hidden_prev, state_full, preferred_element_type=jnp.float32
        )
        gate_in, gate_forget, gate_cand, gate_out = split_gates(pre_act, cell_local)
        cell_new = CLIP * jnp.tanh(
            (
                jax.nn.sigmoid(gate_forget) * cell_prev
                + jax.nn.sigmoid(gate_in) * jnp.tanh(gate_cand)
            )
            / CLIP
        )
        cell_low = (jax.nn.sigmoid(gate_out) * jnp.tanh(cell_new)).astype(jnp.bfloat16)
        partial_sum = jnp.einsum(
            "drc,dcp->drp", cell_low, lproj_full, preferred_element_type=jnp.float32
        )
        stat_kept = lax.psum(partial_sum, "mp")
        hidden_new = (CLIP * jnp.tanh(stat_kept / CLIP)).astype(jnp.bfloat16)
        return (
            (cell_new, hidden_new),
            (hidden_new, pre_act, cell_prev, cell_new, cell_low, hidden_prev, stat_kept),
        )

    carry_end, kept_steps = lax.scan(
        forward_step, (init_cell, init_hidden), (scan_input, keep_masks)
    )
    states, pre_acts, cell_prevs, cell_news, cell_lows, hidden_prevs, stat_kepts = kept_steps
    hidden = jnp.concatenate(
        [jnp.transpose(states[:, 0], (1, 0, 2)), jnp.transpose(states[::-1, 1], (1, 0, 2))], axis=-1
    )
    cot_float = cotangent.astype(jnp.float32)
    out_grads = jnp.transpose(
        jnp.stack([cot_float[:, :, :PROJ], cot_float[:, ::-1, PROJ:]]), (2, 0, 1, 3)
    )

    def backward_step(carry, inputs):
        grad_hidden, grad_cell = carry
        out_grad, keep_now, pre_act, cell_prev, cell_new, stat_kept = inputs
        grad_result = out_grad + grad_hidden
        tanh_stat = jnp.tanh(stat_kept / CLIP)
        grad_stat = (grad_result * (1.0 - tanh_stat * tanh_stat)).astype(jnp.bfloat16)
        grad_cellout = jnp.einsum(
            "drp,dcp->drc", grad_stat, lproj_full, preferred_element_type=jnp.float32
        )
        gate_in, gate_forget, gate_cand, gate_out = split_gates(pre_act, cell_local)
        input_gate = jax.nn.sigmoid(gate_in)
        forget_gate = jax.nn.sigmoid(gate_forget)
        candidate = jnp.tanh(gate_cand)
        output_gate = jax.nn.sigmoid(gate_out)
        tanh_cell = jnp.tanh(cell_new)
        grad_total = grad_cellout * output_gate * (1.0 - tanh_cell * tanh_cell) + grad_cell
        grad_inner = grad_total * (1.0 - cell_new / CLIP * (cell_new / CLIP))
        grad_pre = join_gates(
            [
                grad_inner * candidate * input_gate * (1.0 - input_gate),
                grad_inner * cell_prev * forget_gate * (1.0 - forget_gate),
                grad_inner * input_gate * (1.0 - candidate * candidate),
                grad_cellout * tanh_cell * output_gate * (1.0 - output_gate),
            ],
            cell_local,
        ).astype(jnp.bfloat16)
        back_partial = jnp.einsum(
            "drg,dpg->drp", grad_pre, state_full, preferred_element_type=jnp.float32
        )
        back_sum = lax.psum(back_partial.astype(jnp.bfloat16), "mp").astype(jnp.float32)
        keep_cols = keep_now[:, :, None]
        return ((back_sum * keep_cols, grad_inner * forget_gate * keep_cols), (grad_pre, grad_stat))

    zero_hidden = jnp.zeros(out_grads.shape[1:], jnp.float32)
    zero_cell = jnp.zeros(init_cell.shape, jnp.float32)
    carry_back, grad_steps = lax.scan(
        backward_step,
        (zero_hidden, zero_cell),
        (out_grads, keep_masks, pre_acts, cell_prevs, cell_news, stat_kepts),
        reverse=True,
    )
    grad_pres, grad_stats = grad_steps
    grad_state = jnp.einsum(
        "wdrp,wdrg->dpg", hidden_prevs, grad_pres, preferred_element_type=jnp.float32
    )
    grad_lproj = jnp.einsum(
        "wdrc,wdrp->dcp", cell_lows, grad_stats, preferred_element_type=jnp.float32
    )
    token_pres = jnp.stack(
        [jnp.transpose(grad_pres[:, 0], (1, 0, 2)), jnp.transpose(grad_pres[::-1, 1], (1, 0, 2))]
    ).reshape(2, group_tokens, gate_local)
    grad_input = jnp.einsum(
        "np,dng->dpg", embed_sum, token_pres, preferred_element_type=jnp.float32
    )
    grad_bias = jnp.sum(token_pres.astype(jnp.float32), axis=1)
    embed_partial = jnp.einsum(
        "dng,dpg->np", token_pres, input_full, preferred_element_type=jnp.float32
    )
    grad_embed_all = lax.psum(embed_partial.astype(jnp.bfloat16), "mp")
    grad_embed_local = lax.dynamic_slice_in_dim(grad_embed_all, token_start, tok_share, 0)
    grad_input, grad_state, grad_lproj = (
        lax.psum_scatter(
            grad_input.astype(jnp.bfloat16), "dp", scatter_dimension=1, tiled=True
        ).astype(jnp.float32),
        lax.psum_scatter(
            grad_state.astype(jnp.bfloat16), "dp", scatter_dimension=1, tiled=True
        ).astype(jnp.float32),
        lax.psum_scatter(
            grad_lproj.astype(jnp.bfloat16), "dp", scatter_dimension=2, tiled=True
        ).astype(jnp.float32),
    )
    grad_pb = jnp.sum(grad_embed_local.astype(jnp.float32), axis=0)
    grad_hw = [None, None]
    grad_hb = [None, None]
    grad_pw = jnp.dot(top_low.T, grad_embed_local, preferred_element_type=jnp.float32)
    grad_layer = jnp.dot(grad_embed_local, proj_full.T, preferred_element_type=jnp.float32)
    for layer_index in (1, 0):
        layer_in = kept_inputs[layer_index]
        mixed = kept_mixed[layer_index]
        transform = mixed[:, :FILTERS]
        gate_value = jax.nn.sigmoid(mixed[:, FILTERS:])
        grad_gate = (
            grad_layer * (layer_in - jax.nn.silu(transform)) * gate_value * (1.0 - gate_value)
        )
        grad_trans = grad_layer * (1.0 - gate_value) * silu_slope(transform)
        grad_mixed = jnp.concatenate([grad_trans, grad_gate], axis=1).astype(jnp.bfloat16)
        grad_hw[layer_index] = jnp.dot(
            layer_in.astype(jnp.bfloat16).T, grad_mixed, preferred_element_type=jnp.float32
        )
        grad_hb[layer_index] = jnp.sum(grad_mixed.astype(jnp.float32), axis=0)
        grad_layer = grad_layer * gate_value + jnp.dot(
            grad_mixed, high_full[layer_index].T, preferred_element_type=jnp.float32
        )
    hw_terms = jnp.stack(grad_hw).reshape(2, FILTERS, 2, FILTERS)
    grad_pre_pool = grad_layer * silu_slope(pre_pool)
    grad_cb = jnp.sum(grad_pre_pool, axis=0)

    def conv_back(carry, inputs):
        grad_conv, grad_table = carry
        id_block, grad_block = inputs
        one_hot, columns = char_columns(id_block, table_low)
        conv_out = jnp.dot(columns, conv_matrix, preferred_element_type=jnp.float32).reshape(
            block_size, CHARS, FILTERS
        )
        exp_values = jnp.exp(conv_out) * valid_mask
        exp_total = jnp.sum(exp_values, axis=1)
        grad_conv_out = (
            (grad_block[:, None, :] * exp_values / exp_total[:, None, :])
            .astype(jnp.bfloat16)
            .reshape(block_size * CHARS, FILTERS)
        )
        grad_conv = grad_conv + jnp.dot(
            columns.T, grad_conv_out, preferred_element_type=jnp.float32
        )
        grad_columns = jnp.dot(
            grad_conv_out, conv_matrix.T, preferred_element_type=jnp.float32
        ).reshape(block_size, CHARS, TAPS, CDIM)
        grad_chars = jnp.zeros((block_size, CHARS + TAPS - 1, CDIM), jnp.float32)
        for tap_index in range(TAPS):
            grad_chars = grad_chars.at[:, tap_index : tap_index + CHARS, :].add(
                grad_columns[:, :, tap_index, :]
            )
        grad_chars = grad_chars[:, :CHARS, :].reshape(block_size * CHARS, CDIM)
        grad_table = grad_table + jnp.dot(
            one_hot.astype(jnp.float32).T, grad_chars, precision=lax.Precision.HIGHEST
        )
        return ((grad_conv, grad_table), None)

    grad_blocks = grad_pre_pool.reshape(tok_share // block_size, block_size, FILTERS)
    conv_init = (
        jnp.zeros((TAPS * CDIM, FILTERS), jnp.float32),
        jnp.zeros((VOCAB, CDIM), jnp.float32),
    )
    conv_sums, unused = lax.scan(conv_back, conv_init, (id_blocks, grad_blocks))
    grad_conv = conv_sums[0].reshape(TAPS, CDIM, FILTERS) * tap_mask[:, None, :].astype(jnp.float32)
    grad_table = conv_sums[1]
    bias_placed = lax.dynamic_update_slice_in_dim(
        jnp.zeros((2, GATES), jnp.float32), grad_bias, mp_index * gate_local, 1
    )
    grad_table, grad_conv, grad_cb, grad_hbs, grad_pb, bias_placed = lax.psum(
        (grad_table, grad_conv, grad_cb, jnp.stack(grad_hb), grad_pb, bias_placed), ("dp", "mp")
    )
    grad_lbias = lax.dynamic_slice_in_dim(bias_placed, mp_index * gate_local, gate_local, 1)
    grad_cw = lax.dynamic_slice_in_dim(grad_conv, dp_index * dp_width, dp_width, 2)
    hw_part, pw_part = (
        lax.psum_scatter(
            hw_terms.astype(jnp.bfloat16), "dp", scatter_dimension=1, tiled=True
        ).astype(jnp.float32),
        lax.psum_scatter(
            grad_pw.astype(jnp.bfloat16), "dp", scatter_dimension=0, tiled=True
        ).astype(jnp.float32),
    )
    hw_sum, grad_pws = (
        lax.psum(hw_part.astype(jnp.bfloat16), "mp").astype(jnp.float32),
        lax.psum(pw_part.astype(jnp.bfloat16), "mp").astype(jnp.float32),
    )
    grad_hws = hw_sum.reshape(2, hw_sum.shape[1], 2 * FILTERS)
    return (
        hidden,
        grad_table,
        grad_cw,
        grad_cb,
        grad_hws,
        grad_hbs,
        grad_pws,
        grad_pb,
        grad_input,
        grad_state,
        grad_lbias,
        grad_lproj,
    )


def solution(mesh):
    in_specs = (
        P(("dp", "mp"), None),
        P(),
        P("dp"),
        P("dp"),
        P(),
        P(None, None, "dp"),
        P(),
        P(None, "dp", None),
        P(),
        P("dp", None),
        P(),
        P(None, "dp", "mp"),
        P(None, "dp", "mp"),
        P(None, "mp"),
        P(None, "mp", "dp"),
        P(None, "dp", "mp"),
        P(None, "dp", None),
        P("dp", None, None),
    )
    out_specs = (
        P("dp", None, None),
        P(),
        P(None, None, "dp"),
        P(),
        P(None, "dp", None),
        P(),
        P("dp", None),
        P(),
        P(None, "dp", "mp"),
        P(None, "dp", "mp"),
        P(None, "mp"),
        P(None, "mp", "dp"),
    )
    return jax.shard_map(shards, mesh=mesh, in_specs=in_specs, out_specs=out_specs, check_vma=False)
```

profile of v0, /device:TPU:0, one launch (start us, length us, event | category | flops | bytes accessed | tf_op | source)
XLA Modules:
  0.0 5865.6 jit_solution(9366199452954956182)
XLA Ops:
  28.8 107.1 %while.84 = (s32[]{:T(128)}, f32[14,20,2048]{2,1,0:T(8,128)}, s32[14,20,50]{2,1,0:T(8,128)S(1)}, bf16[262,16]{0,1:T(8,128)(2,1)S(1)}, bf16[112,2048]{1,0:T(8,128)(2,1)S(1)}, /*index=5*/s32[2048]{0:T(1024)S(1)}, s32[]{:T(128)}) while((s32[]{:T(128)}, f32[14,20,2048]{2,1,0:T(8,128)}, s32[14,20,50]{2,1,0:T(8,128)S(1)}, ...), condition=%wide.region_2.3_spmd.clone, body=%wide.region_0.2_spmd.clone.sunk | while | flops 471755776 | bytes 2911793 | solution.py:127
  143.7 77.0 %all-gather.6.cloned.1.call-done = bf16[2,2048,4096]{2,1,0:T(8,128)(2,1)} async-done(((bf16[2,512,4096]{2,1,0:T(8,128)(2,1)}), bf16[2,2048,4096]{2,1,0:T(8,128)(2,1)}) %all-gather.6.cloned.1.call-update) | async-done | bytes 33554448 | tf_op jit(solution)/shard_map/all_gather | solution.py:100
  283.3 109.9 %all-reduce.13.cloned.1.call-done = bf16[2240,512]{1,0:T(8,128)(2,1)} async-done(((bf16[2240,512]{1,0:T(8,128)(2,1)}), bf16[2240,512]{1,0:T(8,128)(2,1)}) %all-reduce.13.cloned.1.call-update) | async-done | bytes 2293776 | tf_op jit(solution)/shard_map/psum | solution.py:152
  583.9 1831.3 %while.83 = (s32[]{:T(128)}, f32[2,112,512]{2,1,0:T(8,128)S(1)}, bf16[2,112,512]{2,1,0:T(8,128)(2,1)S(1)}, bf16[20,2,112,512]{3,2,0,1:T(8,128)(2,1)}, f32[20,2,1...) while((s32[]{:T(128)}, f32[2,112,512]{2,1,0:T(8,128)S(1)}, ...), condition=%wide.region_7.8_spmd, body=%wide.region_5.7_spmd.sunk | while | flops 590758144 | bytes 46535792 | solution.py:197
  603.4 68.8 %all-reduce.21.cloned.1.call-done = f32[2,112,512]{2,1,0:T(8,128)} async-done(((f32[2,112,512]{2,1,0:T(8,128)}), f32[2,112,512]{2,1,0:T(8,128)}) %all-reduce.21.cloned.1.call-update) | async-done | bytes 458768 | tf_op jit(solution)/shard_map/while/body/eval_jaxpr/psum | solution.py:190
  786.6 68.7 %all-reduce.21.cloned.1.call-done = f32[2,112,512]{2,1,0:T(8,128)} async-done(((f32[2,112,512]{2,1,0:T(8,128)}), f32[2,112,512]{2,1,0:T(8,128)}) %all-reduce.21.cloned.1.call-update) | async-done | bytes 458768 | tf_op jit(solution)/shard_map/while/body/eval_jaxpr/psum | solution.py:190
  878.2 68.7 %all-reduce.21.cloned.1.call-done = f32[2,112,512]{2,1,0:T(8,128)} async-done(((f32[2,112,512]{2,1,0:T(8,128)}), f32[2,112,512]{2,1,0:T(8,128)}) %all-reduce.21.cloned.1.call-update) | async-done | bytes 458768 | tf_op jit(solution)/shard_map/while/body/eval_jaxpr/psum | solution.py:190
  969.7 68.7 %all-reduce.21.cloned.1.call-done = f32[2,112,512]{2,1,0:T(8,128)} async-done(((f32[2,112,512]{2,1,0:T(8,128)}), f32[2,112,512]{2,1,0:T(8,128)}) %all-reduce.21.cloned.1.call-update) | async-done | bytes 458768 | tf_op jit(solution)/shard_map/while/body/eval_jaxpr/psum | solution.py:190
  1061.3 68.7 %all-reduce.21.cloned.1.call-done = f32[2,112,512]{2,1,0:T(8,128)} async-done(((f32[2,112,512]{2,1,0:T(8,128)}), f32[2,112,512]{2,1,0:T(8,128)}) %all-reduce.21.cloned.1.call-update) | async-done | bytes 458768 | tf_op jit(solution)/shard_map/while/body/eval_jaxpr/psum | solution.py:190
  1152.9 68.7 %all-reduce.21.cloned.1.call-done = f32[2,112,512]{2,1,0:T(8,128)} async-done(((f32[2,112,512]{2,1,0:T(8,128)}), f32[2,112,512]{2,1,0:T(8,128)}) %all-reduce.21.cloned.1.call-update) | async-done | bytes 458768 | tf_op jit(solution)/shard_map/while/body/eval_jaxpr/psum | solution.py:190
  1335.9 68.7 %all-reduce.21.cloned.1.call-done = f32[2,112,512]{2,1,0:T(8,128)} async-done(((f32[2,112,512]{2,1,0:T(8,128)}), f32[2,112,512]{2,1,0:T(8,128)}) %all-reduce.21.cloned.1.call-update) | async-done | bytes 458768 | tf_op jit(solution)/shard_map/while/body/eval_jaxpr/psum | solution.py:190
  1427.5 68.7 %all-reduce.21.cloned.1.call-done = f32[2,112,512]{2,1,0:T(8,128)} async-done(((f32[2,112,512]{2,1,0:T(8,128)}), f32[2,112,512]{2,1,0:T(8,128)}) %all-reduce.21.cloned.1.call-update) | async-done | bytes 458768 | tf_op jit(solution)/shard_map/while/body/eval_jaxpr/psum | solution.py:190
  1519.0 68.7 %all-reduce.21.cloned.1.call-done = f32[2,112,512]{2,1,0:T(8,128)} async-done(((f32[2,112,512]{2,1,0:T(8,128)}), f32[2,112,512]{2,1,0:T(8,128)}) %all-reduce.21.cloned.1.call-update) | async-done | bytes 458768 | tf_op jit(solution)/shard_map/while/body/eval_jaxpr/psum | solution.py:190
  1610.5 68.7 %all-reduce.21.cloned.1.call-done = f32[2,112,512]{2,1,0:T(8,128)} async-done(((f32[2,112,512]{2,1,0:T(8,128)}), f32[2,112,512]{2,1,0:T(8,128)}) %all-reduce.21.cloned.1.call-update) | async-done | bytes 458768 | tf_op jit(solution)/shard_map/while/body/eval_jaxpr/psum | solution.py:190
  1702.1 68.7 %all-reduce.21.cloned.1.call-done = f32[2,112,512]{2,1,0:T(8,128)} async-done(((f32[2,112,512]{2,1,0:T(8,128)}), f32[2,112,512]{2,1,0:T(8,128)}) %all-reduce.21.cloned.1.call-update) | async-done | bytes 458768 | tf_op jit(solution)/shard_map/while/body/eval_jaxpr/psum | solution.py:190
  1885.1 68.8 %all-reduce.21.cloned.1.call-done = f32[2,112,512]{2,1,0:T(8,128)} async-done(((f32[2,112,512]{2,1,0:T(8,128)}), f32[2,112,512]{2,1,0:T(8,128)}) %all-reduce.21.cloned.1.call-update) | async-done | bytes 458768 | tf_op jit(solution)/shard_map/while/body/eval_jaxpr/psum | solution.py:190
  1976.9 68.7 %all-reduce.21.cloned.1.call-done = f32[2,112,512]{2,1,0:T(8,128)} async-done(((f32[2,112,512]{2,1,0:T(8,128)}), f32[2,112,512]{2,1,0:T(8,128)}) %all-reduce.21.cloned.1.call-update) | async-done | bytes 458768 | tf_op jit(solution)/shard_map/while/body/eval_jaxpr/psum | solution.py:190
  2068.3 68.7 %all-reduce.21.cloned.1.call-done = f32[2,112,512]{2,1,0:T(8,128)} async-done(((f32[2,112,512]{2,1,0:T(8,128)}), f32[2,112,512]{2,1,0:T(8,128)}) %all-reduce.21.cloned.1.call-update) | async-done | bytes 458768 | tf_op jit(solution)/shard_map/while/body/eval_jaxpr/psum | solution.py:190
  2159.9 68.7 %all-reduce.21.cloned.1.call-done = f32[2,112,512]{2,1,0:T(8,128)} async-done(((f32[2,112,512]{2,1,0:T(8,128)}), f32[2,112,512]{2,1,0:T(8,128)}) %all-reduce.21.cloned.1.call-update) | async-done | bytes 458768 | tf_op jit(solution)/shard_map/while/body/eval_jaxpr/psum | solution.py:190
  2343.0 68.7 %all-reduce.21.cloned.1.call-done = f32[2,112,512]{2,1,0:T(8,128)} async-done(((f32[2,112,512]{2,1,0:T(8,128)}), f32[2,112,512]{2,1,0:T(8,128)}) %all-reduce.21.cloned.1.call-update) | async-done | bytes 458768 | tf_op jit(solution)/shard_map/while/body/eval_jaxpr/psum | solution.py:190
  2424.4 1977.8 %while.85 = (s32[]{:T(128)}, f32[2,112,512]{2,1,0:T(8,128)}, f32[2,112,512]{2,1,0:T(8,128)}, bf16[20,2,112,2048]{3,2,1,0:T(8,128)(2,1)}, bf16[20,2,112,512]{3,2,...) while((s32[]{:T(128)}, f32[2,112,512]{2,1,0:T(8,128)}, ...), condition=%wide.region_10.11_spmd.clone, body=%wide.region_8.10_spmd.clone.sunk | while | flops 594542592 | bytes 56856416 | solution.py:244
  4518.5 104.4 %all-reduce.15.cloned.1.call-done = bf16[2240,512]{1,0:T(8,128)(2,1)} async-done(((bf16[2240,512]{1,0:T(8,128)(2,1)}), bf16[2240,512]{1,0:T(8,128)(2,1)}) %all-reduce.15.cloned.1.call-update) | async-done | bytes 2293776 | tf_op jit(solution)/shard_map/psum | solution.py:267
  4793.3 537.4 %while.86 = (s32[]{:T(128)}, f32[112,2048]{1,0:T(8,128)S(1)}, f32[262,16]{0,1:T(8,128)S(1)}, s32[14,20,50]{2,1,0:T(8,128)}, bf16[262,16]{0,1:T(8,128)(2,1)S(1)},...) while((s32[]{:T(128)}, f32[112,2048]{1,0:T(8,128)S(1)}, ...), condition=%wide.region_14.15_spmd.clone, body=%wide.region_12.14_spmd.clone.sunk | while | flops 1448498944 | bytes 55997560 | solution.py:342
  5557.3 287.7 %all-reduce.19.cloned.1.call-done = (bf16[2,512,4096]{1,2,0:T(8,128)(2,1)}, bf16[512,512]{1,0:T(8,128)(2,1)}) async-done(((bf16[2,512,4096]{1,2,0:T(8,128)(2,1)}, bf16[512,512]{1,0:T(8,128)(2,1)}), (bf16[2,512,4096]{1,2,0:T(8,128)(2,1)}, bf16[512,512]{1,0:T(8,128)(2,1)})) %all-reduce.19.cloned.1.call-update) | async-done | bytes 8912912 | tf_op jit(solution)/shard_map/psum | solution.py:362
  (2233 shorter events, 4162.0 us)
Async XLA Ops:
  7.2 213.4 %all-gather.6.cloned.1.call-start = ((), (), s32[]{:S(2)}) async-start(), calls=%async_computation.5 | async-start | bytes 41943040 | tf_op jit(solution)/shard_map/all_gather | solution.py:100
  16.3 229.2 %all-gather.8.cloned.1.call-start = ((), (), s32[]{:S(2)}) async-start(), calls=%async_computation.6 | async-start | bytes 2621440 | tf_op jit(solution)/shard_map/all_gather | solution.py:101
  18.3 264.9 %all-gather.10.cloned.1.call-start = ((), (), s32[]{:S(2)}) async-start(), calls=%async_computation.8 | async-start | bytes 5242880 | tf_op jit(solution)/shard_map/all_gather | solution.py:104
  19.5 373.6 %all-reduce.13.cloned.1.call-start = ((), (), s32[]{:S(2)}) async-start(), calls=%async_computation.7 | async-start | bytes 4587520 | tf_op jit(solution)/shard_map/psum | solution.py:152
  249.9 328.7 %all-gather.14.cloned.1.call-start = ((), (), s32[]{:S(2)}) async-start(), calls=%async_computation.10 | async-start | bytes 1310720 | tf_op jit(solution)/shard_map/all_gather | solution.py:106
  260.8 317.9 %all-gather.12.cloned.1.call-start = ((), (), s32[]{:S(2)}) async-start(), calls=%async_computation.9 | async-start | bytes 5242880 | tf_op jit(solution)/shard_map/all_gather | solution.py:105
  2424.8 97.1 %all-reduce.23.cloned.1.call-start = ((), (), s32[]{:S(2)}) async-start(), calls=%async_computation.20 | async-start | bytes 458752 | tf_op jit(solution)/shard_map/while/body/eval_jaxpr/psum | solution.py:238
  2523.8 97.1 %all-reduce.23.cloned.1.call-start = ((), (), s32[]{:S(2)}) async-start(), calls=%async_computation.20 | async-start | bytes 458752 | tf_op jit(solution)/shard_map/while/body/eval_jaxpr/psum | solution.py:238
  2622.6 97.1 %all-reduce.23.cloned.1.call-start = ((), (), s32[]{:S(2)}) async-start(), calls=%async_computation.20 | async-start | bytes 458752 | tf_op jit(solution)/shard_map/while/body/eval_jaxpr/psum | solution.py:238
  2721.5 97.1 %all-reduce.23.cloned.1.call-start = ((), (), s32[]{:S(2)}) async-start(), calls=%async_computation.20 | async-start | bytes 458752 | tf_op jit(solution)/shard_map/while/body/eval_jaxpr/psum | solution.py:238
  2820.4 97.1 %all-reduce.23.cloned.1.call-start = ((), (), s32[]{:S(2)}) async-start(), calls=%async_computation.20 | async-start | bytes 458752 | tf_op jit(solution)/shard_map/while/body/eval_jaxpr/psum | solution.py:238
  3117.0 97.1 %all-reduce.23.cloned.1.call-start = ((), (), s32[]{:S(2)}) async-start(), calls=%async_computation.20 | async-start | bytes 458752 | tf_op jit(solution)/shard_map/while/body/eval_jaxpr/psum | solution.py:238
  3215.9 97.1 %all-reduce.23.cloned.1.call-start = ((), (), s32[]{:S(2)}) async-start(), calls=%async_computation.20 | async-start | bytes 458752 | tf_op jit(solution)/shard_map/while/body/eval_jaxpr/psum | solution.py:238
  3809.1 97.1 %all-reduce.23.cloned.1.call-start = ((), (), s32[]{:S(2)}) async-start(), calls=%async_computation.20 | async-start | bytes 458752 | tf_op jit(solution)/shard_map/while/body/eval_jaxpr/psum | solution.py:238
  4105.6 97.1 %all-reduce.23.cloned.1.call-start = ((), (), s32[]{:S(2)}) async-start(), calls=%async_computation.20 | async-start | bytes 458752 | tf_op jit(solution)/shard_map/while/body/eval_jaxpr/psum | solution.py:238
  4204.5 97.1 %all-reduce.23.cloned.1.call-start = ((), (), s32[]{:S(2)}) async-start(), calls=%async_computation.20 | async-start | bytes 458752 | tf_op jit(solution)/shard_map/while/body/eval_jaxpr/psum | solution.py:238
  4402.3 220.6 %all-reduce.15.cloned.1.call-start = ((), (), s32[]{:S(2)}) async-start(), calls=%async_computation.11 | async-start | bytes 4587520 | tf_op jit(solution)/shard_map/psum | solution.py:267
  4516.0 866.9 %reduce-scatter.10.cloned.1.call-start = ((), (), s32[]{:S(2)}) async-start(), calls=%async_computation.12 | async-start | bytes 41943040 | tf_op jit(solution)/shard_map/reduce_scatter | solution.py:354
  4741.2 653.2 %reduce-scatter.12.cloned.1.call-start = ((), (), s32[]{:S(2)}) async-start(), calls=%async_computation.13 | async-start | bytes 2621440 | tf_op jit(solution)/shard_map/reduce_scatter | solution.py:357
  4746.0 653.9 %reduce-scatter.18.cloned.1.call-start = ((), (), s32[]{:S(2)}) async-start(), calls=%async_computation.16 | async-start | bytes 1310720
  4772.5 688.9 %all-reduce.17.cloned.1.call-start = ((), (), s32[]{:S(2)}) async-start(), calls=%async_computation.17 | async-start | bytes 2097152 | tf_op jit(solution)/shard_map/psum | solution.py:348
  5331.7 175.9 %reduce-scatter.16.cloned.1.call-start = ((), (), s32[]{:S(2)}) async-start(), calls=%async_computation.15 | async-start | bytes 5242880
  5366.1 188.5 %reduce-scatter.14.cloned.1.call-start = ((), (), s32[]{:S(2)}) async-start(), calls=%async_computation.14 | async-start | bytes 5242880 | tf_op jit(solution)/shard_map/reduce_scatter | solution.py:273
  5382.8 462.2 %all-reduce.19.cloned.1.call-start = ((), (), s32[]{:S(2)}) async-start(), calls=%async_computation.18 | async-start | bytes 17825792 | tf_op jit(solution)/shard_map/psum | solution.py:362
  (244 other events, 4375.4 us)
Sparse Core Ops, SparseCore 0:
  16.4 204.2 all-gather.5
  285.6 107.5 all-reduce.12
  600.8 71.3 all-reduce.20
  692.5 71.2 all-reduce.20
  784.0 71.2 all-reduce.20
  875.6 71.2 all-reduce.20
  967.1 71.2 all-reduce.20
  1058.7 71.2 all-reduce.20
  1150.3 71.2 all-reduce.20
  1333.3 71.2 all-reduce.20
  1424.9 71.2 all-reduce.20
  1516.4 71.2 all-reduce.20
  1607.9 71.2 all-reduce.20
  1699.5 71.2 all-reduce.20
  1791.1 71.2 all-reduce.20
  1882.5 71.3 all-reduce.20
  1974.3 71.2 all-reduce.20
  2065.7 71.2 all-reduce.20
  2157.3 71.2 all-reduce.20
  2340.3 71.2 all-reduce.20
  4516.1 106.7 all-reduce.14
  4741.3 234.0 reduce-scatter.9
  5331.9 129.5 all-reduce.16
  5559.7 285.2 all-reduce.18
  (30 shorter events, 1785.6 us)
where the time goes:
time: 5890 us; the launch traced here: 5870 us
  waiting for transfers between devices  3410 us (58%)
  local copies, waits for them, and re-layouts  1310 us (22%)
  matrix products  600 us (10%)
  other arithmetic  452 us (8%)
    psum x20, waiting for transfers between devices, forward_step(): stat_kept = lax.psum(partial_sum, 'mp')  1370 us
    psum x20, waiting for transfers between devices, backward_step(): lax.psum(back_partial.astype(jnp.bfloat16), 'mp').astype(jnp.float32)  1360 us
    psum x1, waiting for transfers between devices, shards(): lax.psum(hw_part.astype(jnp.bfloat16), 'mp').astype(jnp.float32)  288 us
    scatter-add x98, local copies, waits for them, and re-layouts, conv_back(): grad_chars.at[:, tap_index:tap_index + CHARS, :]  260 us
    dynamic_update_slice x100, other arithmetic, shards(): lax.scan(forward_step, (init_cell, init_hidden), (scan_input, keep_masks))  152 us
    dot_general x20, matrix products, forward_step(): jnp.einsum('drp,dpg->drg', hidden_prev, state_full, preferred_element_typ...  118 us
  transfers between devices with their start and end apart: 54, of which 47 were waited for; matrix products, arithmetic and copies ran while one was open for 19% of the time, Pallas kernels for 0%

commit v1 on v0

--- a/solution.py
+++ b/solution.py
@@ -1,8 +1,11 @@
+import functools
 import math
 
 import jax
 import jax.numpy as jnp
 from jax import lax
+from jax.experimental import pallas as pl
+from jax.experimental.pallas import tpu as pltpu
 from jax.sharding import PartitionSpec as P
 
 VOCAB = 262
@@ -63,6 +66,453 @@
         [padded[:, tap_index : tap_index + CHARS, :] for tap_index in range(TAPS)], axis=2
     )
     return (one_hot, columns.reshape(-1, TAPS * CDIM))
+
+
+def sigmoid_of(value):
+    return 0.5 * jnp.tanh(0.5 * value) + 0.5
+
+
+def mp_barrier(size):
+    me = lax.axis_index("mp")
+    barrier = pltpu.get_barrier_semaphore()
+    for offset in range(1, size):
+        peer = lax.rem(me + offset, size)
+        pl.semaphore_signal(
+            barrier, inc=1, device_id={"mp": peer}, device_id_type=pl.DeviceIdType.MESH
+        )
+    pl.semaphore_wait(barrier, size - 1)
+
+
+class Exchange:
+    def __init__(self, size, part_ref, sum_ref, all_ref, sems):
+        self.size = size
+        self.me = lax.axis_index("mp")
+        self.part_ref, self.sum_ref, self.all_ref = part_ref, sum_ref, all_ref
+        self.part_send, self.part_recv, self.all_send, self.all_recv = sems
+
+    def part_copy(self, way, offset, incoming):
+        peer = lax.rem(self.me + (self.size - offset if incoming else offset), self.size)
+        return pltpu.make_async_remote_copy(
+            src_ref=self.part_ref.at[way, peer],
+            dst_ref=self.sum_ref.at[way, peer if incoming else self.me],
+            send_sem=self.part_send.at[way, offset],
+            recv_sem=self.part_recv.at[way, offset],
+            device_id={"mp": peer},
+            device_id_type=pl.DeviceIdType.MESH,
+        )
+
+    def all_copy(self, way, offset, incoming):
+        peer = lax.rem(self.me + (self.size - offset if incoming else offset), self.size)
+        slot = peer if incoming else self.me
+        return pltpu.make_async_remote_copy(
+            src_ref=self.all_ref.at[way, slot],
+            dst_ref=self.all_ref.at[way, slot],
+            send_sem=self.all_send.at[way, offset],
+            recv_sem=self.all_recv.at[way, offset],
+            device_id={"mp": peer},
+            device_id_type=pl.DeviceIdType.MESH,
+        )
+
+    def send_parts(self, way):
+        for offset in range(1, self.size):
+            self.part_copy(way, offset, False).start()
+
+    def take_sum(self, way):
+        total = self.part_ref[way, self.me].astype(jnp.float32)
+        for offset in range(1, self.size):
+            self.part_copy(way, offset, True).wait_recv()
+            peer = lax.rem(self.me + self.size - offset, self.size)
+            total = total + self.sum_ref[way, peer].astype(jnp.float32)
+        for offset in range(1, self.size):
+            self.part_copy(way, offset, False).wait_send()
+        return total
+
+    def send_all(self, way, value):
+        self.all_ref[way, self.me] = value
+        for offset in range(1, self.size):
+            self.all_copy(way, offset, False).start()
+
+    def wait_all(self, way):
+        for offset in range(1, self.size):
+            self.all_copy(way, offset, True).wait_recv()
+        for offset in range(1, self.size):
+            self.all_copy(way, offset, False).wait_send()
+
+
+def forward_kernel(
+    size,
+    emb_ref,
+    win_ref,
+    wst_ref,
+    wpr_ref,
+    bias_ref,
+    cell_ref,
+    hid_ref,
+    reset_ref,
+    embt_ref,
+    gate0_ref,
+    gate1_ref,
+    cprev0_ref,
+    cprev1_ref,
+    cnew0_ref,
+    cnew1_ref,
+    low0_ref,
+    low1_ref,
+    hprev0_ref,
+    hprev1_ref,
+    stat0_ref,
+    stat1_ref,
+    out0_ref,
+    out1_ref,
+    pre_ref,
+    state_ref,
+    part_ref,
+    sum_ref,
+    all_ref,
+    part_send,
+    part_recv,
+    all_send,
+    all_recv,
+):
+    step = pl.program_id(0)
+    rows = reset_ref.shape[0]
+    units = cell_ref.shape[2]
+    blocks = units // UNIT_BLOCK
+    wide = 4 * UNIT_BLOCK
+    comm = Exchange(size, part_ref, sum_ref, all_ref, (part_send, part_recv, all_send, all_recv))
+    gate_refs = (gate0_ref, gate1_ref)
+    cprev_refs = (cprev0_ref, cprev1_ref)
+    cnew_refs = (cnew0_ref, cnew1_ref)
+    low_refs = (low0_ref, low1_ref)
+    hprev_refs = (hprev0_ref, hprev1_ref)
+    stat_refs = (stat0_ref, stat1_ref)
+    out_refs = (out0_ref, out1_ref)
+
+    def time_of(way, at):
+        return at if way == 0 else WIN - 1 - at
+
+    def input_part(way, at):
+        emb = emb_ref[:, time_of(way, at)].reshape(rows, PROJ)
+        for block in range(blocks):
+            cols = slice(block * wide, (block + 1) * wide)
+            pre_ref[way, :, cols] = (
+                jnp.dot(emb, win_ref[way, :, cols], preferred_element_type=jnp.float32)
+                + bias_ref[way, :, cols]
+            )
+
+    def emit_hidden(way):
+        out_refs[way][0] = all_ref[way].reshape(rows, PROJ)
+
+    def cell_step(way):
+        now = time_of(way, step)
+        keep = jnp.where(reset_ref[...] - way == now, 0.0, 1.0)
+        keep_low = jnp.concatenate([keep.astype(jnp.bfloat16)] * (PROJ // UNIT_BLOCK), axis=1)
+        hidden_prev = all_ref[way].reshape(rows, PROJ) * keep_low
+        hprev_refs[way][0] = hidden_prev
+        if way == 0:
+            embt_ref[0] = emb_ref[:, step].reshape(rows, PROJ)
+        for block in range(blocks):
+            cols = slice(block * wide, (block + 1) * wide)
+            unit = slice(block * UNIT_BLOCK, (block + 1) * UNIT_BLOCK)
+            pre = pre_ref[way, :, cols] + jnp.dot(
+                hidden_prev, wst_ref[way, :, cols], preferred_element_type=jnp.float32
+            )
+            gate_in = sigmoid_of(pre[:, :UNIT_BLOCK])
+            gate_forget = sigmoid_of(pre[:, UNIT_BLOCK : 2 * UNIT_BLOCK])
+            gate_cand = jnp.tanh(pre[:, 2 * UNIT_BLOCK : 3 * UNIT_BLOCK])
+            gate_out = sigmoid_of(pre[:, 3 * UNIT_BLOCK :])
+            cell_prev = state_ref[way, :, unit] * keep
+            cell_new = CLIP * jnp.tanh(
+                (gate_forget * cell_prev + gate_in * gate_cand) * (1.0 / CLIP)
+            )
+            gate_refs[way][0, :, cols] = jnp.concatenate(
+                [gate_in, gate_forget, gate_cand, gate_out], axis=1
+            )
+            cprev_refs[way][0, :, unit] = cell_prev
+            cnew_refs[way][0, :, unit] = cell_new
+            state_ref[way, :, unit] = cell_new
+            low_refs[way][0, :, unit] = (gate_out * jnp.tanh(cell_new)).astype(jnp.bfloat16)
+        partial = jnp.dot(low_refs[way][0], wpr_ref[way], preferred_element_type=jnp.float32)
+        part_ref[way] = partial.astype(jnp.bfloat16).reshape(size, rows // size, PROJ)
+        comm.send_parts(way)
+
+    def close_step(way):
+        total = comm.take_sum(way)
+        stat_refs[way][0] = total
+        comm.send_all(way, (CLIP * jnp.tanh(total * (1.0 / CLIP))).astype(jnp.bfloat16))
+
+    @pl.when(step == 0)
+    def _():
+        for way in range(2):
+            all_ref[way] = hid_ref[way]
+            state_ref[way] = cell_ref[way]
+            input_part(way, 0)
+        mp_barrier(size)
+
+    @pl.when(step > 0)
+    def _():
+        comm.wait_all(0)
+        emit_hidden(0)
+
+    @pl.when(step < WIN)
+    def _():
+        cell_step(0)
+
+    @pl.when(step > 0)
+    def _():
+        close_step(1)
+
+    @pl.when(step < WIN)
+    def _():
+        @pl.when(step < WIN - 1)
+        def _():
+            input_part(0, step + 1)
+
+        close_step(0)
+
+    @pl.when(step > 0)
+    def _():
+        comm.wait_all(1)
+        emit_hidden(1)
+
+    @pl.when(step < WIN)
+    def _():
+        cell_step(1)
+
+        @pl.when(step < WIN - 1)
+        def _():
+            input_part(1, step + 1)
+
+
+def lstm_forward(size, emb, win, wst, wpr, bias, cell, hid, reset):
+    rows = reset.shape[0]
+    part = rows // size
+    gates = win.shape[2]
+    units = cell.shape[2]
+    last = WIN - 1
+    vmem = pl.BlockSpec(memory_space=pltpu.VMEM)
+
+    def block(shape, index):
+        return pl.BlockSpec((1,) + shape, lambda w: (index(w), 0, 0))
+
+    now0 = lambda w: jnp.minimum(w, last)
+    now1 = lambda w: last - jnp.minimum(w, last)
+    past0 = lambda w: jnp.maximum(w - 1, 0)
+    past1 = lambda w: last - jnp.maximum(w - 1, 0)
+    outs = [((rows, PROJ), jnp.bfloat16, now0)]
+    for width, kind in ((gates, jnp.float32), (units, jnp.float32), (units, jnp.float32), (units, jnp.bfloat16), (PROJ, jnp.bfloat16)):
+        outs += [((rows, width), kind, now0), ((rows, width), kind, now1)]
+    outs += [((part, PROJ), jnp.float32, now0), ((part, PROJ), jnp.float32, past1)]
+    outs += [((rows, PROJ), jnp.bfloat16, past0), ((rows, PROJ), jnp.bfloat16, past1)]
+    return pl.pallas_call(
+        functools.partial(forward_kernel, size),
+        grid=(WIN + 1,),
+        in_specs=[vmem] * 8,
+        out_specs=[block(shape, index) for shape, kind, index in outs],
+        out_shape=[jax.ShapeDtypeStruct((WIN,) + shape, kind) for shape, kind, index in outs],
+        scratch_shapes=[
+            pltpu.VMEM((2, rows, gates), jnp.float32),
+            pltpu.VMEM((2, rows, units), jnp.float32),
+            pltpu.VMEM((2, size, part, PROJ), jnp.bfloat16),
+            pltpu.VMEM((2, size, part, PROJ), jnp.bfloat16),
+            pltpu.VMEM((2, size, part, PROJ), jnp.bfloat16),
+        ]
+        + [pltpu.SemaphoreType.DMA((2, size))] * 4,
+        compiler_params=pltpu.CompilerParams(
+            collective_id=1, has_side_effects=True, vmem_limit_bytes=56 * 2**20
+        ),
+    )(emb, win, wst, wpr, bias, cell, hid, reset)
+
+
+def backward_kernel(
+    size,
+    gate0_ref,
+    gate1_ref,
+    cprev0_ref,
+    cprev1_ref,
+    cnew0_ref,
+    cnew1_ref,
+    cot0_ref,
+    cot1_ref,
+    stat0_ref,
+    stat1_ref,
+    win_ref,
+    wst_ref,
+    wpr_ref,
+    reset_ref,
+    first_cot_ref,
+    first_stat_ref,
+    da0_ref,
+    da1_ref,
+    ds0_ref,
+    ds1_ref,
+    de0_ref,
+    de1_ref,
+    bias_ref,
+    cell_ref,
+    part_ref,
+    sum_ref,
+    all_ref,
+    part_send,
+    part_recv,
+    all_send,
+    all_recv,
+):
+    step = pl.program_id(0)
+    rows = reset_ref.shape[0]
+    part = rows // size
+    units = cell_ref.shape[2]
+    blocks = units // UNIT_BLOCK
+    wide = 4 * UNIT_BLOCK
+    comm = Exchange(size, part_ref, sum_ref, all_ref, (part_send, part_recv, all_send, all_recv))
+    gate_refs = (gate0_ref, gate1_ref)
+    cprev_refs = (cprev0_ref, cprev1_ref)
+    cnew_refs = (cnew0_ref, cnew1_ref)
+    da_refs = (da0_ref, da1_ref)
+    ds_refs = (ds0_ref, ds1_ref)
+    de_refs = (de0_ref, de1_ref)
+
+    def time_of(way, at):
+        return WIN - 1 - at if way == 0 else at
+
+    def stat_step(way, at, cot, stat, total):
+        grad = cot.astype(jnp.float32)
+        if total is not None:
+            own = reset_ref[pl.ds(comm.me * part, part), :] - way
+            keep = jnp.where(own == time_of(way, at - 1), 0.0, 1.0)
+            grad = grad + total * jnp.concatenate([keep] * (PROJ // UNIT_BLOCK), axis=1)
+        slope = jnp.tanh(stat * (1.0 / CLIP))
+        comm.send_all(way, (grad * (1.0 - slope * slope)).astype(jnp.bfloat16))
+
+    def cell_step(way):
+        comm.wait_all(way)
+        now = time_of(way, step)
+        keep = jnp.where(reset_ref[...] - way == now, 0.0, 1.0)
+        grad_stat = all_ref[way].reshape(rows, PROJ)
+        ds_refs[way][0] = grad_stat
+        for block in range(blocks):
+            cols = slice(block * wide, (block + 1) * wide)
+            unit = slice(block * UNIT_BLOCK, (block + 1) * UNIT_BLOCK)
+            grad_out = lax.dot_general(
+                grad_stat,
+                wpr_ref[way, unit, :],
+                (((1,), (1,)), ((), ())),
+                preferred_element_type=jnp.float32,
+            )
+            gates = gate_refs[way][0, :, cols]
+            gate_in = gates[:, :UNIT_BLOCK]
+            gate_forget = gates[:, UNIT_BLOCK : 2 * UNIT_BLOCK]
+            gate_cand = gates[:, 2 * UNIT_BLOCK : 3 * UNIT_BLOCK]
+            gate_out = gates[:, 3 * UNIT_BLOCK :]
+            cell_prev = cprev_refs[way][0, :, unit]
+            cell_new = cnew_refs[way][0, :, unit]
+            tanh_cell = jnp.tanh(cell_new)
+            grad_total = (
+                grad_out * gate_out * (1.0 - tanh_cell * tanh_cell) + cell_ref[way, :, unit]
+            )
+            scaled = cell_new * (1.0 / CLIP)
+            grad_inner = grad_total * (1.0 - scaled * scaled)
+            cell_ref[way, :, unit] = grad_inner * gate_forget * keep
+            grad_pre = jnp.concatenate(
+                [
+                    grad_inner * gate_cand * gate_in * (1.0 - gate_in),
+                    grad_inner * cell_prev * gate_forget * (1.0 - gate_forget),
+                    grad_inner * gate_in * (1.0 - gate_cand * gate_cand),
+                    grad_out * tanh_cell * gate_out * (1.0 - gate_out),
+                ],
+                axis=1,
+            ).astype(jnp.bfloat16)
+            da_refs[way][0, :, cols] = grad_pre
+            bias_ref[way, :, cols] += jnp.sum(
+                grad_pre.astype(jnp.float32).reshape(rows // 8, 8, wide), axis=0
+            )
+
+        @pl.when(step < WIN - 1)
+        def _():
+            partial = lax.dot_general(
+                da_refs[way][0],
+                wst_ref[way],
+                (((1,), (1,)), ((), ())),
+                preferred_element_type=jnp.float32,
+            )
+            part_ref[way] = partial.astype(jnp.bfloat16).reshape(size, part, PROJ)
+            comm.send_parts(way)
+
+    def embed_step(way):
+        de_refs[way][0] = lax.dot_general(
+            da_refs[way][0],
+            win_ref[way],
+            (((1,), (1,)), ((), ())),
+            preferred_element_type=jnp.float32,
+        )
+
+    @pl.when(step == 0)
+    def _():
+        cell_ref[...] = jnp.zeros(cell_ref.shape, jnp.float32)
+        bias_ref[...] = jnp.zeros(bias_ref.shape, jnp.float32)
+        mp_barrier(size)
+        for way in range(2):
+            stat_step(way, 0, first_cot_ref[way], first_stat_ref[way], None)
+
+    cell_step(0)
+
+    @pl.when(step > 0)
+    def _():
+        stat_step(1, step, cot1_ref[0], stat1_ref[0], comm.take_sum(1))
+
+    embed_step(0)
+
+    @pl.when(step < WIN - 1)
+    def _():
+        stat_step(0, step + 1, cot0_ref[0], stat0_ref[0], comm.take_sum(0))
+
+    cell_step(1)
+    embed_step(1)
+
+
+def lstm_backward(size, gates, cprevs, cnews, cots, stats, win, wst, wpr, reset):
+    rows = reset.shape[0]
+    part = rows // size
+    width = win.shape[2]
+    units = cprevs[0].shape[2]
+    last = WIN - 1
+    vmem = pl.BlockSpec(memory_space=pltpu.VMEM)
+
+    def block(shape, index):
+        return pl.BlockSpec((1,) + shape, lambda w: (index(w), 0, 0))
+
+    now0 = lambda w: last - w
+    now1 = lambda w: w
+    next0 = lambda w: jnp.maximum(last - 1 - w, 0)
+    ins = []
+    for size_of in (width, units, units):
+        ins += [block((rows, size_of), now0), block((rows, size_of), now1)]
+    ins += [block((part, PROJ), next0), block((part, PROJ), now1)] * 2
+    ins += [vmem] * 6
+    outs = []
+    for size_of, kind in ((width, jnp.bfloat16), (PROJ, jnp.bfloat16), (PROJ, jnp.float32)):
+        outs += [((rows, size_of), kind, now0), ((rows, size_of), kind, now1)]
+    first_cot = jnp.stack([cots[0][last], cots[1][0]])
+    first_stat = jnp.stack([stats[0][last], stats[1][0]])
+    return pl.pallas_call(
+        functools.partial(backward_kernel, size),
+        grid=(WIN,),
+        in_specs=ins,
+        out_specs=[block(shape, index) for shape, kind, index in outs]
+        + [pl.BlockSpec((2, 8, width), lambda w: (0, 0, 0))],
+        out_shape=[jax.ShapeDtypeStruct((WIN,) + shape, kind) for shape, kind, index in outs]
+        + [jax.ShapeDtypeStruct((2, 8, width), jnp.float32)],
+        scratch_shapes=[
+            pltpu.VMEM((2, rows, units), jnp.float32),
+            pltpu.VMEM((2, size, part, PROJ), jnp.bfloat16),
+            pltpu.VMEM((2, size, part, PROJ), jnp.bfloat16),
+            pltpu.VMEM((2, size, part, PROJ), jnp.bfloat16),
+        ]
+        + [pltpu.SemaphoreType.DMA((2, size))] * 4,
+        compiler_params=pltpu.CompilerParams(
+            collective_id=2, has_side_effects=True, vmem_limit_bytes=56 * 2**20
+        ),
+    )(*gates, *cprevs, *cnews, *cots, *stats, win, wst, wpr, reset, first_cot, first_stat)
 
 
 def shards(
@@ -87,13 +537,12 @@
 ):
     tok_share = char_ids.shape[0]
     row_count = window_doc.shape[0]
-    group_tokens = row_count * WIN
     cell_local = init_cell.shape[2]
     gate_local = lstm_bias.shape[1]
     mp_index = lax.axis_index("mp")
+    mp_size = lax.axis_size("mp")
     dp_index = lax.axis_index("dp")
     dp_width = conv_weight.shape[2]
-    token_start = mp_index * tok_share
     high_low = highway_weight.astype(jnp.bfloat16)
     conv_full, high_full, proj_full = (
         lax.all_gather(conv_weight.astype(jnp.bfloat16), "dp", axis=2, tiled=True),
@@ -114,6 +563,8 @@
     counts = (CHARS + 1 - widths).astype(jnp.float32)
     table_low = char_table.astype(jnp.bfloat16)
     block_size = math.gcd(tok_share, WIN)
+    rows_own = row_count // mp_size
+    char_ids = char_ids.reshape(rows_own, WIN, CHARS).transpose(1, 0, 2).reshape(tok_share, CHARS)
     id_blocks = char_ids.reshape(tok_share // block_size, block_size, CHARS)
 
     def pool_block(id_block):
@@ -146,136 +597,84 @@
         )
     top_low = layer_value.astype(jnp.bfloat16)
     embed_local = jnp.dot(top_low, proj_full, preferred_element_type=jnp.float32) + proj_bias
-    embed_term = lax.dynamic_update_slice_in_dim(
-        jnp.zeros((group_tokens, PROJ), jnp.float32), embed_local, token_start, 0
-    )
-    embed_sum = lax.psum(embed_term.astype(jnp.bfloat16), "mp")
-    input_pre = (
-        jnp.einsum("np,dpg->dng", embed_sum, input_full, preferred_element_type=jnp.float32)
-        + lstm_bias[:, None, :]
-    )
-    input_pre = input_pre.reshape(2, row_count, WIN, gate_local)
-    scan_input = jnp.transpose(jnp.stack([input_pre[0], input_pre[1][:, ::-1]]), (2, 0, 1, 3))
+    part_rows = -(-rows_own // 16) * 16
+    rows = mp_size * part_rows
+
+    def pad_rows(value, axis):
+        shape = value.shape
+        split = value.reshape(shape[:axis] + (mp_size, rows_own) + shape[axis + 1 :])
+        widths = [(0, 0)] * split.ndim
+        widths[axis + 1] = (0, part_rows - rows_own)
+        return jnp.pad(split, widths)
+
+    def drop_rows(value, axis):
+        shape = value.shape
+        split = value.reshape(shape[:axis] + (mp_size, part_rows) + shape[axis + 1 :])
+        kept = lax.slice_in_dim(split, 0, rows_own, axis=axis + 1)
+        return kept.reshape(shape[:axis] + (row_count,) + shape[axis + 1 :])
+
+    embed_own = jnp.pad(
+        embed_local.astype(jnp.bfloat16).reshape(WIN, rows_own, PROJ),
+        ((0, 0), (0, part_rows - rows_own), (0, 0)),
+    )
+    embed_all = lax.all_gather(embed_own, "mp", axis=0)
     doc_index = jnp.arange(doc_lengths.shape[0])
     chosen_len = jnp.sum(
         jnp.where(window_doc[:, None] == doc_index[None, :], doc_lengths[None, :], 0), axis=1
     )
-    reset_at = chosen_len - window_offset
-    step_ids = jnp.arange(WIN)
-    keep_fwd = (step_ids[None, :] != reset_at[:, None]).astype(jnp.float32)
-    keep_bwd = (step_ids[None, :] != reset_at[:, None] - 1).astype(jnp.float32)[:, ::-1]
-    keep_masks = jnp.transpose(jnp.stack([keep_fwd, keep_bwd]), (2, 0, 1))
-
-    def forward_step(carry, inputs):
-        cell_state, hidden_state = carry
-        step_pre, keep_now = inputs
-        keep_cols = keep_now[:, :, None]
-        cell_prev = cell_state * keep_cols
-        hidden_prev = hidden_state * keep_cols.astype(jnp.bfloat16)
-        pre_act = step_pre + jnp.einsum(
-            "drp,dpg->drg", hidden_prev, state_full, preferred_element_type=jnp.float32
-        )
-        gate_in, gate_forget, gate_cand, gate_out = split_gates(pre_act, cell_local)
-        cell_new = CLIP * jnp.tanh(
-            (
-                jax.nn.sigmoid(gate_forget) * cell_prev
-                + jax.nn.sigmoid(gate_in) * jnp.tanh(gate_cand)
-            )
-            / CLIP
-        )
-        cell_low = (jax.nn.sigmoid(gate_out) * jnp.tanh(cell_new)).astype(jnp.bfloat16)
-        partial_sum = jnp.einsum(
-            "drc,dcp->drp", cell_low, lproj_full, preferred_element_type=jnp.float32
-        )
-        stat_kept = lax.psum(partial_sum, "mp")
-        hidden_new = (CLIP * jnp.tanh(stat_kept / CLIP)).astype(jnp.bfloat16)
-        return (
-            (cell_new, hidden_new),
-            (hidden_new, pre_act, cell_prev, cell_new, cell_low, hidden_prev, stat_kept),
-        )
-
-    carry_end, kept_steps = lax.scan(
-        forward_step, (init_cell, init_hidden), (scan_input, keep_masks)
-    )
-    states, pre_acts, cell_prevs, cell_news, cell_lows, hidden_prevs, stat_kepts = kept_steps
+    reset_at = (chosen_len - window_offset).astype(jnp.int32)
+    reset_rows = pad_rows(reset_at[:, None], 0).reshape(rows, 1)
+    reset_wide = jnp.broadcast_to(reset_rows, (rows, UNIT_BLOCK))
+    cell_rows = pad_rows(init_cell, 1).reshape(2, rows, cell_local)
+    hidden_rows = pad_rows(init_hidden, 1)
+    kept = lstm_forward(
+        mp_size,
+        embed_all,
+        input_full,
+        state_full,
+        lproj_full,
+        lstm_bias[:, None, :],
+        cell_rows,
+        hidden_rows,
+        reset_wide,
+    )
+    embed_time = kept[0]
+    gates, cprevs, cnews, lows, hprevs, stats, outs = (
+        kept[1 + 2 * index : 3 + 2 * index] for index in range(7)
+    )
     hidden = jnp.concatenate(
-        [jnp.transpose(states[:, 0], (1, 0, 2)), jnp.transpose(states[::-1, 1], (1, 0, 2))], axis=-1
-    )
-    cot_float = cotangent.astype(jnp.float32)
-    out_grads = jnp.transpose(
-        jnp.stack([cot_float[:, :, :PROJ], cot_float[:, ::-1, PROJ:]]), (2, 0, 1, 3)
-    )
-
-    def backward_step(carry, inputs):
-        grad_hidden, grad_cell = carry
-        out_grad, keep_now, pre_act, cell_prev, cell_new, stat_kept = inputs
-        grad_result = out_grad + grad_hidden
-        tanh_stat = jnp.tanh(stat_kept / CLIP)
-        grad_stat = (grad_result * (1.0 - tanh_stat * tanh_stat)).astype(jnp.bfloat16)
-        grad_cellout = jnp.einsum(
-            "drp,dcp->drc", grad_stat, lproj_full, preferred_element_type=jnp.float32
-        )
-        gate_in, gate_forget, gate_cand, gate_out = split_gates(pre_act, cell_local)
-        input_gate = jax.nn.sigmoid(gate_in)
-        forget_gate = jax.nn.sigmoid(gate_forget)
-        candidate = jnp.tanh(gate_cand)
-        output_gate = jax.nn.sigmoid(gate_out)
-        tanh_cell = jnp.tanh(cell_new)
-        grad_total = grad_cellout * output_gate * (1.0 - tanh_cell * tanh_cell) + grad_cell
-        grad_inner = grad_total * (1.0 - cell_new / CLIP * (cell_new / CLIP))
-        grad_pre = join_gates(
-            [
-                grad_inner * candidate * input_gate * (1.0 - input_gate),
-                grad_inner * cell_prev * forget_gate * (1.0 - forget_gate),
-                grad_inner * input_gate * (1.0 - candidate * candidate),
-                grad_cellout * tanh_cell * output_gate * (1.0 - output_gate),
-            ],
-            cell_local,
+        [jnp.transpose(drop_rows(value, 1), (1, 0, 2)) for value in outs], axis=-1
+    )
+    own_cot = lax.dynamic_slice_in_dim(cotangent, mp_index * rows_own, rows_own, 0)
+    own_cot = jnp.pad(
+        jnp.transpose(own_cot, (1, 0, 2)), ((0, 0), (0, part_rows - rows_own), (0, 0))
+    )
+    cots = (own_cot[:, :, :PROJ], own_cot[:, :, PROJ:])
+    back = lstm_backward(
+        mp_size, gates, cprevs, cnews, cots, stats, input_full, state_full, lproj_full, reset_wide
+    )
+    das, dss, des = (back[2 * index : 2 * index + 2] for index in range(3))
+    grad_bias = jnp.sum(back[6], axis=1)
+    embed_parts = (des[0] + des[1]).astype(jnp.bfloat16)
+    embed_parts = jnp.transpose(embed_parts.reshape(WIN, mp_size, part_rows, PROJ), (1, 0, 2, 3))
+    grad_embed_local = lax.psum_scatter(embed_parts, "mp", scatter_dimension=0, tiled=True)
+    grad_embed_local = grad_embed_local.reshape(WIN, part_rows, PROJ)[:, :rows_own]
+    grad_embed_local = grad_embed_local.reshape(tok_share, PROJ)
+
+    def outer(left, right):
+        return jnp.dot(
+            left.reshape(WIN * rows, -1).T,
+            right.reshape(WIN * rows, -1),
+            preferred_element_type=jnp.float32,
         ).astype(jnp.bfloat16)
-        back_partial = jnp.einsum(
-            "drg,dpg->drp", grad_pre, state_full, preferred_element_type=jnp.float32
-        )
-        back_sum = lax.psum(back_partial.astype(jnp.bfloat16), "mp").astype(jnp.float32)
-        keep_cols = keep_now[:, :, None]
-        return ((back_sum * keep_cols, grad_inner * forget_gate * keep_cols), (grad_pre, grad_stat))
-
-    zero_hidden = jnp.zeros(out_grads.shape[1:], jnp.float32)
-    zero_cell = jnp.zeros(init_cell.shape, jnp.float32)
-    carry_back, grad_steps = lax.scan(
-        backward_step,
-        (zero_hidden, zero_cell),
-        (out_grads, keep_masks, pre_acts, cell_prevs, cell_news, stat_kepts),
-        reverse=True,
-    )
-    grad_pres, grad_stats = grad_steps
-    grad_state = jnp.einsum(
-        "wdrp,wdrg->dpg", hidden_prevs, grad_pres, preferred_element_type=jnp.float32
-    )
-    grad_lproj = jnp.einsum(
-        "wdrc,wdrp->dcp", cell_lows, grad_stats, preferred_element_type=jnp.float32
-    )
-    token_pres = jnp.stack(
-        [jnp.transpose(grad_pres[:, 0], (1, 0, 2)), jnp.transpose(grad_pres[::-1, 1], (1, 0, 2))]
-    ).reshape(2, group_tokens, gate_local)
-    grad_input = jnp.einsum(
-        "np,dng->dpg", embed_sum, token_pres, preferred_element_type=jnp.float32
-    )
-    grad_bias = jnp.sum(token_pres.astype(jnp.float32), axis=1)
-    embed_partial = jnp.einsum(
-        "dng,dpg->np", token_pres, input_full, preferred_element_type=jnp.float32
-    )
-    grad_embed_all = lax.psum(embed_partial.astype(jnp.bfloat16), "mp")
-    grad_embed_local = lax.dynamic_slice_in_dim(grad_embed_all, token_start, tok_share, 0)
+
+    grad_input = jnp.stack([outer(embed_time, das[way]) for way in range(2)])
+    grad_state = jnp.stack([outer(hprevs[way], das[way]) for way in range(2)])
+    grad_lproj = jnp.stack([outer(lows[way], dss[way]) for way in range(2)])
     grad_input, grad_state, grad_lproj = (
-        lax.psum_scatter(
-            grad_input.astype(jnp.bfloat16), "dp", scatter_dimension=1, tiled=True
-        ).astype(jnp.float32),
-        lax.psum_scatter(
-            grad_state.astype(jnp.bfloat16), "dp", scatter_dimension=1, tiled=True
-        ).astype(jnp.float32),
-        lax.psum_scatter(
-            grad_lproj.astype(jnp.bfloat16), "dp", scatter_dimension=2, tiled=True
-        ).astype(jnp.float32),
+        lax.psum_scatter(grad_input, "dp", scatter_dimension=1, tiled=True).astype(jnp.float32),
+        lax.psum_scatter(grad_state, "dp", scatter_dimension=1, tiled=True).astype(jnp.float32),
+        lax.psum_scatter(grad_lproj, "dp", scatter_dimension=2, tiled=True).astype(jnp.float32),
     )
     grad_pb = jnp.sum(grad_embed_local.astype(jnp.float32), axis=0)
     grad_hw = [None, None]

time: 5890 us -> 2300 us (0.39)
  waiting for transfers between devices: 3410 us -> 728 us
  local copies, waits for them, and re-layouts: 1310 us -> 523 us
  Pallas kernels: 0 us -> 523 us
  other arithmetic: 452 us -> 133 us
  matrix products: 600 us -> 306 us
    psum x42 -> x0, waiting for transfers between devices: 2950 us -> none  [the longest x20 1370 us: forward_step(): stat_kept = lax.psum(partial_sum, 'mp')]
    pallas_call x0 -> x2, Pallas kernels: none -> 523 us  [the longest x1 262 us: lstm_forward(): pl.pallas_call(functools.partial(forward_kernel, size), grid=(WIN + 1,),...]
    dot_general x85 -> x6, matrix products: 334 us -> 44.1 us  [outer(): jnp.dot(left.reshape(WIN * rows, -1).T, right.reshape(WIN * rows, -1), pr...]
    slice x44 -> x4, local copies, waits for them, and re-layouts: 166 us -> 2.48 us  [the longest x2 1.52 us: lstm_backward(): first_stat = jnp.stack([stats[0][last], stats[1][0]])]
    dynamic_update_slice x100 -> x0, other arithmetic: 152 us -> none  [shards(): lax.scan(forward_step, (init_cell, init_hidden), (scan_input, keep_masks))]
    div x200 -> x0, local copies, waits for them, and re-layouts: 109 us -> none  [forward_step(): jax.nn.sigmoid(gate_forget) * cell_prev]
    mul x80 -> x0, other arithmetic: 96.3 us -> none  [the longest x20 36.1 us: backward_step(): back_sum * keep_cols]
    reshape x121 -> x7, local copies, waits for them, and re-layouts: 106 us -> 10.2 us  [the longest x2 8.32 us: drop_rows(): return kept.reshape(shape[:axis] + (row_count,) + shape[axis + 1:])]
  transfers between devices with their start and end apart: 54 -> 14, of which waited for: 47 -> 11; matrix products, arithmetic and copies ran while one was open for 19% -> 35% of each run, Pallas kernels for 0% -> 0%
where the time goes in v1:
time: 2300 us; the launch traced here: 2280 us
  waiting for transfers between devices  728 us (32%)
  local copies, waits for them, and re-layouts  523 us (23%)
  Pallas kernels  523 us (23%)
  matrix products  306 us (13%)
  other arithmetic  133 us (6%)
  blocking collectives  49 us (2%)
    psum x1, waiting for transfers between devices, shards(): lax.psum(hw_part.astype(jnp.bfloat16), 'mp').astype(jnp.float32)  288 us
    pallas_call x1, Pallas kernels, lstm_forward(): pl.pallas_call(functools.partial(forward_kernel, size), grid=(WIN + 1,),...  262 us
    pallas_call x1, Pallas kernels, lstm_backward(): pl.pallas_call(functools.partial(backward_kernel, size), grid=(WIN,), in_...  260 us
    scatter-add x98, local copies, waits for them, and re-layouts, conv_back(): grad_chars.at[:, tap_index:tap_index + CHARS, :]  260 us
    unnamed x16, waiting for transfers between devices  114 us
    concatenate x56, local copies, waits for them, and re-layouts, char_columns(): jnp.concatenate([padded[:, tap_index:tap_index + CHARS, :] for tap_index...  102 us
    all_gather x1, waiting for transfers between devices, shards(): lax.all_gather(high_low, 'dp', axis=1, tiled=True)  72.8 us
    all_gather x1, waiting for transfers between devices, shards(): embed_all = lax.all_gather(embed_own, 'mp', axis=0)  57.3 us
  transfers between devices with their start and end apart: 14, of which 11 were waited for; matrix products, arithmetic and copies ran while one was open for 35% of the time, Pallas kernels for 0%

profile of v1, /device:TPU:0, one launch (start us, length us, event | category | flops | bytes accessed | tf_op | source)
XLA Modules:
  0.0 2282.2 jit_solution(11296995018138720123)
XLA Ops:
  33.6 107.1 %while.36 = (s32[]{:T(128)}, f32[14,20,2048]{2,1,0:T(8,128)}, s32[14,20,50]{2,1,0:T(8,128)S(1)}, bf16[262,16]{0,1:T(8,128)(2,1)S(1)}, bf16[112,2048]{1,0:T(8,128)(2,1)S(1)}, /*index=5*/s32[2048]{0:T(1024)S(1)}, s32[]{:T(128)}) while((s32[]{:T(128)}, f32[14,20,2048]{2,1,0:T(8,128)}, s32[14,20,50]{2,1,0:T(8,128)S(1)}, ...), condition=%wide.region_2.3_spmd.clone, body=%wide.region_0.2_spmd.clone.sunk | while | flops 471755776 | bytes 2911793 | solution.py:578
  147.8 72.8 %all-gather.8.cloned.1.call-done = bf16[2,2048,4096]{2,1,0:T(8,128)(2,1)} async-done(((bf16[2,512,4096]{2,1,0:T(8,128)(2,1)}), bf16[2,2048,4096]{2,1,0:T(8,128)(2,1)}) %all-gather.8.cloned.1.call-update) | async-done | bytes 33554448 | tf_op jit(solution)/shard_map/all_gather | solution.py:549
  263.8 36.5 %all-gather.12.cloned.1.call-done.win_ref = bf16[2,512,2048]{2,1,0:T(8,128)(2,1)} async-done(((bf16[2,128,2048]{2,1,0:T(8,128)(2,1)}), bf16[2,512,2048]{2,1,0:T(8,128)(2,1)}) %all-gather.12.cloned.1.call-update) | async-done | bytes 4194320 | tf_op jit(solution)/shard_map/all_gather | solution.py:553
  300.3 36.5 %all-gather.14.cloned.1.call-done.wst_ref = bf16[2,512,2048]{2,1,0:T(8,128)(2,1)} async-done(((bf16[2,128,2048]{2,1,0:T(8,128)(2,1)}), bf16[2,512,2048]{2,1,0:T(8,128)(2,1)}) %all-gather.14.cloned.1.call-update) | async-done | bytes 4194320 | tf_op jit(solution)/shard_map/all_gather | solution.py:554
  336.8 57.3 %all-gather.18.cloned.1.call-done = bf16[160,16,512]{2,1,0:T(8,128)(2,1)} async-done(((bf16[20,16,512]{2,1,0:T(8,128)(2,1)}), bf16[160,16,512]{2,1,0:T(8,128)(2,1)}) %all-gather.18.cloned.1.call-update) | async-done | bytes 2621456 | tf_op jit(solution)/shard_map/all_gather | solution.py:620
  394.9 262.5 %shard_map.265 = (bf16[20,128,512]{2,1,0:T(8,128)(2,1)}, f32[20,128,2048]{2,1,0:T(8,128)}, f32[20,128,2048]{2,1,0:T(8,128)}, f32[20,128,512]{2,1,0:T(8,128)}, f3...) custom-call(bf16[8,20,16,512]{3,2,1,0:T(8,128)(2,1)} %bitcast.270, ...), custom_call_target="tpu_custom_call" | custom-call | tf_op jit(solution)/shard_map/pallas_call | solution.py:307
  659.5 260.4 %shard_map.266 = (bf16[20,128,2048]{2,1,0:T(8,128)(2,1)}, bf16[20,128,2048]{2,1,0:T(8,128)(2,1)}, bf16[20,128,512]{2,1,0:T(8,128)(2,1)}, bf16[20,128,512]{2,1,0:...) custom-call(f32[20,128,2048]{2,1,0:T(8,128)} %get-tuple-element.362.gate0_ref, ...), custom_call_target="tpu_custom_call" | custom-call | tf_op jit(solution)/shard_map/pallas_call | solution.py:497
  928.5 113.7 %all-reduce.16.cloned.1.call-done = bf16[8,20,16,512]{3,2,0,1:T(8,128)(2,1)} async-done(((bf16[8,20,16,512]{3,2,0,1:T(8,128)(2,1)}), bf16[8,20,16,512]{3,2,0,1:T(8,128)(2,1)}) %all-reduce.16.cloned.1.call-update) | async-done | bytes 2621456
  1051.8 12.8 convolution_convert_fusion
  1064.6 22.6 copy.122
  1087.2 22.5 copy.123
  1109.7 14.3 multiply_convert_fusion.2
  1125.9 12.7 convert_bitcast_fusion
  1138.6 23.1 %pad_maximum_fusion = bf16[2,2048,2,2048]{3,1,2,0:T(8,128)(2,1)} fusion(bf16[1,2048,2,2048]{3,1,2,0:T(8,128)(2,1)} %copy.123, bf16[1,2048,2,2048]{3,1,2,0:T(8,128)(2,1)} %convert_bitcast_fusion), kind=kLoop, calls=%fused_computation.67 | loop fusion | flops 16777216 | bytes 67108864 | tf_op jit(solution)/shard_map/stack | solution.py:701
  1180.6 12.1 fusion.40
  1192.8 15.3 fusion.68
  1211.5 536.8 %while.37 = (s32[]{:T(128)}, f32[112,2048]{1,0:T(8,128)S(1)}, f32[262,16]{0,1:T(8,128)S(1)}, s32[14,20,50]{2,1,0:T(8,128)}, bf16[262,16]{0,1:T(8,128)(2,1)S(1)},...) while((s32[]{:T(128)}, f32[112,2048]{1,0:T(8,128)S(1)}, ...), condition=%wide.region_7.8_spmd.clone, body=%wide.region_5.7_spmd.clone.sunk | while | flops 1448498944 | bytes 55997560 | solution.py:741
  1782.0 11.4 copy.124
  1811.2 40.7 %all-reduce.9 = (f32[262,16]{0,1:T(8,128)}, f32[2048]{0:T(1024)}, f32[2,4096]{1,0:T(2,128)}, f32[512]{0:T(512)}) all-reduce(f32[262,16]{0,1:T(8,128)S(1)} %get-tuple-element.372, f32[2048]{0:T(1024)S(1)} %get-tuple-element.530, f32[2,4096]{1,0:T(2,128)S(1)} %pad_maximum_fusion.11, ...), channel_id=1, replica_groups=mesh['dp'=4,'mp'=8] {'dp','mp'}, use_global_device_ids=true, to_apply=%region_8.9 | all-reduce | flops 14944 | bytes 119552 | tf_op jit(solution)/shard_map/psum | solution.py:747
  1851.9 26.5 %all-reduce.18.cloned.1.call-done = (f32[7,16,2048]{2,1,0:T(8,128)}, f32[2,16384]{1,0:T(2,128)}) async-done(((f32[7,16,2048]{2,1,0:T(8,128)}, f32[2,16384]{1,0:T(2,128)}), (f32[7,16,2048]{2,1,0:T(8,128)}, f32[2,16384]{1,0:T(2,128)})) %all-reduce.18.cloned.1.call-update) | async-done | bytes 1048592 | tf_op jit(solution)/shard_map/psum | solution.py:747
  1881.4 43.1 %reduce-scatter.17.cloned.1.call-done = bf16[2,128,2048]{2,1,0:T(8,128)(2,1)} async-done(((bf16[2,512,2048]{2,1,0:T(8,128)(2,1)}), bf16[2,128,2048]{2,1,0:T(8,128)(2,1)}) %reduce-scatter.17.cloned.1.call-update) | async-done | bytes 1048592 | tf_op jit(solution)/shard_map/reduce_scatter | solution.py:676
  1927.3 44.3 %reduce-scatter.15.cloned.1.call-done = bf16[2,128,2048]{2,1,0:T(8,128)(2,1)} async-done(((bf16[2,512,2048]{2,1,0:T(8,128)(2,1)}), bf16[2,128,2048]{2,1,0:T(8,128)(2,1)}) %reduce-scatter.15.cloned.1.call-update) | async-done | bytes 1048592 | tf_op jit(solution)/shard_map/reduce_scatter | solution.py:675
  1974.4 287.5 %all-reduce.20.cloned.1.call-done = (bf16[2,512,4096]{1,2,0:T(8,128)(2,1)}, bf16[512,512]{1,0:T(8,128)(2,1)}) async-done(((bf16[2,512,4096]{1,2,0:T(8,128)(2,1)}, bf16[512,512]{1,0:T(8,128)(2,1)}), (bf16[2,512,4096]{1,2,0:T(8,128)(2,1)}, bf16[512,512]{1,0:T(8,128)(2,1)})) %all-reduce.20.cloned.1.call-update) | async-done | bytes 8912912 | tf_op jit(solution)/shard_map/psum | solution.py:761
  2261.9 12.5 copy.131
  (843 shorter events, 821.9 us)
Async XLA Ops:
  7.2 213.4 %all-gather.8.cloned.1.call-start = ((), (), s32[]{:S(2)}) async-start(), calls=%async_computation.5 | async-start | bytes 41943040 | tf_op jit(solution)/shard_map/all_gather | solution.py:549
  16.3 229.1 %all-gather.10.cloned.1.call-start = ((), (), s32[]{:S(2)}) async-start(), calls=%async_computation.6 | async-start | bytes 2621440 | tf_op jit(solution)/shard_map/all_gather | solution.py:550
  18.3 245.5 %all-gather.16.cloned.1.call-start = ((), (), s32[]{:S(2)}) async-start(), calls=%async_computation.9 | async-start | bytes 1310720 | tf_op jit(solution)/shard_map/all_gather | solution.py:555
  20.2 280.2 %all-gather.12.cloned.1.call-start = ((), (), s32[]{:S(2)}) async-start(), calls=%async_computation.7 | async-start | bytes 5242880 | tf_op jit(solution)/shard_map/all_gather | solution.py:553
  21.4 11.9 copy-start.32
  21.4 315.4 %all-gather.14.cloned.1.call-start = ((), (), s32[]{:S(2)}) async-start(), calls=%async_computation.8 | async-start | bytes 5242880 | tf_op jit(solution)/shard_map/all_gather | solution.py:554
  24.3 369.9 %all-gather.18.cloned.1.call-start = ((), (), s32[]{:S(2)}) async-start(), calls=%async_computation.14 | async-start | bytes 2949120 | tf_op jit(solution)/shard_map/all_gather | solution.py:620
  231.4 9.4 copy-start.5
  248.7 793.5 %all-reduce.16.cloned.1.call-start = ((), (), s32[]{:S(2)}) async-start(), calls=%async_computation.16 | async-start | bytes 5242880
  926.4 855.6 %reduce-scatter.11.cloned.1.call-start = ((), (), s32[]{:S(2)}) async-start(), calls=%async_computation.10 | async-start | bytes 41943040 | tf_op jit(solution)/shard_map/reduce_scatter | solution.py:753
  1087.2 22.5 copy-start.4
  1161.7 631.7 %reduce-scatter.13.cloned.1.call-start = ((), (), s32[]{:S(2)}) async-start(), calls=%async_computation.11 | async-start | bytes 2621440 | tf_op jit(solution)/shard_map/reduce_scatter | solution.py:756
  1165.6 640.8 %reduce-scatter.19.cloned.1.call-start = ((), (), s32[]{:S(2)}) async-start(), calls=%async_computation.15 | async-start | bytes 1310720
  1180.6 697.9 %all-reduce.18.cloned.1.call-start = ((), (), s32[]{:S(2)}) async-start(), calls=%async_computation.17 | async-start | bytes 2097152 | tf_op jit(solution)/shard_map/psum | solution.py:747
  1180.6 12.2 copy-start.7
  1180.6 12.2 copy-start.9
  1180.6 12.2 copy-start.47
  1192.8 15.3 copy-start.25
  1211.5 536.8 %copy-start.28 = (f32[7,2048]{1,0:T(8,128)S(1)}, f32[7,2048]{1,0:T(8,128)}, u32[]{:S(2)}) copy-start(f32[7,2048]{1,0:T(8,128)} %get-tuple-element.526) | copy-start | bytes 172036
  1749.3 175.2 %reduce-scatter.17.cloned.1.call-start = ((), (), s32[]{:S(2)}) async-start(), calls=%async_computation.13 | async-start | bytes 5242880 | tf_op jit(solution)/shard_map/reduce_scatter | solution.py:676
  1749.4 9.4 copy-start.16
  1761.2 210.4 %reduce-scatter.15.cloned.1.call-start = ((), (), s32[]{:S(2)}) async-start(), calls=%async_computation.12 | async-start | bytes 5242880 | tf_op jit(solution)/shard_map/reduce_scatter | solution.py:675
  1781.9 480.0 %all-reduce.20.cloned.1.call-start = ((), (), s32[]{:S(2)}) async-start(), calls=%async_computation.18 | async-start | bytes 17825792 | tf_op jit(solution)/shard_map/psum | solution.py:761
  2261.9 12.5 copy-start.24
  (64 other events, 211.0 us)
Sparse Core Ops, SparseCore 0:
  16.4 204.2 all-gather.7
  222.8 22.5 all-gather.9
  246.9 16.8 all-gather.15
  265.8 34.4 all-gather.11
  302.3 34.4 all-gather.13
  339.5 54.6 all-gather.17
  926.5 115.6 all-reduce.15
  1161.8 233.9 reduce-scatter.10
  1398.9 31.4 reduce-scatter.12
  1433.5 24.9 reduce-scatter.18
  1749.4 128.9 all-reduce.17
  1881.0 43.5 reduce-scatter.16
  1927.0 44.4 reduce-scatter.14
  1976.6 285.2 all-reduce.19

commit v2 on v1

--- a/solution.py
+++ b/solution.py
@@ -52,20 +52,6 @@
 def silu_slope(value):
     sigma = jax.nn.sigmoid(value)
     return sigma * (1.0 + value * (1.0 - sigma))
-
-
-def char_columns(id_block, table_low):
-    flat_ids = id_block.reshape(-1)
-    one_hot = flat_ids[:, None] == jnp.arange(VOCAB)[None, :]
-    char_vecs = jnp.dot(
-        one_hot.astype(jnp.bfloat16), table_low, preferred_element_type=jnp.float32
-    ).astype(jnp.bfloat16)
-    char_vecs = char_vecs.reshape(id_block.shape[0], CHARS, CDIM)
-    padded = jnp.pad(char_vecs, ((0, 0), (0, TAPS - 1), (0, 0)))
-    columns = jnp.concatenate(
-        [padded[:, tap_index : tap_index + CHARS, :] for tap_index in range(TAPS)], axis=2
-    )
-    return (one_hot, columns.reshape(-1, TAPS * CDIM))
 
 
 def sigmoid_of(value):
@@ -346,9 +332,8 @@
     da1_ref,
     ds0_ref,
     ds1_ref,
-    de0_ref,
-    de1_ref,
     bias_ref,
+    de_ref,
     cell_ref,
     part_ref,
     sum_ref,
@@ -357,6 +342,11 @@
     part_recv,
     all_send,
     all_recv,
+    held_ref,
+    embed_part_ref,
+    embed_got_ref,
+    embed_send,
+    embed_recv,
 ):
     step = pl.program_id(0)
     rows = reset_ref.shape[0]
@@ -370,7 +360,6 @@
     cnew_refs = (cnew0_ref, cnew1_ref)
     da_refs = (da0_ref, da1_ref)
     ds_refs = (ds0_ref, ds1_ref)
-    de_refs = (de0_ref, de1_ref)
 
     def time_of(way, at):
         return WIN - 1 - at if way == 0 else at
@@ -438,13 +427,48 @@
             part_ref[way] = partial.astype(jnp.bfloat16).reshape(size, part, PROJ)
             comm.send_parts(way)
 
+    def embed_copy(src, dst, offset):
+        return pltpu.make_async_remote_copy(
+            src_ref=src,
+            dst_ref=dst,
+            send_sem=embed_send.at[offset],
+            recv_sem=embed_recv.at[offset],
+            device_id={"mp": lax.rem(comm.me + offset, size)},
+            device_id_type=pl.DeviceIdType.MESH,
+        )
+
     def embed_step(way):
-        de_refs[way][0] = lax.dot_general(
+        now = time_of(way, step)
+        value = lax.dot_general(
             da_refs[way][0],
             win_ref[way],
             (((1,), (1,)), ((), ())),
             preferred_element_type=jnp.float32,
         )
+
+        @pl.when(step < WIN // 2)
+        def _():
+            held_ref[now] = value
+
+        @pl.when(step >= WIN // 2)
+        def _():
+            both = (value + held_ref[now]).astype(jnp.bfloat16)
+            embed_part_ref[now] = both.reshape(size, part, PROJ)
+            for offset in range(1, size):
+                peer = lax.rem(comm.me + offset, size)
+                embed_copy(
+                    embed_part_ref.at[now, peer], embed_got_ref.at[comm.me, now], offset
+                ).start()
+
+    def embed_finish():
+        total = embed_part_ref[:, comm.me].astype(jnp.float32)
+        for offset in range(1, size):
+            peer = lax.rem(comm.me + size - offset, size)
+            embed_copy(embed_got_ref.at[peer], embed_got_ref.at[peer], offset).wait_recv()
+            total = total + embed_got_ref[peer].astype(jnp.float32)
+        de_ref[...] = total.astype(jnp.bfloat16)
+        for offset in range(1, size):
+            embed_copy(embed_got_ref.at[comm.me], embed_got_ref.at[comm.me], offset).wait_send()
 
     @pl.when(step == 0)
     def _():
@@ -468,6 +492,10 @@
 
     cell_step(1)
     embed_step(1)
+
+    @pl.when(step == WIN - 1)
+    def _():
+        embed_finish()
 
 
 def lstm_backward(size, gates, cprevs, cnews, cots, stats, win, wst, wpr, reset):
@@ -490,7 +518,7 @@
     ins += [block((part, PROJ), next0), block((part, PROJ), now1)] * 2
     ins += [vmem] * 6
     outs = []
-    for size_of, kind in ((width, jnp.bfloat16), (PROJ, jnp.bfloat16), (PROJ, jnp.float32)):
+    for size_of, kind in ((width, jnp.bfloat16), (PROJ, jnp.bfloat16)):
         outs += [((rows, size_of), kind, now0), ((rows, size_of), kind, now1)]
     first_cot = jnp.stack([cots[0][last], cots[1][0]])
     first_stat = jnp.stack([stats[0][last], stats[1][0]])
@@ -499,20 +527,747 @@
         grid=(WIN,),
         in_specs=ins,
         out_specs=[block(shape, index) for shape, kind, index in outs]
-        + [pl.BlockSpec((2, 8, width), lambda w: (0, 0, 0))],
+        + [pl.BlockSpec((2, 8, width), lambda w: (0, 0, 0)), vmem],
         out_shape=[jax.ShapeDtypeStruct((WIN,) + shape, kind) for shape, kind, index in outs]
-        + [jax.ShapeDtypeStruct((2, 8, width), jnp.float32)],
+        + [
+            jax.ShapeDtypeStruct((2, 8, width), jnp.float32),
+            jax.ShapeDtypeStruct((WIN, part, PROJ), jnp.bfloat16),
+        ],
         scratch_shapes=[
             pltpu.VMEM((2, rows, units), jnp.float32),
             pltpu.VMEM((2, size, part, PROJ), jnp.bfloat16),
             pltpu.VMEM((2, size, part, PROJ), jnp.bfloat16),
             pltpu.VMEM((2, size, part, PROJ), jnp.bfloat16),
         ]
-        + [pltpu.SemaphoreType.DMA((2, size))] * 4,
+        + [pltpu.SemaphoreType.DMA((2, size))] * 4
+        + [
+            pltpu.VMEM((WIN, rows, PROJ), jnp.float32),
+            pltpu.VMEM((WIN, size, part, PROJ), jnp.bfloat16),
+            pltpu.VMEM((size, WIN, part, PROJ), jnp.bfloat16),
+        ]
+        + [pltpu.SemaphoreType.DMA((size,))] * 2,
         compiler_params=pltpu.CompilerParams(
             collective_id=2, has_side_effects=True, vmem_limit_bytes=56 * 2**20
         ),
     )(*gates, *cprevs, *cnews, *cots, *stats, win, wst, wpr, reset, first_cot, first_stat)
+
+
+SHIFTS = 8
+GROUP = SHIFTS * CDIM
+FBLOCK = 256
+
+
+def position_bound(first, width, taps):
+    index = first + lax.broadcasted_iota(jnp.int32, (1, width), 1)
+    bound = jnp.full((1, width), CHARS - 1, jnp.int32)
+    for exponent in range(taps - 1):
+        bound = bound - (index >= (FILTERS // 64) * (1 << exponent)).astype(jnp.int32)
+    return bound
+
+
+def group_counts():
+    full = (CHARS - SHIFTS) // SHIFTS + 1
+    return full, CHARS - full * SHIFTS
+
+
+def windows(vec_ref, count):
+    tokens = vec_ref.shape[1]
+    low = vec_ref[0:count].reshape(count * tokens, GROUP)
+    high = vec_ref[1 : count + 1].reshape(count * tokens, GROUP)
+    return jnp.concatenate([low, high], axis=1)
+
+
+def conv_forward_kernel(ids_ref, table_ref, weight_ref, total_ref, vec_ref):
+    block = pl.program_id(0)
+    groups, tokens, _ = vec_ref.shape
+    full, extra = group_counts()
+
+    @pl.when(block == 0)
+    def _():
+        vocab = table_ref.shape[1]
+        for group in range(groups):
+            acc = jnp.zeros((tokens, GROUP), jnp.float32)
+            for shift in range(SHIFTS):
+                place = group * SHIFTS + shift
+                if place < CHARS:
+                    column = ids_ref[:, place : place + 1]
+                    hot = column == lax.broadcasted_iota(jnp.int32, (tokens, vocab), 1)
+                    acc = acc + jnp.dot(
+                        jnp.where(hot, 1.0, 0.0).astype(jnp.bfloat16),
+                        table_ref[shift],
+                        preferred_element_type=jnp.float32,
+                    )
+            vec_ref[group] = acc.astype(jnp.bfloat16)
+
+    bound = position_bound(block * FBLOCK, FBLOCK, TAPS)
+    left = windows(vec_ref, full)
+    total = jnp.zeros((tokens, FBLOCK), jnp.float32)
+    for shift in range(SHIFTS):
+        out = jnp.dot(left, weight_ref[shift], preferred_element_type=jnp.float32)
+        values = jnp.exp(out).reshape(full, tokens, FBLOCK)
+        for group in range(full):
+            place = group * SHIFTS + shift
+            term = values[group]
+            if place > CHARS - TAPS:
+                term = jnp.where(bound >= place, term, 0.0)
+            total = total + term
+    total_ref[...] = total
+
+    @pl.when(block == 0)
+    def _():
+        for shift in range(extra):
+            out = jnp.dot(
+                vec_ref[full], weight_ref[shift, :GROUP], preferred_element_type=jnp.float32
+            )
+            total_ref[...] += jnp.where(bound >= full * SHIFTS + shift, jnp.exp(out), 0.0)
+
+
+def conv_forward(ids, table_shift, weights):
+    tokens = ids.shape[0]
+    groups = -(-CHARS // SHIFTS)
+    vocab = table_shift.shape[1]
+    return pl.pallas_call(
+        conv_forward_kernel,
+        grid=(FILTERS // FBLOCK,),
+        in_specs=[
+            pl.BlockSpec((tokens, CHARS), lambda f: (0, 0)),
+            pl.BlockSpec((SHIFTS, vocab, GROUP), lambda f: (0, 0, 0)),
+            pl.BlockSpec((SHIFTS, 2 * GROUP, FBLOCK), lambda f: (0, 0, f)),
+        ],
+        out_specs=[
+            pl.BlockSpec((tokens, FBLOCK), lambda f: (0, f)),
+            pl.BlockSpec((groups, tokens, GROUP), lambda f: (0, 0, 0)),
+        ],
+        out_shape=[
+            jax.ShapeDtypeStruct((tokens, FILTERS), jnp.float32),
+            jax.ShapeDtypeStruct((groups, tokens, GROUP), jnp.bfloat16),
+        ],
+        compiler_params=pltpu.CompilerParams(vmem_limit_bytes=56 * 2**20),
+        cost_estimate=pl.CostEstimate(
+            flops=2 * tokens * CHARS * 256 * FILTERS,
+            bytes_accessed=12 * 2**20,
+            transcendentals=tokens * CHARS * FILTERS,
+        ),
+    )(ids, table_shift, weights)
+
+
+def conv_shift_step(
+    shift, vec_ref, turned_ref, turned_extra_ref, ratio_ref, weight_ref, grad_ref, low_ref, char_ref, held_ref
+):
+    groups, tokens, _ = vec_ref.shape
+    full, extra = group_counts()
+    left = windows(vec_ref, full)
+    own_rows = pl.ds(pl.multiple_of(shift * CDIM, CDIM), TAPS * CDIM)
+
+    @pl.when(shift == 0)
+    def _():
+        grad_ref[...] = jnp.zeros(grad_ref.shape, jnp.float32)
+        char_ref[...] = jnp.zeros(char_ref.shape, jnp.float32)
+
+    @pl.loop(0, FILTERS // FBLOCK)
+    def _(block):
+        cols = pl.ds(pl.multiple_of(block * FBLOCK, FBLOCK), FBLOCK)
+        bound = position_bound(block * FBLOCK, FBLOCK, TAPS)
+        ratio = ratio_ref[:, cols]
+        out = jnp.dot(left, weight_ref[0, :, cols], preferred_element_type=jnp.float32)
+        values = jnp.exp(out).reshape(full, tokens, FBLOCK)
+        for group in range(full):
+            term = values[group] * ratio
+            if (group + 1) * SHIFTS - 1 > CHARS - TAPS:
+                term = jnp.where(bound >= group * SHIFTS + shift, term, 0.0)
+            low_ref[pl.ds(group * tokens, tokens), cols] = term.astype(jnp.bfloat16)
+        held_ref[...] = jnp.dot(
+            turned_ref[...], low_ref[:, cols], preferred_element_type=jnp.float32
+        )
+        grad_ref[:, cols] += held_ref[own_rows, :]
+
+    back = lax.dot_general(
+        low_ref[...],
+        weight_ref[0],
+        (((1,), (1,)), ((), ())),
+        preferred_element_type=jnp.float32,
+    ).reshape(full, tokens, 2 * GROUP)
+    for group in range(full):
+        char_ref[group] += back[group, :, :GROUP]
+        char_ref[group + 1] += back[group, :, GROUP:]
+
+    @pl.when(shift < extra)
+    def _():
+        cols = slice(0, FBLOCK)
+        bound = position_bound(0, FBLOCK, TAPS)
+        out = jnp.dot(
+            vec_ref[full], weight_ref[0, :GROUP, cols], preferred_element_type=jnp.float32
+        )
+        term = jnp.exp(out) * ratio_ref[:, cols]
+        term = jnp.where(bound >= full * SHIFTS + shift, term, 0.0).astype(jnp.bfloat16)
+        held_ref[...] = jnp.concatenate(
+            [
+                jnp.dot(turned_extra_ref[...], term, preferred_element_type=jnp.float32),
+                jnp.zeros((GROUP, FBLOCK), jnp.float32),
+            ],
+            axis=0,
+        )
+        grad_ref[:, cols] += held_ref[own_rows, :]
+        char_ref[full] += lax.dot_general(
+            term,
+            weight_ref[0, :GROUP, cols],
+            (((1,), (1,)), ((), ())),
+            preferred_element_type=jnp.float32,
+        )
+
+
+def table_gradient(hot_ref, hot_extra_ref, char_ref, vocab):
+    tokens = char_ref.shape[1]
+    full, extra = group_counts()
+    lane = lax.broadcasted_iota(jnp.int32, (vocab, GROUP), 1) // CDIM
+
+    def split(value):
+        high = value.astype(jnp.bfloat16)
+        rest = (value - high.astype(jnp.float32)).astype(jnp.bfloat16)
+        return jnp.concatenate([high, rest], axis=1)
+
+    main = split(char_ref[0:full].reshape(full * tokens, GROUP))
+    last = split(char_ref[full])
+    acc = jnp.zeros((vocab, GROUP), jnp.float32)
+    for at in range(SHIFTS):
+        row = hot_ref[at : at + 1, :]
+        hot = row == lax.broadcasted_iota(jnp.int32, (vocab, full * tokens), 0)
+        out = jnp.dot(
+            jnp.where(hot, 1.0, 0.0).astype(jnp.bfloat16),
+            main,
+            preferred_element_type=jnp.float32,
+        )
+        if at < extra:
+            row = hot_extra_ref[at : at + 1, :]
+            hot = row == lax.broadcasted_iota(jnp.int32, (vocab, tokens), 0)
+            out = out + jnp.dot(
+                jnp.where(hot, 1.0, 0.0).astype(jnp.bfloat16),
+                last,
+                preferred_element_type=jnp.float32,
+            )
+        acc = jnp.where(lane == at, out[:, :GROUP] + out[:, GROUP:], acc)
+    return acc
+
+
+def conv_backward_kernel(
+    hot_ref,
+    hot_extra_ref,
+    vec_ref,
+    turned_ref,
+    turned_extra_ref,
+    ratio_ref,
+    weight_ref,
+    grad_ref,
+    table_ref,
+    low_ref,
+    char_ref,
+    held_ref,
+):
+    shift = pl.program_id(0)
+    conv_shift_step(
+        shift, vec_ref, turned_ref, turned_extra_ref, ratio_ref, weight_ref, grad_ref, low_ref, char_ref, held_ref
+    )
+
+    @pl.when(shift == SHIFTS - 1)
+    def _():
+        table_ref[...] = table_gradient(hot_ref, hot_extra_ref, char_ref, table_ref.shape[0])
+
+
+def conv_operands(ids, vectors):
+    groups, tokens, _ = vectors.shape
+    full, extra = group_counts()
+    turned = jnp.transpose(vectors, (0, 2, 1))
+    pieces = [
+        jnp.transpose(turned[half : half + full], (1, 0, 2)).reshape(GROUP, full * tokens)
+        for half in range(2)
+    ]
+    ids_turned = ids.T
+    hot_main = jnp.transpose(ids_turned[: full * SHIFTS].reshape(full, SHIFTS, tokens), (1, 0, 2))
+    hot_main = hot_main.reshape(SHIFTS, full * tokens)
+    hot_extra = ids_turned[full * SHIFTS :]
+    return hot_main, hot_extra, vectors, jnp.concatenate(pieces, axis=0), turned[full]
+
+
+def conv_backward(ids, vectors, ratio, weights):
+    groups, tokens, _ = vectors.shape
+    full, _ = group_counts()
+    vocab = -(-VOCAB // 8) * 8
+    grad, table = pl.pallas_call(
+        conv_backward_kernel,
+        grid=(SHIFTS,),
+        in_specs=[pl.BlockSpec(memory_space=pltpu.VMEM)] * 6
+        + [pl.BlockSpec((1, 2 * GROUP, FILTERS), lambda s: (s, 0, 0))],
+        out_specs=[
+            pl.BlockSpec((TAPS * CDIM, FILTERS), lambda s: (0, 0)),
+            pl.BlockSpec((vocab, GROUP), lambda s: (0, 0)),
+        ],
+        out_shape=[
+            jax.ShapeDtypeStruct((TAPS * CDIM, FILTERS), jnp.float32),
+            jax.ShapeDtypeStruct((vocab, GROUP), jnp.float32),
+        ],
+        scratch_shapes=[
+            pltpu.VMEM((full * tokens, FILTERS), jnp.bfloat16),
+            pltpu.VMEM((groups, tokens, GROUP), jnp.float32),
+            pltpu.VMEM((2 * GROUP, FBLOCK), jnp.float32),
+        ],
+        compiler_params=pltpu.CompilerParams(vmem_limit_bytes=58 * 2**20),
+        cost_estimate=pl.CostEstimate(
+            flops=6 * tokens * CHARS * 256 * FILTERS,
+            bytes_accessed=16 * 2**20,
+            transcendentals=tokens * CHARS * FILTERS,
+        ),
+    )(*conv_operands(ids, vectors), ratio, weights)
+    table = table.reshape(vocab, SHIFTS, CDIM).sum(axis=1)[:VOCAB]
+    return grad, table
+
+
+MESH = pl.DeviceIdType.MESH
+CHUNK_ROWS = 16
+
+
+def tail_kernel(
+    chunks,
+    hot_ref,
+    hot_extra_ref,
+    vec_ref,
+    turned_ref,
+    turned_extra_ref,
+    ratio_ref,
+    weight_ref,
+    part1_ref,
+    part0_ref,
+    sum_ref,
+    conv_ref,
+    table_ref,
+    grad_ref,
+    low_ref,
+    char_ref,
+    held_ref,
+    own_ref,
+    got_y_ref,
+    got_x_ref,
+    got_z_ref,
+    all_z_ref,
+    all_x_ref,
+    wide_ref,
+    conv_acc_ref,
+    conv_got_ref,
+    conv_two_ref,
+    conv_in_ref,
+    table_acc_ref,
+    table_got_ref,
+    load_sem,
+    store_sem,
+    y_send,
+    y_recv,
+    x_send,
+    x_recv,
+    z_send,
+    z_recv,
+    g_send,
+    g_recv,
+    h_send,
+    h_recv,
+    small_send,
+    small_recv,
+):
+    tick = pl.program_id(0)
+    dp = lax.axis_index("dp")
+    mp = lax.axis_index("mp")
+    core, high = lax.rem(dp, 2), dp // 2
+    near, ring = lax.rem(mp, 2), mp // 2
+    per_layer = chunks // 2
+    width = FILTERS * 2
+    quarter = width // 4
+    core_peer = {"dp": dp + 1 - 2 * core, "mp": mp}
+    high_peer = {"dp": dp + 2 - 4 * high, "mp": mp}
+    near_peer = {"dp": dp, "mp": mp + 1 - 2 * near}
+
+    def ring_index(offset):
+        return lax.rem(ring + offset, 4)
+
+    def ring_peer(offset):
+        return {"dp": dp, "mp": 2 * ring_index(offset) + near}
+
+    def remote(src, dst, send, recv, peer):
+        return pltpu.make_async_remote_copy(
+            src_ref=src, dst_ref=dst, send_sem=send, recv_sem=recv, device_id=peer, device_id_type=MESH
+        )
+
+    def y_copy(part, chunk, row):
+        return remote(
+            part.at[1 - high, row], got_y_ref.at[chunk], y_send.at[chunk], y_recv.at[chunk], high_peer
+        )
+
+    def load(chunk, act):
+        slot = lax.rem(chunk, 2)
+        for layer, part in enumerate((part1_ref, part0_ref)):
+
+            @pl.when(chunk // per_layer == layer)
+            def _():
+                copy = pltpu.make_async_copy(
+                    part.at[high, chunk - layer * per_layer], own_ref.at[slot], load_sem.at[slot]
+                )
+                getattr(copy, act)()
+
+    def x_copy(chunk):
+        return remote(
+            got_y_ref.at[chunk, 1 - near],
+            got_x_ref.at[chunk],
+            x_send.at[chunk],
+            x_recv.at[chunk],
+            near_peer,
+        )
+
+    def columns(index):
+        return pl.ds(pl.multiple_of(index * quarter, quarter), quarter)
+
+    def z_copy(chunk, offset):
+        return remote(
+            got_x_ref.at[chunk, :, columns(ring_index(offset))],
+            got_z_ref.at[chunk, offset - 1],
+            z_send.at[chunk, offset - 1],
+            z_recv.at[chunk, offset - 1],
+            ring_peer(offset),
+        )
+
+    def g_copy(chunk, offset, incoming):
+        cols = columns(ring_index(4 - offset) if incoming else ring)
+        return remote(
+            all_z_ref.at[chunk, :, cols],
+            all_z_ref.at[chunk, :, cols],
+            g_send.at[chunk, offset - 1],
+            g_recv.at[chunk, offset - 1],
+            ring_peer(offset),
+        )
+
+    def h_copy(chunk):
+        return remote(
+            all_z_ref.at[chunk], all_x_ref.at[chunk], h_send.at[chunk], h_recv.at[chunk], near_peer
+        )
+
+    def store(chunk):
+        slot = lax.rem(chunk, 2)
+        layer = 1 - chunk // per_layer
+        return pltpu.make_async_copy(
+            wide_ref.at[slot],
+            sum_ref.at[layer, lax.rem(chunk, per_layer)],
+            store_sem.at[slot],
+        )
+
+    def when_chunk(chunk, body):
+        @pl.when(jnp.logical_and(chunk >= 0, chunk < chunks))
+        def _():
+            body(chunk)
+
+    def do_y(chunk):
+        y_copy(part1_ref, chunk, 0).wait_recv()
+        load(chunk, "wait")
+        slot = lax.rem(chunk, 2)
+        for half in range(2):
+            got_y_ref[chunk, half] = (
+                got_y_ref[chunk, half].astype(jnp.float32) + own_ref[slot, half].astype(jnp.float32)
+            ).astype(jnp.bfloat16)
+        x_copy(chunk).start()
+
+        @pl.when(chunk + 2 < chunks)
+        def _():
+            load(chunk + 2, "start")
+
+    def do_x(chunk):
+        x_copy(chunk).wait_recv()
+        got_x_ref[chunk] = (
+            got_x_ref[chunk].astype(jnp.float32) + got_y_ref[chunk, near].astype(jnp.float32)
+        ).astype(jnp.bfloat16)
+        for offset in range(1, 4):
+            z_copy(chunk, offset).start()
+
+    def do_z(chunk):
+        cols = columns(ring)
+        total = got_x_ref[chunk, :, cols].astype(jnp.float32)
+        for offset in range(1, 4):
+            z_copy(chunk, offset).wait_recv()
+            total = total + got_z_ref[chunk, offset - 1].astype(jnp.float32)
+        all_z_ref[chunk, :, cols] = total.astype(jnp.bfloat16)
+        for offset in range(1, 4):
+            g_copy(chunk, offset, False).start()
+
+    def do_g(chunk):
+        for offset in range(1, 4):
+            g_copy(chunk, offset, True).wait_recv()
+        h_copy(chunk).start()
+
+    def do_h(chunk):
+        h_copy(chunk).wait_recv()
+
+        @pl.when(chunk >= 2)
+        def _():
+            store(chunk - 2).wait()
+
+        slot = lax.rem(chunk, 2)
+        wide_ref[slot, near] = all_z_ref[chunk].astype(jnp.float32)
+        wide_ref[slot, 1 - near] = all_x_ref[chunk].astype(jnp.float32)
+        store(chunk).start()
+
+    def small_copies(stage):
+        if stage == 0:
+            copies = [
+                remote(
+                    conv_two_ref.at[1, y],
+                    conv_in_ref.at[y],
+                    small_send.at[0, y],
+                    small_recv.at[0, y],
+                    core_peer,
+                )
+                for y in range(2)
+            ]
+            peer = core_peer
+        else:
+            if stage == 1:
+                src = conv_two_ref.at[0, 1 - high]
+                peer = high_peer
+            else:
+                src = conv_acc_ref.at[stage - 2]
+                bit = 1 << (stage - 2)
+                flip = lax.rem(mp // bit, 2)
+                peer = {"dp": dp, "mp": mp + bit - 2 * bit * flip}
+            copies = [
+                remote(
+                    src,
+                    conv_got_ref.at[stage - 1],
+                    small_send.at[stage, 0],
+                    small_recv.at[stage, 0],
+                    peer,
+                )
+            ]
+        copies.append(
+            remote(
+                table_acc_ref.at[stage],
+                table_got_ref.at[stage],
+                small_send.at[stage, 2],
+                small_recv.at[stage, 2],
+                peer,
+            )
+        )
+        return copies
+
+    def small_start(stage):
+        for copy in small_copies(stage):
+            copy.start()
+
+    def small_finish(stage):
+        for copy in small_copies(stage):
+            copy.wait()
+        total = table_acc_ref[stage] + table_got_ref[stage]
+        if stage < 4:
+            table_acc_ref[stage + 1] = total
+        else:
+            table_ref[...] = total
+        if stage == 0:
+            for y in range(2):
+                conv_two_ref[0, y] = conv_two_ref[0, y] + conv_in_ref[y]
+        elif stage == 1:
+            conv_acc_ref[0] = conv_two_ref[0, high] + conv_got_ref[0]
+        else:
+            value = conv_acc_ref[stage - 2] + conv_got_ref[stage - 1]
+            if stage < 4:
+                conv_acc_ref[stage - 1] = value
+            else:
+                conv_ref[...] = value
+
+    @pl.when(tick == 0)
+    def _():
+        barrier = pltpu.get_barrier_semaphore()
+        for peer in [core_peer, high_peer, near_peer] + [ring_peer(offset) for offset in (1, 2, 3)]:
+            pl.semaphore_signal(barrier, inc=1, device_id=peer, device_id_type=MESH)
+        pl.semaphore_wait(barrier, 6)
+
+        @pl.loop(0, per_layer)
+        def _(row):
+            y_copy(part1_ref, row, row).start()
+
+        @pl.loop(0, per_layer)
+        def _(row):
+            y_copy(part0_ref, per_layer + row, row).start()
+
+        load(jnp.int32(0), "start")
+        load(jnp.int32(1), "start")
+
+    @pl.when(tick < SHIFTS)
+    def _():
+        conv_shift_step(
+            tick,
+            vec_ref,
+            turned_ref,
+            turned_extra_ref,
+            ratio_ref,
+            weight_ref,
+            grad_ref,
+            low_ref,
+            char_ref,
+            held_ref,
+        )
+
+    @pl.when(tick == SHIFTS - 1)
+    def _():
+        table_acc_ref[0] = table_gradient(hot_ref, hot_extra_ref, char_ref, table_ref.shape[0])
+        span = FILTERS // 4
+        for y in range(2):
+            mine = pl.ds(pl.multiple_of((2 * y + core) * span, span), span)
+            theirs = pl.ds(pl.multiple_of((2 * y + 1 - core) * span, span), span)
+            conv_two_ref[0, y] = grad_ref[:, mine]
+            conv_two_ref[1, y] = grad_ref[:, theirs]
+        small_start(0)
+
+    for stage in range(5):
+
+        @pl.when(tick == SHIFTS + stage)
+        def _():
+            small_finish(stage)
+            if stage < 4:
+                small_start(stage + 1)
+
+    for beat in range(2):
+        at = tick * 2 + beat
+        when_chunk(at, do_y)
+        when_chunk(at - 1, do_x)
+        when_chunk(at - 2, do_z)
+        when_chunk(at - 3, do_g)
+        when_chunk(at - 4, do_h)
+
+    @pl.when(tick == chunks // 2 + 1)
+    def _():
+        for chunk in (chunks - 2, chunks - 1):
+            store(jnp.int32(chunk)).wait()
+
+        @pl.loop(0, chunks)
+        def _(chunk):
+            y_copy(part1_ref, chunk, 0).wait_send()
+            x_copy(chunk).wait_send()
+            for offset in range(1, 4):
+                z_copy(chunk, offset).wait_send()
+                g_copy(chunk, offset, False).wait_send()
+            h_copy(chunk).wait_send()
+
+
+def conv_backward_and_sum(ids, vectors, ratio, weights, parts):
+    groups, tokens, _ = vectors.shape
+    full, _ = group_counts()
+    vocab = -(-VOCAB // 8) * 8
+    width = parts[0].shape[1]
+    rows = parts[0].shape[0] // 2
+    per_layer = rows // (2 * CHUNK_ROWS)
+    chunks = 2 * per_layer
+    parts = [part.reshape(2, per_layer, 2, CHUNK_ROWS, width) for part in parts]
+    conv_rows = TAPS * CDIM
+    span = FILTERS // 4
+    bf16, f32 = jnp.bfloat16, jnp.float32
+    dma = pltpu.SemaphoreType.DMA
+    last = SHIFTS - 1
+    sums, grad, table = pl.pallas_call(
+        functools.partial(tail_kernel, chunks),
+        grid=(chunks // 2 + 2,),
+        in_specs=[pl.BlockSpec(memory_space=pltpu.VMEM)] * 6
+        + [pl.BlockSpec((1, 2 * GROUP, FILTERS), lambda t: (jnp.minimum(t, last), 0, 0))]
+        + [pl.BlockSpec(memory_space=pl.ANY)] * 2,
+        out_specs=[
+            pl.BlockSpec(memory_space=pl.ANY),
+            pl.BlockSpec(memory_space=pltpu.VMEM),
+            pl.BlockSpec(memory_space=pltpu.VMEM),
+        ],
+        out_shape=[
+            jax.ShapeDtypeStruct((2, per_layer, 2, CHUNK_ROWS, width), f32),
+            jax.ShapeDtypeStruct((conv_rows, span), f32),
+            jax.ShapeDtypeStruct((vocab, GROUP), f32),
+        ],
+        scratch_shapes=[
+            pltpu.VMEM((conv_rows, FILTERS), f32),
+            pltpu.VMEM((full * tokens, FILTERS), bf16),
+            pltpu.VMEM((groups, tokens, GROUP), f32),
+            pltpu.VMEM((2 * GROUP, FBLOCK), f32),
+            pltpu.VMEM((2, 2, CHUNK_ROWS, width), bf16),
+            pltpu.VMEM((chunks, 2, CHUNK_ROWS, width), bf16),
+            pltpu.VMEM((chunks, CHUNK_ROWS, width), bf16),
+            pltpu.VMEM((chunks, 3, CHUNK_ROWS, width // 4), bf16),
+            pltpu.VMEM((chunks, CHUNK_ROWS, width), bf16),
+            pltpu.VMEM((chunks, CHUNK_ROWS, width), bf16),
+            pltpu.VMEM((2, 2, CHUNK_ROWS, width), f32),
+            pltpu.VMEM((3, conv_rows, span), f32),
+            pltpu.VMEM((4, conv_rows, span), f32),
+            pltpu.VMEM((2, 2, conv_rows, span), f32),
+            pltpu.VMEM((2, conv_rows, span), f32),
+            pltpu.VMEM((5, vocab, GROUP), f32),
+            pltpu.VMEM((5, vocab, GROUP), f32),
+            dma((2,)),
+            dma((2,)),
+            dma((chunks,)),
+            dma((chunks,)),
+            dma((chunks,)),
+            dma((chunks,)),
+            dma((chunks, 3)),
+            dma((chunks, 3)),
+            dma((chunks, 3)),
+            dma((chunks, 3)),
+            dma((chunks,)),
+            dma((chunks,)),
+            dma((5, 3)),
+            dma((5, 3)),
+        ],
+        compiler_params=pltpu.CompilerParams(
+            collective_id=3, has_side_effects=True, vmem_limit_bytes=62 * 2**20
+        ),
+    )(*conv_operands(ids, vectors), ratio, weights, *parts)
+    table = table.reshape(vocab, SHIFTS, CDIM).sum(axis=1)[:VOCAB]
+    return sums.reshape(2, rows, width), grad, table
+
+
+def swap(value, axis, bit):
+    size = lax.axis_size(axis)
+    return lax.ppermute(value, axis, [(index, index ^ bit) for index in range(size)])
+
+
+def halves(value, index, dim):
+    half = value.shape[dim] // 2
+    own = lax.dynamic_slice_in_dim(value, index * half, half, dim)
+    other = lax.dynamic_slice_in_dim(value, (1 - index) * half, half, dim)
+    return own, other
+
+
+def scatter_sum(value, axis, dim, paired):
+    if not paired:
+        return lax.psum_scatter(value, axis, scatter_dimension=dim, tiled=True)
+    index = lax.axis_index(axis)
+    shape = value.shape
+    quarter = shape[dim] // 4
+    parts = value.reshape(shape[:dim] + (2, 2, quarter) + shape[dim + 1 :])
+    low, high = index % 2, index // 2
+    own = lax.dynamic_index_in_dim(parts, low, dim + 1, False)
+    other = lax.dynamic_index_in_dim(parts, 1 - low, dim + 1, False)
+    got = swap(other, axis, 1)
+    both = (own.astype(jnp.float32) + got.astype(jnp.float32)).astype(value.dtype)
+    own = lax.dynamic_index_in_dim(both, high, dim, False)
+    other = lax.dynamic_index_in_dim(both, 1 - high, dim, False)
+    got = swap(other, axis, 2)
+    return (own.astype(jnp.float32) + got.astype(jnp.float32)).astype(value.dtype)
+
+
+def weight_part(left, right):
+    tokens, depth = left.shape
+    core = lax.axis_index("dp") % 2
+    parts = left.reshape(tokens, 2, 2, depth // 4)
+    own = lax.dynamic_index_in_dim(parts, core, 2, False).reshape(tokens, depth // 2)
+    other = lax.dynamic_index_in_dim(parts, 1 - core, 2, False).reshape(tokens, depth // 2)
+    left_all = jnp.concatenate([own, swap(other, "dp", 1)], axis=0)
+    right_all = jnp.concatenate([right, swap(right, "dp", 1)], axis=0)
+    return jnp.dot(left_all.T, right_all, preferred_element_type=jnp.float32).astype(jnp.bfloat16)
+
+
+def weight_grad(left, right, paired):
+    if not paired:
+        part = jnp.dot(left.T, right, preferred_element_type=jnp.float32).astype(jnp.bfloat16)
+        return lax.psum_scatter(part, "dp", scatter_dimension=0, tiled=True)
+    own, other = halves(weight_part(left, right), lax.axis_index("dp") // 2, 0)
+    return (own.astype(jnp.float32) + swap(other, "dp", 2).astype(jnp.float32)).astype(jnp.bfloat16)
 
 
 def shards(
@@ -541,6 +1296,7 @@
     gate_local = lstm_bias.shape[1]
     mp_index = lax.axis_index("mp")
     mp_size = lax.axis_size("mp")
+    paired = lax.axis_size("dp") == 4 and mp_size == 8
     dp_index = lax.axis_index("dp")
     dp_width = conv_weight.shape[2]
     high_low = highway_weight.astype(jnp.bfloat16)
@@ -559,23 +1315,29 @@
     conv_matrix = (conv_full * tap_mask[:, None, :].astype(jnp.bfloat16)).reshape(
         TAPS * CDIM, FILTERS
     )
-    valid_mask = (jnp.arange(CHARS)[:, None] <= CHARS - widths[None, :]).astype(jnp.float32)
+    conv_shifted = jnp.stack(
+        [
+            jnp.pad(conv_matrix, ((CDIM * shift, 2 * GROUP - CDIM * (shift + TAPS)), (0, 0)))
+            for shift in range(SHIFTS)
+        ]
+    )
     counts = (CHARS + 1 - widths).astype(jnp.float32)
     table_low = char_table.astype(jnp.bfloat16)
-    block_size = math.gcd(tok_share, WIN)
+    table_shifted = jnp.stack(
+        [
+            jnp.pad(
+                table_low,
+                ((0, -VOCAB % UNIT_BLOCK), (CDIM * shift, GROUP - CDIM * (shift + 1))),
+            )
+            for shift in range(SHIFTS)
+        ]
+    )
     rows_own = row_count // mp_size
-    char_ids = char_ids.reshape(rows_own, WIN, CHARS).transpose(1, 0, 2).reshape(tok_share, CHARS)
-    id_blocks = char_ids.reshape(tok_share // block_size, block_size, CHARS)
-
-    def pool_block(id_block):
-        one_hot, columns = char_columns(id_block, table_low)
-        conv_out = jnp.dot(columns, conv_matrix, preferred_element_type=jnp.float32).reshape(
-            block_size, CHARS, FILTERS
-        )
-        exp_total = jnp.sum(jnp.exp(conv_out) * valid_mask, axis=1)
-        return jnp.log(exp_total / counts)
-
-    pooled = lax.map(pool_block, id_blocks).reshape(tok_share, FILTERS)
+    ids_time = char_ids.reshape(rows_own, WIN, CHARS).transpose(1, 0, 2).reshape(tok_share, CHARS)
+    tok_pad = -tok_share % 16
+    ids_time = jnp.pad(ids_time, ((0, tok_pad), (0, 0)))
+    exp_total, char_vecs = conv_forward(ids_time, table_shifted, conv_shifted)
+    pooled = jnp.log(exp_total[:tok_share] / counts)
     pre_pool = pooled + conv_bias
     layer_value = jax.nn.silu(pre_pool)
     kept_inputs = []
@@ -653,13 +1415,9 @@
     back = lstm_backward(
         mp_size, gates, cprevs, cnews, cots, stats, input_full, state_full, lproj_full, reset_wide
     )
-    das, dss, des = (back[2 * index : 2 * index + 2] for index in range(3))
-    grad_bias = jnp.sum(back[6], axis=1)
-    embed_parts = (des[0] + des[1]).astype(jnp.bfloat16)
-    embed_parts = jnp.transpose(embed_parts.reshape(WIN, mp_size, part_rows, PROJ), (1, 0, 2, 3))
-    grad_embed_local = lax.psum_scatter(embed_parts, "mp", scatter_dimension=0, tiled=True)
-    grad_embed_local = grad_embed_local.reshape(WIN, part_rows, PROJ)[:, :rows_own]
-    grad_embed_local = grad_embed_local.reshape(tok_share, PROJ)
+    das, dss = back[0:2], back[2:4]
+    grad_bias = jnp.sum(back[4], axis=1)
+    grad_embed_local = back[5][:, :rows_own].reshape(tok_share, PROJ)
 
     def outer(left, right):
         return jnp.dot(
@@ -668,18 +1426,20 @@
             preferred_element_type=jnp.float32,
         ).astype(jnp.bfloat16)
 
-    grad_input = jnp.stack([outer(embed_time, das[way]) for way in range(2)])
-    grad_state = jnp.stack([outer(hprevs[way], das[way]) for way in range(2)])
-    grad_lproj = jnp.stack([outer(lows[way], dss[way]) for way in range(2)])
     grad_input, grad_state, grad_lproj = (
-        lax.psum_scatter(grad_input, "dp", scatter_dimension=1, tiled=True).astype(jnp.float32),
-        lax.psum_scatter(grad_state, "dp", scatter_dimension=1, tiled=True).astype(jnp.float32),
-        lax.psum_scatter(grad_lproj, "dp", scatter_dimension=2, tiled=True).astype(jnp.float32),
+        jnp.stack(
+            [
+                scatter_sum(outer(left[way], right[way]), "dp", dim, paired).astype(jnp.float32)
+                for way in range(2)
+            ]
+        )
+        for left, right, dim in (((embed_time,) * 2, das, 0), (hprevs, das, 0), (lows, dss, 1))
     )
     grad_pb = jnp.sum(grad_embed_local.astype(jnp.float32), axis=0)
-    grad_hw = [None, None]
+    summed = []
     grad_hb = [None, None]
-    grad_pw = jnp.dot(top_low.T, grad_embed_local, preferred_element_type=jnp.float32)
+    pw_part = weight_grad(top_low, grad_embed_local, paired)
+    pw_sum = lax.psum(pw_part, "mp")
     grad_layer = jnp.dot(grad_embed_local, proj_full.T, preferred_element_type=jnp.float32)
     for layer_index in (1, 0):
         layer_in = kept_inputs[layer_index]
@@ -691,77 +1451,47 @@
         )
         grad_trans = grad_layer * (1.0 - gate_value) * silu_slope(transform)
         grad_mixed = jnp.concatenate([grad_trans, grad_gate], axis=1).astype(jnp.bfloat16)
-        grad_hw[layer_index] = jnp.dot(
-            layer_in.astype(jnp.bfloat16).T, grad_mixed, preferred_element_type=jnp.float32
-        )
+        layer_low = layer_in.astype(jnp.bfloat16)
+        if paired:
+            summed.append(weight_part(layer_low, grad_mixed))
+        else:
+            summed.append(lax.psum(weight_grad(layer_low, grad_mixed, paired), "mp"))
         grad_hb[layer_index] = jnp.sum(grad_mixed.astype(jnp.float32), axis=0)
         grad_layer = grad_layer * gate_value + jnp.dot(
             grad_mixed, high_full[layer_index].T, preferred_element_type=jnp.float32
         )
-    hw_terms = jnp.stack(grad_hw).reshape(2, FILTERS, 2, FILTERS)
     grad_pre_pool = grad_layer * silu_slope(pre_pool)
     grad_cb = jnp.sum(grad_pre_pool, axis=0)
 
-    def conv_back(carry, inputs):
-        grad_conv, grad_table = carry
-        id_block, grad_block = inputs
-        one_hot, columns = char_columns(id_block, table_low)
-        conv_out = jnp.dot(columns, conv_matrix, preferred_element_type=jnp.float32).reshape(
-            block_size, CHARS, FILTERS
-        )
-        exp_values = jnp.exp(conv_out) * valid_mask
-        exp_total = jnp.sum(exp_values, axis=1)
-        grad_conv_out = (
-            (grad_block[:, None, :] * exp_values / exp_total[:, None, :])
-            .astype(jnp.bfloat16)
-            .reshape(block_size * CHARS, FILTERS)
-        )
-        grad_conv = grad_conv + jnp.dot(
-            columns.T, grad_conv_out, preferred_element_type=jnp.float32
-        )
-        grad_columns = jnp.dot(
-            grad_conv_out, conv_matrix.T, preferred_element_type=jnp.float32
-        ).reshape(block_size, CHARS, TAPS, CDIM)
-        grad_chars = jnp.zeros((block_size, CHARS + TAPS - 1, CDIM), jnp.float32)
-        for tap_index in range(TAPS):
-            grad_chars = grad_chars.at[:, tap_index : tap_index + CHARS, :].add(
-                grad_columns[:, :, tap_index, :]
-            )
-        grad_chars = grad_chars[:, :CHARS, :].reshape(block_size * CHARS, CDIM)
-        grad_table = grad_table + jnp.dot(
-            one_hot.astype(jnp.float32).T, grad_chars, precision=lax.Precision.HIGHEST
-        )
-        return ((grad_conv, grad_table), None)
-
-    grad_blocks = grad_pre_pool.reshape(tok_share // block_size, block_size, FILTERS)
-    conv_init = (
-        jnp.zeros((TAPS * CDIM, FILTERS), jnp.float32),
-        jnp.zeros((VOCAB, CDIM), jnp.float32),
-    )
-    conv_sums, unused = lax.scan(conv_back, conv_init, (id_blocks, grad_blocks))
-    grad_conv = conv_sums[0].reshape(TAPS, CDIM, FILTERS) * tap_mask[:, None, :].astype(jnp.float32)
-    grad_table = conv_sums[1]
-    bias_placed = lax.dynamic_update_slice_in_dim(
-        jnp.zeros((2, GATES), jnp.float32), grad_bias, mp_index * gate_local, 1
-    )
-    grad_table, grad_conv, grad_cb, grad_hbs, grad_pb, bias_placed = lax.psum(
-        (grad_table, grad_conv, grad_cb, jnp.stack(grad_hb), grad_pb, bias_placed), ("dp", "mp")
-    )
-    grad_lbias = lax.dynamic_slice_in_dim(bias_placed, mp_index * gate_local, gate_local, 1)
-    grad_cw = lax.dynamic_slice_in_dim(grad_conv, dp_index * dp_width, dp_width, 2)
-    hw_part, pw_part = (
-        lax.psum_scatter(
-            hw_terms.astype(jnp.bfloat16), "dp", scatter_dimension=1, tiled=True
-        ).astype(jnp.float32),
-        lax.psum_scatter(
-            grad_pw.astype(jnp.bfloat16), "dp", scatter_dimension=0, tiled=True
-        ).astype(jnp.float32),
-    )
-    hw_sum, grad_pws = (
-        lax.psum(hw_part.astype(jnp.bfloat16), "mp").astype(jnp.float32),
-        lax.psum(pw_part.astype(jnp.bfloat16), "mp").astype(jnp.float32),
-    )
-    grad_hws = hw_sum.reshape(2, hw_sum.shape[1], 2 * FILTERS)
+    ratio = jnp.pad(grad_pre_pool / exp_total[:tok_share], ((0, tok_pad), (0, 0)))
+    low_mask = tap_mask[:, None, :].astype(jnp.float32)
+    if paired:
+        grad_hws, grad_conv, grad_table = conv_backward_and_sum(
+            ids_time, char_vecs, ratio, conv_shifted, summed
+        )
+        own_mask = lax.dynamic_slice_in_dim(low_mask, dp_index * dp_width, dp_width, 2)
+        grad_cw = grad_conv.reshape(TAPS, CDIM, dp_width) * own_mask
+        small = []
+    else:
+        grad_conv, grad_table = conv_backward(ids_time, char_vecs, ratio, conv_shifted)
+        grad_conv = grad_conv.reshape(TAPS, CDIM, FILTERS) * low_mask
+        small = [grad_table, grad_conv]
+        grad_hws = jnp.stack([summed[1].astype(jnp.float32), summed[0].astype(jnp.float32)])
+    small += [grad_cb, jnp.stack(grad_hb), grad_pb]
+    flat = jnp.concatenate([value.reshape(-1) for value in small])
+    flat = jnp.pad(flat, (0, -flat.size % 1024)).reshape(-1, UNIT_BLOCK)
+    flat = lax.psum(flat, ("dp", "mp")).reshape(-1)
+    pieces = []
+    start = 0
+    for value in small:
+        pieces.append(flat[start : start + value.size].reshape(value.shape))
+        start += value.size
+    grad_cb, grad_hbs, grad_pb = pieces[-3:]
+    if not paired:
+        grad_table = pieces[0]
+        grad_cw = lax.dynamic_slice_in_dim(pieces[1], dp_index * dp_width, dp_width, 2)
+    grad_lbias = lax.psum(grad_bias, "dp")
+    grad_pws = pw_sum.astype(jnp.float32)
     return (
         hidden,
         grad_table,

time: 2300 us -> 1620 us (0.70)
  local copies, waits for them, and re-layouts: 523 us -> 116 us
  waiting for transfers between devices: 728 us -> 331 us
  Pallas kernels: 523 us -> 906 us
  matrix products: 306 us -> 117 us
  other arithmetic: 133 us -> 55.5 us
    pallas_call x0 -> x2, Pallas kernels: none -> 349 us  [the longest x1 324 us: conv_backward_and_sum(): pl.pallas_call(functools.partial(tail_kernel, chunks), grid=(chunks // 2...]
    scatter-add x98 -> x0, local copies, waits for them, and re-layouts: 260 us -> none  [conv_back(): grad_chars.at[:, tap_index:tap_index + CHARS, :]]
    psum x2 -> x1, waiting for transfers between devices: 314 us -> 59.9 us  [shards(): pw_sum = lax.psum(pw_part, 'mp')]
    dot_general x101 -> x3, matrix products: 206 us -> 29.5 us  [weight_part(): jnp.dot(left_all.T, right_all, preferred_element_type=jnp.float32)]
    unnamed x16 -> x7, waiting for transfers between devices: 114 us -> 0.11 us
    concatenate x56 -> x0, local copies, waits for them, and re-layouts: 102 us -> none  [char_columns(): jnp.concatenate([padded[:, tap_index:tap_index + CHARS, :] for tap_index...]
    reduce_scatter x4 -> x0, waiting for transfers between devices: 87.4 us -> none  [the longest x1 44.3 us: shards(): lax.psum_scatter(grad_input, 'dp', scatter_dimension=1, tiled=True)]
    all_gather x1, waiting for transfers between devices: 72.8 us -> 150 us  [shards(): lax.all_gather(high_low, 'dp', axis=1, tiled=True)]
  transfers between devices with their start and end apart: 14 -> 26, of which waited for: 11 -> 10; matrix products, arithmetic and copies ran while one was open for 35% -> 15% of each run, Pallas kernels for 0% -> 36%
where the time goes in v2:
time: 1620 us
  Pallas kernels  906 us (56%)
  waiting for transfers between devices  331 us (20%)
  matrix products  117 us (7%)
  local copies, waits for them, and re-layouts  116 us (7%)
  blocking collectives  66.2 us (4%)
  other arithmetic  55.5 us (3%)
    pallas_call x1, Pallas kernels, conv_backward_and_sum(): pl.pallas_call(functools.partial(tail_kernel, chunks), grid=(chunks // 2...  324 us
    pallas_call x1, Pallas kernels, lstm_backward(): pl.pallas_call(functools.partial(backward_kernel, size), grid=(WIN,), in_...  298 us
    pallas_call x1, Pallas kernels, lstm_forward(): pl.pallas_call(functools.partial(forward_kernel, size), grid=(WIN + 1,),...  260 us
    all_gather x1, waiting for transfers between devices, shards(): lax.all_gather(high_low, 'dp', axis=1, tiled=True)  150 us
    psum x1, waiting for transfers between devices, shards(): pw_sum = lax.psum(pw_part, 'mp')  59.9 us
    all_gather x1, waiting for transfers between devices, shards(): embed_all = lax.all_gather(embed_own, 'mp', axis=0)  56.7 us
    psum x1, blocking collectives, shards(): flat = lax.psum(flat, ('dp', 'mp')).reshape(-1)  46.2 us
    unnamed x168, local copies, waits for them, and re-layouts  37.4 us
  transfers between devices with their start and end apart: 26, of which 10 were waited for; matrix products, arithmetic and copies ran while one was open for 15% of the time, Pallas kernels for 36%

profile of v2, /device:TPU:0, one launch (start us, length us, event | category | flops | bytes accessed | tf_op | source)
XLA Modules:
  0.0 1618.1 jit_solution(7440548716094678162)
XLA Ops:
  7.2 9.0 convert_element_type.401
  24.4 8.3 all_gather.24
  43.5 24.4 %shard_map.265 = (f32[288,2048]{1,0:T(8,128)}, bf16[7,288,128]{2,1,0:T(8,128)(2,1)}) custom-call(s32[288,50]{1,0:T(8,128)} %pad.96.clone.ids_ref, bf16[8,384,128]{2,1,0:T(8,128)(2,1)} %copy-done.51, bf16[8,256,2048]{2,1,0:T(8,128)(2,1)} %bitcast_dynamic-update-slice_fusion.weight_ref), custom_call_target="tpu_custom_call" | custom-call | flops 15099494400 | bytes 12582912 | tf_op jit(solution)/shard_map/pallas_call | solution.py:629
  70.6 150.1 %all-gather.8.cloned.1.call-done = bf16[2,2048,4096]{2,1,0:T(8,128)(2,1)} async-done(((bf16[2,512,4096]{2,1,0:T(8,128)(2,1)}), bf16[2,2048,4096]{2,1,0:T(8,128)(2,1)}) %all-gather.8.cloned.1.call-update) | async-done | bytes 33554448 | tf_op jit(solution)/shard_map/all_gather | solution.py:1305
  220.7 8.6 fusion.5
  231.6 10.0 fusion.4
  283.8 15.9 dynamic-slice_reduce_fusion.3
  303.9 32.4 %all-gather.14.cloned.1.call-done.wst_ref = bf16[2,512,2048]{2,1,0:T(8,128)(2,1)} async-done(((bf16[2,128,2048]{2,1,0:T(8,128)(2,1)}), bf16[2,512,2048]{2,1,0:T(8,128)(2,1)}) %all-gather.14.cloned.1.call-update) | async-done | bytes 4194320 | tf_op jit(solution)/shard_map/all_gather | solution.py:1310
  336.3 56.7 %all-gather.18.cloned.1.call-done = bf16[160,16,512]{2,1,0:T(8,128)(2,1)} async-done(((bf16[20,16,512]{2,1,0:T(8,128)(2,1)}), bf16[160,16,512]{2,1,0:T(8,128)(2,1)}) %all-gather.18.cloned.1.call-update) | async-done | bytes 2621456 | tf_op jit(solution)/shard_map/all_gather | solution.py:1382
  393.7 259.6 %shard_map.266 = (bf16[20,128,512]{2,1,0:T(8,128)(2,1)}, f32[20,128,2048]{2,1,0:T(8,128)}, f32[20,128,2048]{2,1,0:T(8,128)}, f32[20,128,512]{2,1,0:T(8,128)}, f3...) custom-call(bf16[8,20,16,512]{3,2,1,0:T(8,128)(2,1)} %bitcast.257, ...), custom_call_target="tpu_custom_call" | custom-call | tf_op jit(solution)/shard_map/pallas_call | solution.py:293
  655.5 297.9 %shard_map.267 = (bf16[20,128,2048]{2,1,0:T(8,128)(2,1)}, bf16[20,128,2048]{2,1,0:T(8,128)(2,1)}, bf16[20,128,512]{2,1,0:T(8,128)(2,1)}, bf16[20,128,512]{2,1,0:...) custom-call(f32[20,128,2048]{2,1,0:T(8,128)} %get-tuple-element.42.gate0_ref, ...), custom_call_target="tpu_custom_call" | custom-call | tf_op jit(solution)/shard_map/pallas_call | solution.py:525
  964.7 14.5 multiply_convert_fusion.1
  994.2 9.3 bitcast_convert_fusion.1
  1004.6 8.7 bitcast_convert_fusion.3
  1028.6 12.0 fusion.68
  1040.6 46.2 %psum.21 = f32[88,128]{1,0:T(8,128)S(1)} all-reduce(f32[88,128]{1,0:T(8,128)S(1)} %fusion.62), channel_id=1, replica_groups=mesh['dp'=4,'mp'=8] {'dp','mp'}, use_global_device_ids=true, to_apply=%region_6.7 | all-reduce | flops 11264 | bytes 90112 | tf_op jit(solution)/shard_map/psum | solution.py:1483
  1107.3 11.7 psum.23
  1131.8 9.4 collective-permute-done.6
  1154.7 59.9 %all-reduce.26.cloned.1.call-done = bf16[512,512]{1,0:T(8,128)(2,1)} async-done(((bf16[512,512]{1,0:T(8,128)(2,1)}), bf16[512,512]{1,0:T(8,128)(2,1)}) %all-reduce.26.cloned.1.call-update) | async-done | bytes 524304 | tf_op jit(solution)/shard_map/psum | solution.py:1442
  1221.3 10.6 collective-permute-done.8
  1244.3 10.9 convolution_convert_fusion
  1255.2 16.2 %convolution_convert_fusion.1 = bf16[1024,4096]{1,0:T(8,128)(2,1)} fusion(bf16[280,4096]{1,0:T(8,128)(2,1)S(1)} %collective-permute-done.1, bf16[280,2048]{1,0:T(8,128)(2,1)S(1)} %copy-done.8, bf16[280,2048]{1,0:T(8,128)(2,1)S(1)} %get-tuple-element.74, bf16[280,1024]{1,0:T(8,128)(2,1)} %collective-permute-done, bf16[280,1024]{1,0:T(8,128)(2,1)S(1)} %bitcast.280), kind=kOutput, calls=%fused_computation.7 | convolution fusion | flops 4717871104 | bytes 14123008 | tf_op jit(solution)/shard_map/dot_general | solution.py:1262
  1271.4 324.5 %shard_map.268 = (f32[2,16,2,16,4096]{4,3,2,1,0:T(8,128)}, f32[112,512]{1,0:T(8,128)}, f32[264,128]{1,0:T(8,128)}) custom-call(s32[8,1728]{1,0:T(8,128)} %reshape.284.hot_ref, s32[2,288]{1,0:T(2,128)} %slice.135.hot_extra_ref, bf16[7,288,128]{2,1,0:T(8,128)(2,1)} %get-tuple-element.41.vec_ref, bf16[256,1728]{1,0:T(8,128)(2,1)} %pad_maximum_fusion.3.turned_ref, ...), custom_call_target="tpu_custom_call" | custom-call | tf_op jit(solution)/shard_map/pallas_call | solution.py:1167
  1599.2 11.7 copy.202
  (339 shorter events, 183.8 us)
Async XLA Ops:
  7.2 213.5 %all-gather.8.cloned.1.call-start = ((), (), s32[]{:S(2)}) async-start(), calls=%async_computation | async-start | bytes 41943040 | tf_op jit(solution)/shard_map/all_gather | solution.py:1305
  16.3 229.1 %all-gather.10.cloned.1.call-start = ((), (), s32[]{:S(2)}) async-start(), calls=%async_computation.1 | async-start | bytes 2621440 | tf_op jit(solution)/shard_map/all_gather | solution.py:1306
  18.4 285.5 %all-gather.16.cloned.1.call-start = ((), (), s32[]{:S(2)}) async-start(), calls=%async_computation.4 | async-start | bytes 1310720 | tf_op jit(solution)/shard_map/all_gather | solution.py:1311
  20.2 283.7 %all-gather.12.cloned.1.call-start = ((), (), s32[]{:S(2)}) async-start(), calls=%async_computation.2 | async-start | bytes 5242880 | tf_op jit(solution)/shard_map/all_gather | solution.py:1309
  21.4 314.9 %all-gather.14.cloned.1.call-start = ((), (), s32[]{:S(2)}) async-start(), calls=%async_computation.3 | async-start | bytes 5242880 | tf_op jit(solution)/shard_map/all_gather | solution.py:1310
  24.3 368.7 %all-gather.18.cloned.1.call-start = ((), (), s32[]{:S(2)}) async-start(), calls=%async_computation.6 | async-start | bytes 2949120 | tf_op jit(solution)/shard_map/all_gather | solution.py:1382
  248.7 965.8 %all-reduce.26.cloned.1.call-start = ((), (), s32[]{:S(2)}) async-start(), calls=%async_computation.5 | async-start | bytes 1048576 | tf_op jit(solution)/shard_map/psum | solution.py:1442
  282.6 839.1 %collective-permute-start.4 = (bf16[280,1024]{1,0:T(8,128)(2,1)}, bf16[280,1024]{1,0:T(8,128)(2,1)}, u32[]{:S(2)}, u32[]{:S(2)}) collective-permute-start(bf16[280,1024]{1,0:T(8,128)(2,1)} %bitcast.127), channel_id=1, source_target_pairs={{0,8},{8,0},{16,24},{24,16},{1,9},{9,1},{17,25},{25,17},{2,10},{10... | collective-permute-start | bytes 1720328 | tf_op jit(solution)/shard_map/ppermute | solution.py:1226
  300.6 942.6 %collective-permute-start.2 = (bf16[280,1024]{1,0:T(8,128)(2,1)}, bf16[280,1024]{1,0:T(8,128)(2,1)}, u32[]{:S(2)}, u32[]{:S(2)}) collective-permute-start(bf16[280,1024]{1,0:T(8,128)(2,1)} %bitcast.121), channel_id=1, source_target_pairs={{0,8},{8,0},{16,24},{24,16},{1,9},{9,1},{17,25},{25,17},{2,10},{10... | collective-permute-start | bytes 1720328 | tf_op jit(solution)/shard_map/ppermute | solution.py:1226
  302.7 952.5 %collective-permute-start = (bf16[280,1024]{1,0:T(8,128)(2,1)}, bf16[280,1024]{1,0:T(8,128)(2,1)}, u32[]{:S(2)}, u32[]{:S(2)}) collective-permute-start(bf16[280,1024]{1,0:T(8,128)(2,1)} %bitcast.117), channel_id=1, source_target_pairs={{0,8},{8,0},{16,24},{24,16},{1,9},{9,1},{17,25},{25,17},{2,10},{10... | collective-permute-start | bytes 1720328 | tf_op jit(solution)/shard_map/ppermute | solution.py:1226
  991.9 127.1 %collective-permute-start.15 = (bf16[512,2,128]{2,0,1:T(8,128)(2,1)}, bf16[512,2,128]{2,0,1:T(8,128)(2,1)}, u32[]{:S(2)}, u32[]{:S(2)}) collective-permute-start(bf16[512,2,128]{2,0,1:T(8,128)(2,1)} %bitcast.287), channel_id=1, source_target_pairs={{0,8},{8,0},{16,24},{24,16},{1,9},{9,1},{17,25},{25,17},{2,10},{10... | collective-permute-start | bytes 786440 | tf_op jit(solution)/shard_map/ppermute | solution.py:1226
  993.7 126.3 %collective-permute-start.17 = (bf16[512,2,128]{2,0,1:T(8,128)(2,1)}, bf16[512,2,128]{2,0,1:T(8,128)(2,1)}, u32[]{:S(2)}, u32[]{:S(2)}) collective-permute-start(bf16[512,2,128]{2,0,1:T(8,128)(2,1)} %bitcast.286), channel_id=1, source_target_pairs={{0,8},{8,0},{16,24},{24,16},{1,9},{9,1},{17,25},{25,17},{2,10},{10... | collective-permute-start | bytes 786440 | tf_op jit(solution)/shard_map/ppermute | solution.py:1226
  1120.0 22.1 %collective-permute-start.11 = (bf16[2,128,2048]{2,1,0:T(8,128)(2,1)S(1)}, bf16[2,128,2048]{2,1,0:T(8,128)(2,1)}, u32[]{:S(2)}, u32[]{:S(2)}) collective-permute-start(bf16[2,128,2048]{2,1,0:T(8,128)(2,1)S(1)} %copy-done.30), channel_id=1, source_target_pairs={{0,8},{8,0},{16,24},{24,16},{1,9},{9,1},{17,25},{25,17},{2,10},{10... | collective-permute-start | bytes 3145736 | tf_op jit(solution)/shard_map/ppermute | solution.py:1226
  1123.3 7.6 collective-permute-start.18
  1128.1 13.1 collective-permute-start.6
  1130.9 13.8 collective-permute-start.13
  1141.2 7.3 collective-permute-start.7
  1142.2 9.6 collective-permute-start.9
  1144.7 98.5 %collective-permute-start.3 = (bf16[280,4096]{1,0:T(8,128)(2,1)}, bf16[280,4096]{1,0:T(8,128)(2,1)}, u32[]{:S(2)}, u32[]{:S(2)}) collective-permute-start(bf16[280,4096]{1,0:T(8,128)(2,1)} %pad_maximum_fusion.2), channel_id=1, source_target_pairs={{0,8},{8,0},{16,24},{24,16},{1,9},{9,1},{17,25},{25,17},{2,10},{10... | collective-permute-start | bytes 6881288 | tf_op jit(solution)/shard_map/ppermute | solution.py:1226
  1148.5 68.4 %collective-permute-start.12 = (bf16[128,2048]{1,0:T(8,128)(2,1)}, bf16[128,2048]{1,0:T(8,128)(2,1)}, u32[]{:S(2)}, u32[]{:S(2)}) collective-permute-start(bf16[128,2048]{1,0:T(8,128)(2,1)} %dynamic-slice_bitcast_fusion.6), channel_id=1, source_target_pairs={{0,16},{8,24},{16,0},{24,8},{1,17},{9,25},{17,1},{25,9},{2,18},{10... | collective-permute-start | bytes 1572872 | tf_op jit(solution)/shard_map/ppermute | solution.py:1226
  1151.7 67.8 %collective-permute-start.14 = (bf16[128,2048]{1,0:T(8,128)(2,1)}, bf16[128,2048]{1,0:T(8,128)(2,1)}, u32[]{:S(2)}, u32[]{:S(2)}) collective-permute-start(bf16[128,2048]{1,0:T(8,128)(2,1)} %dynamic-slice_bitcast_fusion.5), channel_id=1, source_target_pairs={{0,16},{8,24},{16,0},{24,8},{1,17},{9,25},{17,1},{25,9},{2,18},{10... | collective-permute-start | bytes 1572872 | tf_op jit(solution)/shard_map/ppermute | solution.py:1226
  1216.9 15.1 collective-permute-start.8
  1219.5 20.6 %collective-permute-start.10 = (bf16[128,2048]{1,0:T(8,128)(2,1)}, bf16[128,2048]{1,0:T(8,128)(2,1)S(1)}, u32[]{:S(2)}, u32[]{:S(2)}) collective-permute-start(bf16[128,2048]{1,0:T(8,128)(2,1)} %dynamic-slice_bitcast_fusion.7), channel_id=1, source_target_pairs={{0,16},{8,24},{16,0},{24,8},{1,17},{9,25},{17,1},{25,9},{2,18},{10... | collective-permute-start | bytes 1572872 | tf_op jit(solution)/shard_map/ppermute | solution.py:1226
  1232.0 23.2 %collective-permute-start.1 = (bf16[280,4096]{1,0:T(8,128)(2,1)S(1)}, bf16[280,4096]{1,0:T(8,128)(2,1)S(1)}, u32[]{:S(2)}, u32[]{:S(2)}) collective-permute-start(bf16[280,4096]{1,0:T(8,128)(2,1)S(1)} %copy-done.19), channel_id=1, source_target_pairs={{0,8},{8,0},{16,24},{24,16},{1,9},{9,1},{17,25},{25,17},{2,10},{10... | collective-permute-start | bytes 6881288 | tf_op jit(solution)/shard_map/ppermute | solution.py:1226
  (72 other events, 1397.8 us)
Sparse Core Ops, SparseCore 0:
  16.4 204.2 all-gather.7
  222.8 22.5 all-gather.9
  247.0 16.8 all-gather.15
  265.9 34.4 all-gather.11
  301.8 34.4 all-gather.13
  338.3 54.6 all-gather.17
  1142.3 72.2 all-reduce.25

commit v3 on v2

--- a/solution.py
+++ b/solution.py
@@ -29,24 +29,6 @@
     for exponent in range(6):
         widths = widths + (index_row >= unit_size * (1 << exponent)).astype(jnp.int32)
     return widths
-
-
-def split_gates(pre_act, unit_count):
-    leading = pre_act.shape[:-1]
-    shaped = pre_act.reshape(leading + (unit_count // UNIT_BLOCK, 4, UNIT_BLOCK))
-    return [shaped[..., gate_index, :].reshape(leading + (unit_count,)) for gate_index in range(4)]
-
-
-def join_gates(gate_parts, unit_count):
-    leading = gate_parts[0].shape[:-1]
-    stacked = jnp.stack(
-        [
-            part_value.reshape(leading + (unit_count // UNIT_BLOCK, UNIT_BLOCK))
-            for part_value in gate_parts
-        ],
-        axis=-2,
-    )
-    return stacked.reshape(leading + (4 * unit_count,))
 
 
 def silu_slope(value):
@@ -577,33 +559,32 @@
     return jnp.concatenate([low, high], axis=1)
 
 
-def conv_forward_kernel(ids_ref, table_ref, weight_ref, total_ref, vec_ref):
-    block = pl.program_id(0)
+def char_vectors(ids_ref, table_ref, vec_ref):
     groups, tokens, _ = vec_ref.shape
+    vocab = table_ref.shape[1]
+    for group in range(groups):
+        acc = jnp.zeros((tokens, GROUP), jnp.float32)
+        for shift in range(SHIFTS):
+            place = group * SHIFTS + shift
+            if place < CHARS:
+                column = ids_ref[:, place : place + 1]
+                hot = column == lax.broadcasted_iota(jnp.int32, (tokens, vocab), 1)
+                acc = acc + jnp.dot(
+                    jnp.where(hot, 1.0, 0.0).astype(jnp.bfloat16),
+                    table_ref[shift],
+                    preferred_element_type=jnp.float32,
+                )
+        vec_ref[group] = acc.astype(jnp.bfloat16)
+
+
+def conv_block(block, cols, vec_ref, weight_ref, total_ref):
+    _, tokens, _ = vec_ref.shape
     full, extra = group_counts()
-
-    @pl.when(block == 0)
-    def _():
-        vocab = table_ref.shape[1]
-        for group in range(groups):
-            acc = jnp.zeros((tokens, GROUP), jnp.float32)
-            for shift in range(SHIFTS):
-                place = group * SHIFTS + shift
-                if place < CHARS:
-                    column = ids_ref[:, place : place + 1]
-                    hot = column == lax.broadcasted_iota(jnp.int32, (tokens, vocab), 1)
-                    acc = acc + jnp.dot(
-                        jnp.where(hot, 1.0, 0.0).astype(jnp.bfloat16),
-                        table_ref[shift],
-                        preferred_element_type=jnp.float32,
-                    )
-            vec_ref[group] = acc.astype(jnp.bfloat16)
-
     bound = position_bound(block * FBLOCK, FBLOCK, TAPS)
     left = windows(vec_ref, full)
     total = jnp.zeros((tokens, FBLOCK), jnp.float32)
     for shift in range(SHIFTS):
-        out = jnp.dot(left, weight_ref[shift], preferred_element_type=jnp.float32)
+        out = jnp.dot(left, weight_ref[shift, :, cols], preferred_element_type=jnp.float32)
         values = jnp.exp(out).reshape(full, tokens, FBLOCK)
         for group in range(full):
             place = group * SHIFTS + shift
@@ -611,15 +592,27 @@
             if place > CHARS - TAPS:
                 term = jnp.where(bound >= place, term, 0.0)
             total = total + term
-    total_ref[...] = total
+    total_ref[:, cols] = total
 
     @pl.when(block == 0)
     def _():
         for shift in range(extra):
             out = jnp.dot(
-                vec_ref[full], weight_ref[shift, :GROUP], preferred_element_type=jnp.float32
+                vec_ref[full], weight_ref[shift, :GROUP, cols], preferred_element_type=jnp.float32
             )
-            total_ref[...] += jnp.where(bound >= full * SHIFTS + shift, jnp.exp(out), 0.0)
+            total_ref[:, cols] += jnp.where(
+                bound >= full * SHIFTS + shift, jnp.exp(out), 0.0
+            )
+
+
+def conv_forward_kernel(ids_ref, table_ref, weight_ref, total_ref, vec_ref):
+    block = pl.program_id(0)
+
+    @pl.when(block == 0)
+    def _():
+        char_vectors(ids_ref, table_ref, vec_ref)
+
+    conv_block(block, slice(None), vec_ref, weight_ref, total_ref)
 
 
 def conv_forward(ids, table_shift, weights):
@@ -823,6 +816,10 @@
 
 MESH = pl.DeviceIdType.MESH
 CHUNK_ROWS = 16
+SLACK = 2
+BEATS = 2
+AHEAD = 2
+BIAS_ROWS = 32
 
 
 def tail_kernel(
@@ -836,6 +833,8 @@
     weight_ref,
     part1_ref,
     part0_ref,
+    part2_ref,
+    small_ref,
     sum_ref,
     conv_ref,
     table_ref,
@@ -876,9 +875,11 @@
     mp = lax.axis_index("mp")
     core, high = lax.rem(dp, 2), dp // 2
     near, ring = lax.rem(mp, 2), mp // 2
-    per_layer = chunks // 2
+    per_layer = part1_ref.shape[1]
     width = FILTERS * 2
     quarter = width // 4
+    parts = (part1_ref, part0_ref, part2_ref)
+    vocab = table_ref.shape[0] - small_ref.shape[0]
     core_peer = {"dp": dp + 1 - 2 * core, "mp": mp}
     high_peer = {"dp": dp + 2 - 4 * high, "mp": mp}
     near_peer = {"dp": dp, "mp": mp + 1 - 2 * near}
@@ -899,9 +900,16 @@
             part.at[1 - high, row], got_y_ref.at[chunk], y_send.at[chunk], y_recv.at[chunk], high_peer
         )
 
+    def y_start(chunk):
+        for layer, part in enumerate(parts):
+
+            @pl.when(chunk // per_layer == layer)
+            def _():
+                y_copy(part, chunk, chunk - layer * per_layer).start()
+
     def load(chunk, act):
         slot = lax.rem(chunk, 2)
-        for layer, part in enumerate((part1_ref, part0_ref)):
+        for layer, part in enumerate(parts):
 
             @pl.when(chunk // per_layer == layer)
             def _():
@@ -948,12 +956,7 @@
 
     def store(chunk):
         slot = lax.rem(chunk, 2)
-        layer = 1 - chunk // per_layer
-        return pltpu.make_async_copy(
-            wide_ref.at[slot],
-            sum_ref.at[layer, lax.rem(chunk, per_layer)],
-            store_sem.at[slot],
-        )
+        return pltpu.make_async_copy(wide_ref.at[slot], sum_ref.at[chunk], store_sem.at[slot])
 
     def when_chunk(chunk, body):
         @pl.when(jnp.logical_and(chunk >= 0, chunk < chunks))
@@ -970,6 +973,10 @@
             ).astype(jnp.bfloat16)
         x_copy(chunk).start()
 
+        @pl.when(chunk + AHEAD < chunks)
+        def _():
+            y_start(chunk + AHEAD)
+
         @pl.when(chunk + 2 < chunks)
         def _():
             load(chunk + 2, "start")
@@ -1005,8 +1012,8 @@
             store(chunk - 2).wait()
 
         slot = lax.rem(chunk, 2)
-        wide_ref[slot, near] = all_z_ref[chunk].astype(jnp.float32)
-        wide_ref[slot, 1 - near] = all_x_ref[chunk].astype(jnp.float32)
+        wide_ref[slot, near] = all_z_ref[chunk]
+        wide_ref[slot, 1 - near] = all_x_ref[chunk]
         store(chunk).start()
 
     def small_copies(stage):
@@ -1040,10 +1047,11 @@
                     peer,
                 )
             ]
+        count = table_ref.shape[0] - (BIAS_ROWS if stage > 1 else 0)
         copies.append(
             remote(
-                table_acc_ref.at[stage],
-                table_got_ref.at[stage],
+                table_acc_ref.at[stage, pl.ds(0, count)],
+                table_got_ref.at[stage, pl.ds(0, count)],
                 small_send.at[stage, 2],
                 small_recv.at[stage, 2],
                 peer,
@@ -1058,11 +1066,14 @@
     def small_finish(stage):
         for copy in small_copies(stage):
             copy.wait()
-        total = table_acc_ref[stage] + table_got_ref[stage]
+        count = table_ref.shape[0] - (BIAS_ROWS if stage > 1 else 0)
+        total = table_acc_ref[stage, :count] + table_got_ref[stage, :count]
+        if stage == 1:
+            table_ref[count - BIAS_ROWS :] = total[count - BIAS_ROWS :]
         if stage < 4:
-            table_acc_ref[stage + 1] = total
+            table_acc_ref[stage + 1, :count] = total
         else:
-            table_ref[...] = total
+            table_ref[:count] = total
         if stage == 0:
             for y in range(2):
                 conv_two_ref[0, y] = conv_two_ref[0, y] + conv_in_ref[y]
@@ -1082,13 +1093,8 @@
             pl.semaphore_signal(barrier, inc=1, device_id=peer, device_id_type=MESH)
         pl.semaphore_wait(barrier, 6)
 
-        @pl.loop(0, per_layer)
-        def _(row):
-            y_copy(part1_ref, row, row).start()
-
-        @pl.loop(0, per_layer)
-        def _(row):
-            y_copy(part0_ref, per_layer + row, row).start()
+        for chunk in range(AHEAD):
+            y_start(jnp.int32(chunk))
 
         load(jnp.int32(0), "start")
         load(jnp.int32(1), "start")
@@ -1110,7 +1116,8 @@
 
     @pl.when(tick == SHIFTS - 1)
     def _():
-        table_acc_ref[0] = table_gradient(hot_ref, hot_extra_ref, char_ref, table_ref.shape[0])
+        table_acc_ref[0, :vocab] = table_gradient(hot_ref, hot_extra_ref, char_ref, vocab)
+        table_acc_ref[0, vocab:] = small_ref[...]
         span = FILTERS // 4
         for y in range(2):
             mine = pl.ds(pl.multiple_of((2 * y + core) * span, span), span)
@@ -1127,15 +1134,15 @@
             if stage < 4:
                 small_start(stage + 1)
 
-    for beat in range(2):
-        at = tick * 2 + beat
+    for beat in range(BEATS):
+        at = tick * BEATS + beat
         when_chunk(at, do_y)
-        when_chunk(at - 1, do_x)
-        when_chunk(at - 2, do_z)
-        when_chunk(at - 3, do_g)
-        when_chunk(at - 4, do_h)
-
-    @pl.when(tick == chunks // 2 + 1)
+        when_chunk(at - SLACK, do_x)
+        when_chunk(at - 2 * SLACK, do_z)
+        when_chunk(at - 3 * SLACK, do_g)
+        when_chunk(at - 4 * SLACK, do_h)
+
+    @pl.when(tick == pl.num_programs(0) - 1)
     def _():
         for chunk in (chunks - 2, chunks - 1):
             store(jnp.int32(chunk)).wait()
@@ -1150,15 +1157,14 @@
             h_copy(chunk).wait_send()
 
 
-def conv_backward_and_sum(ids, vectors, ratio, weights, parts):
+def conv_backward_and_sum(ids, vectors, ratio, weights, parts, small):
     groups, tokens, _ = vectors.shape
     full, _ = group_counts()
     vocab = -(-VOCAB // 8) * 8
     width = parts[0].shape[1]
-    rows = parts[0].shape[0] // 2
-    per_layer = rows // (2 * CHUNK_ROWS)
-    chunks = 2 * per_layer
-    parts = [part.reshape(2, per_layer, 2, CHUNK_ROWS, width) for part in parts]
+    parts = [part.reshape(2, -1, 2, CHUNK_ROWS, width) for part in parts]
+    chunks = sum(part.shape[1] for part in parts)
+    table_rows = vocab + small.shape[0]
     conv_rows = TAPS * CDIM
     span = FILTERS // 4
     bf16, f32 = jnp.bfloat16, jnp.float32
@@ -1166,19 +1172,20 @@
     last = SHIFTS - 1
     sums, grad, table = pl.pallas_call(
         functools.partial(tail_kernel, chunks),
-        grid=(chunks // 2 + 2,),
+        grid=(-(-(chunks + 4 * SLACK) // BEATS),),
         in_specs=[pl.BlockSpec(memory_space=pltpu.VMEM)] * 6
         + [pl.BlockSpec((1, 2 * GROUP, FILTERS), lambda t: (jnp.minimum(t, last), 0, 0))]
-        + [pl.BlockSpec(memory_space=pl.ANY)] * 2,
+        + [pl.BlockSpec(memory_space=pl.ANY)] * 3
+        + [pl.BlockSpec(memory_space=pltpu.VMEM)],
         out_specs=[
             pl.BlockSpec(memory_space=pl.ANY),
             pl.BlockSpec(memory_space=pltpu.VMEM),
             pl.BlockSpec(memory_space=pltpu.VMEM),
         ],
         out_shape=[
-            jax.ShapeDtypeStruct((2, per_layer, 2, CHUNK_ROWS, width), f32),
+            jax.ShapeDtypeStruct((chunks, 2, CHUNK_ROWS, width), bf16),
             jax.ShapeDtypeStruct((conv_rows, span), f32),
-            jax.ShapeDtypeStruct((vocab, GROUP), f32),
+            jax.ShapeDtypeStruct((table_rows, GROUP), f32),
         ],
         scratch_shapes=[
             pltpu.VMEM((conv_rows, FILTERS), f32),
@@ -1191,13 +1198,13 @@
             pltpu.VMEM((chunks, 3, CHUNK_ROWS, width // 4), bf16),
             pltpu.VMEM((chunks, CHUNK_ROWS, width), bf16),
             pltpu.VMEM((chunks, CHUNK_ROWS, width), bf16),
-            pltpu.VMEM((2, 2, CHUNK_ROWS, width), f32),
+            pltpu.VMEM((2, 2, CHUNK_ROWS, width), bf16),
             pltpu.VMEM((3, conv_rows, span), f32),
             pltpu.VMEM((4, conv_rows, span), f32),
             pltpu.VMEM((2, 2, conv_rows, span), f32),
             pltpu.VMEM((2, conv_rows, span), f32),
-            pltpu.VMEM((5, vocab, GROUP), f32),
-            pltpu.VMEM((5, vocab, GROUP), f32),
+            pltpu.VMEM((5, table_rows, GROUP), f32),
+            pltpu.VMEM((5, table_rows, GROUP), f32),
             dma((2,)),
             dma((2,)),
             dma((chunks,)),
@@ -1216,9 +1223,309 @@
         compiler_params=pltpu.CompilerParams(
             collective_id=3, has_side_effects=True, vmem_limit_bytes=62 * 2**20
         ),
-    )(*conv_operands(ids, vectors), ratio, weights, *parts)
-    table = table.reshape(vocab, SHIFTS, CDIM).sum(axis=1)[:VOCAB]
-    return sums.reshape(2, rows, width), grad, table
+    )(*conv_operands(ids, vectors), ratio, weights, *parts, small)
+    rest = table[vocab:]
+    table = table[:vocab].reshape(vocab, SHIFTS, CDIM).sum(axis=1)[:VOCAB]
+    found = []
+    start = 0
+    for part in parts:
+        found.append(sums[start : start + part.shape[1]].reshape(-1, width))
+        start += part.shape[1]
+    return found, grad, table, rest
+
+
+GROUPS = tuple(("high", layer, part) for layer in range(2) for part in range(2)) + (("proj", 0, 0),)
+LOCAL = tuple((item, side) for item in range(3) for side in range(2))
+START_STEPS = len(LOCAL) + 4
+
+
+def start_kernel(
+    ids_ref,
+    table_ref,
+    conv_ref,
+    high_ref,
+    proj_ref,
+    win_ref,
+    wst_ref,
+    wpr_ref,
+    total_ref,
+    vec_ref,
+    weight_ref,
+    high_all,
+    proj_all,
+    win_all,
+    wst_all,
+    wpr_all,
+    conv_got,
+    conv_send,
+    conv_recv,
+    own_sem,
+    core_send,
+    core_recv,
+    y_send,
+    y_recv,
+    x_send,
+    x_recv,
+    z_send,
+    z_recv,
+    c_send,
+    c_recv,
+    ly_send,
+    ly_recv,
+    lc_send,
+    lc_recv,
+):
+    step = pl.program_id(0)
+    dp = lax.axis_index("dp")
+    mp = lax.axis_index("mp")
+    core, high = lax.rem(dp, 2), dp // 2
+    near, ring = lax.rem(mp, 2), lax.rem(mp // 2, 2)
+    across = dp + 2 - 4 * high
+    core_peer = {"dp": dp + 1 - 2 * core, "mp": mp}
+    high_peer = {"dp": across, "mp": mp}
+    both_peer = {"dp": across + 1 - 2 * core, "mp": mp}
+    near_peer = {"dp": dp, "mp": mp + 1 - 2 * near}
+    ring_peer = {"dp": dp, "mp": mp + 2 - 4 * ring}
+    lanes = wpr_ref.shape[2]
+    mine = 2 * ring + near
+    beside = 2 * ring + 1 - near
+    beyond = 2 * (1 - ring)
+
+    def from_shard(index, place):
+        kind, layer, part = GROUPS[index]
+        if kind == "high":
+            return high_ref.at[layer, 4 * part + place]
+        return proj_ref.at[place]
+
+    def in_full(index, place, quarter):
+        kind, layer, part = GROUPS[index]
+        if kind == "high":
+            return high_all.at[layer, quarter, 4 * part + place]
+        return proj_all.at[quarter, place]
+
+    def local_full(item, side, quarter):
+        if item == 2:
+            cols = pl.ds(pl.multiple_of(quarter * lanes, lanes), lanes)
+            return wpr_all.at[side, :, cols]
+        return (win_all, wst_all)[item].at[side, quarter]
+
+    def own_pair(index):
+        if index < 2:
+            return high_ref.at[index], high_all.at[index, dp]
+        if index == 2:
+            return proj_ref, proj_all.at[dp]
+        item, side = LOCAL[index - 3]
+        return (win_ref, wst_ref, wpr_ref)[item].at[side], local_full(item, side, dp)
+
+    owned = 3 + len(LOCAL)
+
+    def remote(src, dst, send, recv, peer):
+        return pltpu.make_async_remote_copy(
+            src_ref=src, dst_ref=dst, send_sem=send, recv_sem=recv, device_id=peer, device_id_type=MESH
+        )
+
+    def own_copy(index):
+        src, dst = own_pair(index)
+        return pltpu.make_async_copy(src, dst, own_sem.at[index])
+
+    def core_copy(index):
+        src, dst = own_pair(index)
+        return remote(src, dst, core_send.at[index], core_recv.at[index], core_peer)
+
+    def y_copy(index):
+        return remote(
+            from_shard(index, mine),
+            in_full(index, mine, dp),
+            y_send.at[index],
+            y_recv.at[index],
+            high_peer,
+        )
+
+    def x_copy(index):
+        place = in_full(index, mine, across)
+        return remote(place, place, x_send.at[index], x_recv.at[index], near_peer)
+
+    def z_copy(index, which):
+        place = in_full(index, 2 * ring + which, across)
+        return remote(
+            place, place, z_send.at[index, which], z_recv.at[index, which], ring_peer
+        )
+
+    def c_copy(index, place):
+        ref = in_full(index, place, across)
+        return remote(ref, ref, c_send.at[index, place], c_recv.at[index, place], core_peer)
+
+    def ly_copy(index):
+        item, side = LOCAL[index]
+        return remote(
+            (win_ref, wst_ref, wpr_ref)[item].at[side],
+            local_full(item, side, dp),
+            ly_send.at[index],
+            ly_recv.at[index],
+            high_peer,
+        )
+
+    def lc_copy(index):
+        item, side = LOCAL[index]
+        ref = local_full(item, side, across)
+        return remote(ref, ref, lc_send.at[index], lc_recv.at[index], core_peer)
+
+    conv_peers = (core_peer, high_peer, both_peer)
+
+    def conv_copy(index):
+        return remote(
+            conv_ref, conv_got.at[dp], conv_send.at[index], conv_recv.at[index], conv_peers[index]
+        )
+
+    @pl.when(step == 0)
+    def _():
+        barrier = pltpu.get_barrier_semaphore()
+        for peer in (core_peer, high_peer, both_peer, near_peer, ring_peer):
+            pl.semaphore_signal(barrier, inc=1, device_id=peer, device_id_type=MESH)
+        pl.semaphore_wait(barrier, 5)
+        for index in range(3):
+            conv_copy(index).start()
+        y_copy(0).start()
+        y_copy(1).start()
+        ly_copy(0).start()
+        for index in range(2):
+            core_copy(index).start()
+            own_copy(index).start()
+        char_vectors(ids_ref, table_ref, vec_ref)
+        weight_ref[...] = jnp.zeros(weight_ref.shape, jnp.bfloat16)
+        conv_got[dp] = conv_ref[...]
+        for index in range(3):
+            conv_copy(index).wait()
+        span = conv_ref.shape[1]
+        tap = lax.broadcasted_iota(jnp.int32, (TAPS * CDIM, span), 0) // CDIM
+        for quarter in range(4):
+            bound = position_bound(quarter * span, span, TAPS)
+            part = conv_got[quarter]
+            part = part * jnp.where(tap < CHARS - bound, 1.0, 0.0).astype(jnp.bfloat16)
+            for shift in range(SHIFTS):
+                weight_ref[
+                    shift,
+                    CDIM * shift : CDIM * (shift + TAPS),
+                    quarter * span : (quarter + 1) * span,
+                ] = part
+
+    for index in range(len(GROUPS)):
+
+        @pl.when(step == index + 1)
+        def _():
+            y_copy(index).wait_recv()
+            if index + 2 < len(GROUPS):
+                y_copy(index + 2).start()
+            x_copy(index).start()
+            z_copy(index, near).start()
+            c_copy(index, mine).start()
+
+        @pl.when(step == index + 2)
+        def _():
+            x_copy(index).wait_recv()
+            z_copy(index, 1 - near).start()
+            c_copy(index, beside).start()
+
+        @pl.when(step == index + 3)
+        def _():
+            for which in range(2):
+                z_copy(index, which).wait_recv()
+                c_copy(index, beyond + which).start()
+
+    for index in range(len(LOCAL)):
+        if index:
+
+            @pl.when(step == index)
+            def _():
+                ly_copy(index).start()
+
+        @pl.when(step == index + 1)
+        def _():
+            core_copy(index + 3).start()
+            own_copy(index + 3).start()
+
+        @pl.when(step == index + 3)
+        def _():
+            ly_copy(index).wait_recv()
+            lc_copy(index).start()
+
+    @pl.when(step == 1)
+    def _():
+        core_copy(2).start()
+        own_copy(2).start()
+
+    @pl.when(jnp.logical_and(step >= 1, step <= FILTERS // (2 * FBLOCK)))
+    def _():
+        for half in range(2):
+            block = 2 * (step - 1) + half
+            cols = pl.ds(pl.multiple_of(block * FBLOCK, FBLOCK), FBLOCK)
+            conv_block(block, cols, vec_ref, weight_ref, total_ref)
+
+    @pl.when(step == START_STEPS - 1)
+    def _():
+        for index in range(owned):
+            own_copy(index).wait()
+            core_copy(index).wait()
+        for index in range(len(GROUPS)):
+            y_copy(index).wait_send()
+            x_copy(index).wait_send()
+            for which in range(2):
+                z_copy(index, which).wait_send()
+            for place in range(4):
+                c_copy(index, place).wait()
+        for index in range(len(LOCAL)):
+            ly_copy(index).wait_send()
+            lc_copy(index).wait()
+
+
+def start_gather(ids, table_shift, conv, highway, proj, win, wst, wpr):
+    tokens = ids.shape[0]
+    groups = -(-CHARS // SHIFTS)
+    bf16 = jnp.bfloat16
+    depth, wide = highway.shape[1:]
+    rows = proj.shape[0]
+    highway = highway.reshape(2, 8, depth // 8, wide)
+    proj = proj.reshape(4, rows // 4, PROJ)
+    vmem = pl.BlockSpec(memory_space=pltpu.VMEM)
+    hbm = pl.BlockSpec(memory_space=pl.ANY)
+    dma = pltpu.SemaphoreType.DMA
+    count, local = len(GROUPS), len(LOCAL)
+    total, vec, weight, high, proj, win, wst, wpr = pl.pallas_call(
+        start_kernel,
+        grid=(START_STEPS,),
+        in_specs=[vmem] * 8,
+        out_specs=[vmem] * 3 + [hbm] * 5,
+        out_shape=[
+            jax.ShapeDtypeStruct((tokens, FILTERS), jnp.float32),
+            jax.ShapeDtypeStruct((groups, tokens, GROUP), bf16),
+            jax.ShapeDtypeStruct((SHIFTS, 2 * GROUP, FILTERS), bf16),
+            jax.ShapeDtypeStruct((2, 4) + highway.shape[1:], bf16),
+            jax.ShapeDtypeStruct((4,) + proj.shape, bf16),
+            jax.ShapeDtypeStruct((2, 4) + win.shape[1:], bf16),
+            jax.ShapeDtypeStruct((2, 4) + wst.shape[1:], bf16),
+            jax.ShapeDtypeStruct(wpr.shape[:2] + (4 * wpr.shape[2],), bf16),
+        ],
+        scratch_shapes=[pltpu.VMEM((4,) + conv.shape, bf16)]
+        + [dma((3,))] * 2
+        + [dma((3 + local,))] * 3
+        + [dma((count,))] * 4
+        + [dma((count, 2))] * 2
+        + [dma((count, 4))] * 2
+        + [dma((local,))] * 4,
+        compiler_params=pltpu.CompilerParams(
+            collective_id=4, has_side_effects=True, vmem_limit_bytes=40 * 2**20
+        ),
+    )(ids, table_shift, conv, highway, proj, win, wst, wpr)
+    return (
+        total,
+        vec,
+        weight,
+        high.reshape(2, 4 * depth, wide),
+        proj.reshape(4 * rows, PROJ),
+        win.reshape(2, PROJ, -1),
+        wst.reshape(2, PROJ, -1),
+        wpr,
+    )
 
 
 def swap(value, axis, bit):
@@ -1226,48 +1533,44 @@
     return lax.ppermute(value, axis, [(index, index ^ bit) for index in range(size)])
 
 
-def halves(value, index, dim):
-    half = value.shape[dim] // 2
-    own = lax.dynamic_slice_in_dim(value, index * half, half, dim)
-    other = lax.dynamic_slice_in_dim(value, (1 - index) * half, half, dim)
-    return own, other
-
-
-def scatter_sum(value, axis, dim, paired):
-    if not paired:
-        return lax.psum_scatter(value, axis, scatter_dimension=dim, tiled=True)
+def scatter_start(value, axis, dim):
     index = lax.axis_index(axis)
-    shape = value.shape
-    quarter = shape[dim] // 4
-    parts = value.reshape(shape[:dim] + (2, 2, quarter) + shape[dim + 1 :])
+    quarter = value.shape[dim] // 4
     low, high = index % 2, index // 2
-    own = lax.dynamic_index_in_dim(parts, low, dim + 1, False)
-    other = lax.dynamic_index_in_dim(parts, 1 - low, dim + 1, False)
-    got = swap(other, axis, 1)
-    both = (own.astype(jnp.float32) + got.astype(jnp.float32)).astype(value.dtype)
-    own = lax.dynamic_index_in_dim(both, high, dim, False)
-    other = lax.dynamic_index_in_dim(both, 1 - high, dim, False)
-    got = swap(other, axis, 2)
-    return (own.astype(jnp.float32) + got.astype(jnp.float32)).astype(value.dtype)
+
+    def pick(side, part):
+        return lax.dynamic_slice_in_dim(value, (2 * side + part) * quarter, quarter, dim)
+
+    def both(side):
+        got = swap(pick(side, 1 - low), axis, 1)
+        return (pick(side, low).astype(jnp.float32) + got.astype(jnp.float32)).astype(value.dtype)
+
+    return both(high), swap(both(1 - high), axis, 2)
 
 
 def weight_part(left, right):
     tokens, depth = left.shape
     core = lax.axis_index("dp") % 2
-    parts = left.reshape(tokens, 2, 2, depth // 4)
-    own = lax.dynamic_index_in_dim(parts, core, 2, False).reshape(tokens, depth // 2)
-    other = lax.dynamic_index_in_dim(parts, 1 - core, 2, False).reshape(tokens, depth // 2)
+    quarter = depth // 4
+
+    def columns(which):
+        return jnp.concatenate(
+            [
+                lax.dynamic_slice_in_dim(left, (2 * half + which) * quarter, quarter, 1)
+                for half in range(2)
+            ],
+            axis=1,
+        )
+
+    own, other = columns(core), columns(1 - core)
     left_all = jnp.concatenate([own, swap(other, "dp", 1)], axis=0)
     right_all = jnp.concatenate([right, swap(right, "dp", 1)], axis=0)
     return jnp.dot(left_all.T, right_all, preferred_element_type=jnp.float32).astype(jnp.bfloat16)
 
 
-def weight_grad(left, right, paired):
-    if not paired:
-        part = jnp.dot(left.T, right, preferred_element_type=jnp.float32).astype(jnp.bfloat16)
-        return lax.psum_scatter(part, "dp", scatter_dimension=0, tiled=True)
-    own, other = halves(weight_part(left, right), lax.axis_index("dp") // 2, 0)
-    return (own.astype(jnp.float32) + swap(other, "dp", 2).astype(jnp.float32)).astype(jnp.bfloat16)
+def weight_grad(left, right):
+    part = jnp.dot(left.T, right, preferred_element_type=jnp.float32).astype(jnp.bfloat16)
+    return lax.psum_scatter(part, "dp", scatter_dimension=0, tiled=True)
 
 
 def shards(
@@ -1299,28 +1602,19 @@
     paired = lax.axis_size("dp") == 4 and mp_size == 8
     dp_index = lax.axis_index("dp")
     dp_width = conv_weight.shape[2]
-    high_low = highway_weight.astype(jnp.bfloat16)
-    conv_full, high_full, proj_full = (
-        lax.all_gather(conv_weight.astype(jnp.bfloat16), "dp", axis=2, tiled=True),
-        lax.all_gather(high_low, "dp", axis=1, tiled=True),
-        lax.all_gather(proj_weight.astype(jnp.bfloat16), "dp", axis=0, tiled=True),
-    )
-    input_full, state_full, lproj_full = (
-        lax.all_gather(lstm_input_weight.astype(jnp.bfloat16), "dp", axis=1, tiled=True),
-        lax.all_gather(lstm_state_weight.astype(jnp.bfloat16), "dp", axis=1, tiled=True),
-        lax.all_gather(lstm_proj.astype(jnp.bfloat16), "dp", axis=2, tiled=True),
-    )
     widths = filter_widths(FILTERS)
     tap_mask = jnp.arange(TAPS)[:, None] < widths[None, :]
-    conv_matrix = (conv_full * tap_mask[:, None, :].astype(jnp.bfloat16)).reshape(
-        TAPS * CDIM, FILTERS
-    )
-    conv_shifted = jnp.stack(
-        [
-            jnp.pad(conv_matrix, ((CDIM * shift, 2 * GROUP - CDIM * (shift + TAPS)), (0, 0)))
-            for shift in range(SHIFTS)
-        ]
-    )
+    lows = [
+        value.astype(jnp.bfloat16)
+        for value in (
+            conv_weight,
+            highway_weight,
+            proj_weight,
+            lstm_input_weight,
+            lstm_state_weight,
+            lstm_proj,
+        )
+    ]
     counts = (CHARS + 1 - widths).astype(jnp.float32)
     table_low = char_table.astype(jnp.bfloat16)
     table_shifted = jnp.stack(
@@ -1336,7 +1630,33 @@
     ids_time = char_ids.reshape(rows_own, WIN, CHARS).transpose(1, 0, 2).reshape(tok_share, CHARS)
     tok_pad = -tok_share % 16
     ids_time = jnp.pad(ids_time, ((0, tok_pad), (0, 0)))
-    exp_total, char_vecs = conv_forward(ids_time, table_shifted, conv_shifted)
+    if paired:
+        lows[0] = lows[0].reshape(TAPS * CDIM, dp_width)
+        (
+            exp_total,
+            char_vecs,
+            conv_shifted,
+            high_full,
+            proj_full,
+            input_full,
+            state_full,
+            lproj_full,
+        ) = start_gather(ids_time, table_shifted, *lows)
+    else:
+        conv_full, high_full, proj_full, input_full, state_full, lproj_full = (
+            lax.all_gather(value, "dp", axis=dim, tiled=True)
+            for value, dim in zip(lows, (2, 1, 0, 1, 1, 2))
+        )
+        conv_matrix = (conv_full * tap_mask[:, None, :].astype(jnp.bfloat16)).reshape(
+            TAPS * CDIM, FILTERS
+        )
+        conv_shifted = jnp.stack(
+            [
+                jnp.pad(conv_matrix, ((CDIM * shift, 2 * GROUP - CDIM * (shift + TAPS)), (0, 0)))
+                for shift in range(SHIFTS)
+            ]
+        )
+        exp_total, char_vecs = conv_forward(ids_time, table_shifted, conv_shifted)
     pooled = jnp.log(exp_total[:tok_share] / counts)
     pre_pool = pooled + conv_bias
     layer_value = jax.nn.silu(pre_pool)
@@ -1426,20 +1746,9 @@
             preferred_element_type=jnp.float32,
         ).astype(jnp.bfloat16)
 
-    grad_input, grad_state, grad_lproj = (
-        jnp.stack(
-            [
-                scatter_sum(outer(left[way], right[way]), "dp", dim, paired).astype(jnp.float32)
-                for way in range(2)
-            ]
-        )
-        for left, right, dim in (((embed_time,) * 2, das, 0), (hprevs, das, 0), (lows, dss, 1))
-    )
     grad_pb = jnp.sum(grad_embed_local.astype(jnp.float32), axis=0)
     summed = []
     grad_hb = [None, None]
-    pw_part = weight_grad(top_low, grad_embed_local, paired)
-    pw_sum = lax.psum(pw_part, "mp")
     grad_layer = jnp.dot(grad_embed_local, proj_full.T, preferred_element_type=jnp.float32)
     for layer_index in (1, 0):
         layer_in = kept_inputs[layer_index]
@@ -1455,7 +1764,7 @@
         if paired:
             summed.append(weight_part(layer_low, grad_mixed))
         else:
-            summed.append(lax.psum(weight_grad(layer_low, grad_mixed, paired), "mp"))
+            summed.append(lax.psum(weight_grad(layer_low, grad_mixed), "mp"))
         grad_hb[layer_index] = jnp.sum(grad_mixed.astype(jnp.float32), axis=0)
         grad_layer = grad_layer * gate_value + jnp.dot(
             grad_mixed, high_full[layer_index].T, preferred_element_type=jnp.float32
@@ -1465,33 +1774,62 @@
 
     ratio = jnp.pad(grad_pre_pool / exp_total[:tok_share], ((0, tok_pad), (0, 0)))
     low_mask = tap_mask[:, None, :].astype(jnp.float32)
+    das, dss, _ = lax.optimization_barrier((das, dss, ratio))
+    lstm_parts = [
+        (outer(left[way], right[way]), dim)
+        for left, right, dim in (((embed_time,) * 2, das, 0), (hprevs, das, 0), (lows, dss, 1))
+        for way in range(2)
+    ]
+    shared = [grad_cb, jnp.stack(grad_hb), grad_pb]
+
+    def flatten(values, unit):
+        flat = jnp.concatenate([value.reshape(-1) for value in values])
+        return jnp.pad(flat, (0, -flat.size % unit)).reshape(-1, UNIT_BLOCK)
+
+    def unflatten(flat, values):
+        flat, pieces, start = flat.reshape(-1), [], 0
+        for value in values:
+            pieces.append(flat[start : start + value.size].reshape(value.shape))
+            start += value.size
+        return pieces
+
     if paired:
-        grad_hws, grad_conv, grad_table = conv_backward_and_sum(
-            ids_time, char_vecs, ratio, conv_shifted, summed
-        )
+        lstm_parts = [scatter_start(part, "dp", dim) for part, dim in lstm_parts]
+        pw_part = weight_part(top_low, grad_embed_local).reshape(2, -1, summed[0].shape[1])
+        small = flatten(shared, 8 * UNIT_BLOCK)
+        count = small.shape[0]
+        small = jnp.concatenate([small, grad_bias.reshape(BIAS_ROWS, UNIT_BLOCK)])
+        (high_one, high_zero, pw_sum), grad_conv, grad_table, rest = conv_backward_and_sum(
+            ids_time, char_vecs, ratio, conv_shifted, summed + [pw_part], small
+        )
+        lstm_parts, rest = lax.optimization_barrier((lstm_parts, rest))
+        lstm_parts = [
+            own.astype(jnp.float32) + got.astype(jnp.float32) for own, got in lstm_parts
+        ]
         own_mask = lax.dynamic_slice_in_dim(low_mask, dp_index * dp_width, dp_width, 2)
         grad_cw = grad_conv.reshape(TAPS, CDIM, dp_width) * own_mask
-        small = []
+        grad_cb, grad_hbs, grad_pb = unflatten(rest[:count], shared)
+        grad_lbias = rest[count:].reshape(grad_bias.shape)
+        grad_hws = jnp.stack([high_zero.astype(jnp.float32), high_one.astype(jnp.float32)])
+        grad_pws = pw_sum.reshape(-1, PROJ).astype(jnp.float32)
     else:
+        lstm_parts = [
+            lax.psum_scatter(part, "dp", scatter_dimension=dim, tiled=True).astype(jnp.float32)
+            for part, dim in lstm_parts
+        ]
+        pw_part = weight_grad(top_low, grad_embed_local)
+        grad_pws = lax.psum(pw_part, "mp").astype(jnp.float32)
         grad_conv, grad_table = conv_backward(ids_time, char_vecs, ratio, conv_shifted)
         grad_conv = grad_conv.reshape(TAPS, CDIM, FILTERS) * low_mask
-        small = [grad_table, grad_conv]
         grad_hws = jnp.stack([summed[1].astype(jnp.float32), summed[0].astype(jnp.float32)])
-    small += [grad_cb, jnp.stack(grad_hb), grad_pb]
-    flat = jnp.concatenate([value.reshape(-1) for value in small])
-    flat = jnp.pad(flat, (0, -flat.size % 1024)).reshape(-1, UNIT_BLOCK)
-    flat = lax.psum(flat, ("dp", "mp")).reshape(-1)
-    pieces = []
-    start = 0
-    for value in small:
-        pieces.append(flat[start : start + value.size].reshape(value.shape))
-        start += value.size
-    grad_cb, grad_hbs, grad_pb = pieces[-3:]
-    if not paired:
-        grad_table = pieces[0]
-        grad_cw = lax.dynamic_slice_in_dim(pieces[1], dp_index * dp_width, dp_width, 2)
-    grad_lbias = lax.psum(grad_bias, "dp")
-    grad_pws = pw_sum.astype(jnp.float32)
+        shared = [grad_table, grad_conv] + shared
+        flat = lax.psum(flatten(shared, 8 * UNIT_BLOCK), ("dp", "mp"))
+        grad_table, grad_conv, grad_cb, grad_hbs, grad_pb = unflatten(flat, shared)
+        grad_cw = lax.dynamic_slice_in_dim(grad_conv, dp_index * dp_width, dp_width, 2)
+        grad_lbias = lax.psum(grad_bias, "dp")
+    grad_input, grad_state, grad_lproj = (
+        jnp.stack(lstm_parts[2 * index : 2 * index + 2]) for index in range(3)
+    )
     return (
         hidden,
         grad_table,

time: 1620 us -> 1310 us (0.81)
  waiting for transfers between devices: 331 us -> 23.1 us
  blocking collectives: 66.2 us -> 0 us
  Pallas kernels: 906 us -> 962 us
  local copies, waits for them, and re-layouts: 116 us -> 99.7 us
    all_gather x5 -> x0, waiting for transfers between devices: 183 us -> none  [the longest x1 150 us: shards(): lax.all_gather(high_low, 'dp', axis=1, tiled=True)]
    psum x1 -> x0, waiting for transfers between devices: 59.9 us -> none  [shards(): pw_sum = lax.psum(pw_part, 'mp')]
    psum x2 -> x0, blocking collectives: 57.9 us -> none  [the longest x1 46.2 us: shards(): flat = lax.psum(flat, ('dp', 'mp')).reshape(-1)]
    pallas_call x2, Pallas kernels: 349 us -> 404 us  [the longest x1 275 us: conv_backward_and_sum(): pl.pallas_call(functools.partial(tail_kernel, chunks), grid=(-(-(chunks +...]
    all_gather x1, waiting for transfers between devices: 56.7 us -> 23 us  [shards(): embed_all = lax.all_gather(embed_own, 'mp', axis=0)]
    slice x4 -> x9, local copies, waits for them, and re-layouts: 1.18 us -> 34.5 us  [the longest x1 26.2 us: shards(): high_full[layer_index]]
    ppermute x19 -> x24, waiting for transfers between devices: 31.2 us -> 0.06 us  [swap(): lax.ppermute(value, axis, [(index, index ^ bit) for index in range(size)])]
    unnamed x168 -> x184, local copies, waits for them, and re-layouts: 37.4 us -> 14.5 us
  transfers between devices with their start and end apart: 26 -> 25, of which waited for: 10 -> 1; matrix products, arithmetic and copies ran while one was open for 15% -> 14% of each run, Pallas kernels for 36% -> 64%
where the time goes in v3:
time: 1310 us; the launch traced here: 1300 us
  Pallas kernels  962 us (73%)
  matrix products  113 us (9%)
  local copies, waits for them, and re-layouts  99.7 us (8%)
  other arithmetic  69.9 us (5%)
  waiting for transfers between devices  23.1 us (2%)
  between operations  15.3 us (1%)
  starting transfers between devices  14.4 us (1%)
    pallas_call x1, Pallas kernels, lstm_backward(): pl.pallas_call(functools.partial(backward_kernel, size), grid=(WIN,), in_...  298 us
    pallas_call x1, Pallas kernels, conv_backward_and_sum(): pl.pallas_call(functools.partial(tail_kernel, chunks), grid=(-(-(chunks +...  275 us
    pallas_call x1, Pallas kernels, lstm_forward(): pl.pallas_call(functools.partial(forward_kernel, size), grid=(WIN + 1,),...  260 us
    pallas_call x1, Pallas kernels, start_gather(): pl.pallas_call(start_kernel, grid=(START_STEPS,), in_specs=[vmem] * 8, ou...  129 us
    dot_general x3, matrix products, weight_part(): jnp.dot(left_all.T, right_all, preferred_element_type=jnp.float32)  30.9 us
    dot_general x6, matrix products, outer(): jnp.dot(left.reshape(WIN * rows, -1).T, right.reshape(WIN * rows, -1), pr...  30.2 us
  transfers between devices with their start and end apart: 25, of which 1 were waited for; matrix products, arithmetic and copies ran while one was open for 14% of the time, Pallas kernels for 64%

profile of v3, /device:TPU:0, one launch (start us, length us, event | category | flops | bytes accessed | tf_op | source)
XLA Modules:
  0.0 1297.8 jit_solution(13659378481856939358)
XLA Ops:
  11.1 9.1 convert_element_type.366
  23.5 128.8 %shard_map.265 = (f32[288,2048]{1,0:T(8,128)S(1)}, bf16[7,288,128]{2,1,0:T(8,128)(2,1)S(1)}, bf16[8,256,2048]{2,1,0:T(8,128)(2,1)}, bf16[2,4,8,64,4096]{4,3,2,1,...) custom-call(s32[288,50]{1,0:T(8,128)S(1)} %pad.64.clone.ids_ref, ...), custom_call_target="tpu_custom_call" | custom-call | tf_op jit(solution)/shard_map/pallas_call | solution.py:1493
  152.4 26.2 %fusion.47 = (bf16[1,4,8,64,4096]{4,3,2,1,0:T(8,128)(2,1)}, bf16[1,4,8,64,4096]{4,3,2,1,0:T(8,128)(2,1)}) fusion(bf16[2,4,8,64,4096]{4,3,2,1,0:T(8,128)(2,1)} %get-tuple-element.62), kind=kLoop, calls=%fused_computation.172 | loop fusion | bytes 67108864 | tf_op jit(solution)/shard_map/slice | solution.py:1669
  180.7 11.3 convolution_add_fusion.1
  195.8 6.9 convolution_add_fusion
  241.6 23.0 %all-gather.3.cloned.1.call-done = bf16[160,16,512]{2,1,0:T(8,128)(2,1)} async-done(((bf16[20,16,512]{2,1,0:T(8,128)(2,1)}), bf16[160,16,512]{2,1,0:T(8,128)(2,1)}) %all-gather.3.cloned.1.call-update) | async-done | bytes 2621456 | tf_op jit(solution)/shard_map/all_gather | solution.py:1702
  265.3 260.3 %shard_map.266 = (bf16[20,128,512]{2,1,0:T(8,128)(2,1)}, f32[20,128,2048]{2,1,0:T(8,128)}, f32[20,128,2048]{2,1,0:T(8,128)}, f32[20,128,512]{2,1,0:T(8,128)}, f3...) custom-call(bf16[8,20,16,512]{3,2,1,0:T(8,128)(2,1)} %bitcast.155, ...), custom_call_target="tpu_custom_call" | custom-call | tf_op jit(solution)/shard_map/pallas_call | solution.py:275
  527.8 298.0 %shard_map.267 = (bf16[20,128,2048]{2,1,0:T(8,128)(2,1)}, bf16[20,128,2048]{2,1,0:T(8,128)(2,1)}, bf16[20,128,512]{2,1,0:T(8,128)(2,1)}, bf16[20,128,512]{2,1,0:...) custom-call(f32[20,128,2048]{2,1,0:T(8,128)} %get-tuple-element.70.gate0_ref, ...), custom_call_target="tpu_custom_call" | custom-call | tf_op jit(solution)/shard_map/pallas_call | solution.py:507
  829.2 7.2 multiply_convert_fusion.3
  837.8 14.1 %multiply_convert_fusion.1 = (bf16[280,2048]{1,0:T(8,128)(2,1)}, bf16[280,2048]{1,0:T(8,128)(2,1)}, f32[280,2048]{1,0:T(8,128)}) fusion(f32[280,4096]{1,0:T(8,128)} %convolution_add_fusion.1, f32[2048]{0:T(1024)S(1)} %copy-done.60, f32[2048]{0:T(1024)S(1)} %subtract_convert_fusion, f32[288,2048]{1,0:T(8,128)S(1)} %get-tuple-element.61, ...), kind=kOutput, calls=%fused_computation.36 | convolution fusion | flops 4719984640 | bytes 35143680 | tf_op jit(solution)/shard_map/dot_general | solution.py:1769
  857.6 12.0 fusion.49
  871.2 4.9 fusion.21
  879.9 5.8 bitcast_convert_fusion
  887.4 5.8 bitcast_convert_fusion.2
  893.3 5.8 bitcast_convert_fusion.3
  899.2 6.2 bitcast_convert_fusion.1
  912.4 4.8 reshape.246
  917.2 4.5 pad_maximum_fusion
  945.0 5.0 collective-permute-start.23
  953.4 12.4 convolution_convert_fusion
  968.0 15.2 %convolution_convert_fusion.1 = bf16[1024,4096]{1,0:T(8,128)(2,1)} fusion(bf16[280,4096]{1,0:T(8,128)(2,1)S(1)} %collective-permute-done.1, bf16[280,2048]{1,0:T(8,128)(2,1)S(1)} %copy-done.12, bf16[280,2048]{1,0:T(8,128)(2,1)S(1)} %get-tuple-element.118, bf16[280,1024]{1,0:T(8,128)(2,1)S(1)} %collective-permute-done, bf16[280,512]{1,0:T(8,128)(2,1)S(1)} %copy-done.50, ...), kind=kOutput, calls=%fused_computation.2 | convolution fusion | flops 4719017984 | bytes 14123008 | tf_op jit(solution)/shard_map/dot_general | solution.py:1568
  983.2 275.0 %shard_map.268 = (bf16[34,2,16,4096]{3,2,1,0:T(8,128)(2,1)}, f32[112,512]{1,0:T(8,128)}, f32[384,128]{1,0:T(8,128)}) custom-call(s32[8,1728]{1,0:T(8,128)} %reshape.248.hot_ref, s32[2,288]{1,0:T(2,128)} %slice.163.hot_extra_ref, bf16[7,288,128]{2,1,0:T(8,128)(2,1)} %copy-done.2, bf16[256,1728]{1,0:T(8,128)(2,1)} %pad_maximum_fusion.5.turned_ref, ...), custom_call_target="tpu_custom_call" | custom-call | tf_op jit(solution)/shard_map/pallas_call | solution.py:1173
  1260.3 6.1 fusion.48
  1280.6 9.5 maximum_convert_fusion
  (341 shorter events, 124.5 us)
Async XLA Ops:
  7.2 257.4 %all-gather.3.cloned.1.call-start = ((), (), s32[]{:S(2)}) async-start(), calls=%async_computation | async-start | bytes 2949120 | tf_op jit(solution)/shard_map/all_gather | solution.py:1702
  212.2 715.8 %collective-permute-start.4 = (bf16[280,1024]{1,0:T(8,128)(2,1)}, bf16[280,1024]{1,0:T(8,128)(2,1)}, u32[]{:S(2)}, u32[]{:S(2)}) collective-permute-start(bf16[280,1024]{1,0:T(8,128)(2,1)} %pad_maximum_fusion.8), channel_id=1, source_target_pairs={{0,8},{8,0},{16,24},{24,16},{1,9},{9,1},{17,25},{25,17},{2,10},{10... | collective-permute-start | bytes 1720328 | tf_op jit(solution)/shard_map/ppermute | solution.py:1533
  876.9 46.5 %collective-permute-start.21 = (bf16[512,128]{1,0:T(8,128)(2,1)}, bf16[512,128]{1,0:T(8,128)(2,1)}, u32[]{:S(2)}, u32[]{:S(2)}) collective-permute-start(bf16[512,128]{1,0:T(8,128)(2,1)} %get-tuple-element.159), channel_id=1, source_target_pairs={{0,8},{8,0},{16,24},{24,16},{1,9},{9,1},{17,25},{25,17},{2,10},{10... | collective-permute-start | bytes 393224 | tf_op jit(solution)/shard_map/ppermute | solution.py:1533
  876.9 46.9 %collective-permute-start.22 = (bf16[512,128]{1,0:T(8,128)(2,1)}, bf16[512,128]{1,0:T(8,128)(2,1)}, u32[]{:S(2)}, u32[]{:S(2)}) collective-permute-start(bf16[512,128]{1,0:T(8,128)(2,1)} %get-tuple-element.158), channel_id=1, source_target_pairs={{0,8},{8,0},{16,24},{24,16},{1,9},{9,1},{17,25},{25,17},{2,10},{10... | collective-permute-start | bytes 393224 | tf_op jit(solution)/shard_map/ppermute | solution.py:1533
  879.8 44.1 %collective-permute-start.18 = (bf16[512,128]{1,0:T(8,128)(2,1)}, bf16[512,128]{1,0:T(8,128)(2,1)}, u32[]{:S(2)}, u32[]{:S(2)}) collective-permute-start(bf16[512,128]{1,0:T(8,128)(2,1)} %get-tuple-element.163), channel_id=1, source_target_pairs={{0,8},{8,0},{16,24},{24,16},{1,9},{9,1},{17,25},{25,17},{2,10},{10... | collective-permute-start | bytes 393224 | tf_op jit(solution)/shard_map/ppermute | solution.py:1533
  887.0 41.6 %collective-permute-start.15 = (bf16[128,2048]{1,0:T(8,128)(2,1)}, bf16[128,2048]{1,0:T(8,128)(2,1)}, u32[]{:S(2)}, u32[]{:S(2)}) collective-permute-start(bf16[128,2048]{1,0:T(8,128)(2,1)} %get-tuple-element.125), channel_id=1, source_target_pairs={{0,8},{8,0},{16,24},{24,16},{1,9},{9,1},{17,25},{25,17},{2,10},{10... | collective-permute-start | bytes 1572872 | tf_op jit(solution)/shard_map/ppermute | solution.py:1533
  923.3 5.2 collective-permute-start.5
  923.8 10.9 collective-permute-start.16
  926.1 25.2 %collective-permute-start.3 = (bf16[280,4096]{1,0:T(8,128)(2,1)}, bf16[280,4096]{1,0:T(8,128)(2,1)}, u32[]{:S(2)}, u32[]{:S(2)}) collective-permute-start(bf16[280,4096]{1,0:T(8,128)(2,1)} %pad_maximum_fusion.2), channel_id=1, source_target_pairs={{0,8},{8,0},{16,24},{24,16},{1,9},{9,1},{17,25},{25,17},{2,10},{10... | collective-permute-start | bytes 6881288 | tf_op jit(solution)/shard_map/ppermute | solution.py:1533
  928.0 9.9 collective-permute-start.12
  928.5 10.0 collective-permute-start.13
  928.6 10.1 collective-permute-start.10
  934.8 6.9 collective-permute-start.9
  938.0 6.6 collective-permute-start.6
  938.5 6.5 collective-permute-start.7
  938.6 29.3 %collective-permute-start.1 = (bf16[280,4096]{1,0:T(8,128)(2,1)S(1)}, bf16[280,4096]{1,0:T(8,128)(2,1)S(1)}, u32[]{:S(2)}, u32[]{:S(2)}) collective-permute-start(bf16[280,4096]{1,0:T(8,128)(2,1)S(1)} %copy-done.20), channel_id=1, source_target_pairs={{0,8},{8,0},{16,24},{24,16},{1,9},{9,1},{17,25},{25,17},{2,10},{10... | collective-permute-start | bytes 6881288 | tf_op jit(solution)/shard_map/ppermute | solution.py:1533
  941.6 9.7 collective-permute-start.2
  944.6 21.3 %collective-permute-start = (bf16[280,1024]{1,0:T(8,128)(2,1)S(1)}, bf16[280,1024]{1,0:T(8,128)(2,1)S(1)}, u32[]{:S(2)}, u32[]{:S(2)}) collective-permute-start(bf16[280,1024]{1,0:T(8,128)(2,1)S(1)} %copy-done.38), channel_id=1, source_target_pairs={{0,8},{8,0},{16,24},{24,16},{1,9},{9,1},{17,25},{25,17},{2,10},{10... | collective-permute-start | bytes 1720328 | tf_op jit(solution)/shard_map/ppermute | solution.py:1533
  945.0 20.9 %collective-permute-start.23 = (bf16[512,128]{1,0:T(8,128)(2,1)S(1)}, bf16[512,128]{1,0:T(8,128)(2,1)S(1)}, u32[]{:S(2)}, u32[]{:S(2)}) collective-permute-start(bf16[512,128]{1,0:T(8,128)(2,1)S(1)} %copy-done.56), channel_id=1, source_target_pairs={{0,16},{8,24},{16,0},{24,8},{1,17},{9,25},{17,1},{25,9},{2,18},{10... | collective-permute-start | bytes 393224 | tf_op jit(solution)/shard_map/ppermute | solution.py:1533
  951.4 307.6 %collective-permute-start.20 = (bf16[512,128]{1,0:T(8,128)(2,1)}, bf16[512,128]{1,0:T(8,128)(2,1)}, u32[]{:S(2)}, u32[]{:S(2)}) collective-permute-start(bf16[512,128]{1,0:T(8,128)(2,1)} %get-tuple-element.160), channel_id=1, source_target_pairs={{0,16},{8,24},{16,0},{24,8},{1,17},{9,25},{17,1},{25,9},{2,18},{10... | collective-permute-start | bytes 393224 | tf_op jit(solution)/shard_map/ppermute | solution.py:1533
  951.4 307.6 %collective-permute-start.17 = (bf16[128,2048]{1,0:T(8,128)(2,1)}, bf16[128,2048]{1,0:T(8,128)(2,1)}, u32[]{:S(2)}, u32[]{:S(2)}) collective-permute-start(bf16[128,2048]{1,0:T(8,128)(2,1)} %get-tuple-element.122), channel_id=1, source_target_pairs={{0,16},{8,24},{16,0},{24,8},{1,17},{9,25},{17,1},{25,9},{2,18},{10... | collective-permute-start | bytes 1572872 | tf_op jit(solution)/shard_map/ppermute | solution.py:1533
  965.8 293.1 %collective-permute-start.14 = (bf16[128,2048]{1,0:T(8,128)(2,1)}, bf16[128,2048]{1,0:T(8,128)(2,1)}, u32[]{:S(2)}, u32[]{:S(2)}) collective-permute-start(bf16[128,2048]{1,0:T(8,128)(2,1)} %get-tuple-element.126), channel_id=1, source_target_pairs={{0,16},{8,24},{16,0},{24,8},{1,17},{9,25},{17,1},{25,9},{2,18},{10... | collective-permute-start | bytes 1572872 | tf_op jit(solution)/shard_map/ppermute | solution.py:1533
  965.9 293.1 %collective-permute-start.11 = (bf16[128,2048]{1,0:T(8,128)(2,1)}, bf16[128,2048]{1,0:T(8,128)(2,1)}, u32[]{:S(2)}, u32[]{:S(2)}) collective-permute-start(bf16[128,2048]{1,0:T(8,128)(2,1)} %get-tuple-element.130), channel_id=1, source_target_pairs={{0,16},{8,24},{16,0},{24,8},{1,17},{9,25},{17,1},{25,9},{2,18},{10... | collective-permute-start | bytes 1572872 | tf_op jit(solution)/shard_map/ppermute | solution.py:1533
  967.9 291.1 %collective-permute-start.8 = (bf16[128,2048]{1,0:T(8,128)(2,1)}, bf16[128,2048]{1,0:T(8,128)(2,1)S(1)}, u32[]{:S(2)}, u32[]{:S(2)}) collective-permute-start(bf16[128,2048]{1,0:T(8,128)(2,1)} %get-tuple-element.134), channel_id=1, source_target_pairs={{0,16},{8,24},{16,0},{24,8},{1,17},{9,25},{17,1},{25,9},{2,18},{10... | collective-permute-start | bytes 1572872 | tf_op jit(solution)/shard_map/ppermute | solution.py:1533
  (86 other events, 735.0 us)
Sparse Core Ops, SparseCore 0:
  209.2 55.3 all-gather.2

commit v4 on v3

--- a/solution.py
+++ b/solution.py
@@ -534,6 +534,501 @@
     )(*gates, *cprevs, *cnews, *cots, *stats, win, wst, wpr, reset, first_cot, first_stat)
 
 
+class RingExchange(Exchange):
+    def __init__(self, part_ref, sum_ref, all_ref, sems):
+        super().__init__(4, part_ref, sum_ref, all_ref, sems)
+        self.near = lax.rem(self.me, 2)
+        self.me = self.me // 2
+
+    def part_copy(self, way, offset, incoming):
+        peer = lax.rem(self.me + (4 - offset if incoming else offset), 4)
+        return pltpu.make_async_remote_copy(
+            src_ref=self.part_ref.at[way, peer],
+            dst_ref=self.sum_ref.at[way, peer if incoming else self.me],
+            send_sem=self.part_send.at[way, offset],
+            recv_sem=self.part_recv.at[way, offset],
+            device_id={"mp": 2 * peer + self.near},
+            device_id_type=pl.DeviceIdType.MESH,
+        )
+
+    def all_copy(self, way, offset, incoming):
+        peer = lax.rem(self.me + (4 - offset if incoming else offset), 4)
+        slot = peer if incoming else self.me
+        return pltpu.make_async_remote_copy(
+            src_ref=self.all_ref.at[way, slot],
+            dst_ref=self.all_ref.at[way, slot],
+            send_sem=self.all_send.at[way, offset],
+            recv_sem=self.all_recv.at[way, offset],
+            device_id={"mp": 2 * peer + self.near},
+            device_id_type=pl.DeviceIdType.MESH,
+        )
+
+
+def ring_forward_kernel(
+    emb_ref,
+    win_ref,
+    wst_ref,
+    wpr_ref,
+    bias_ref,
+    cell_ref,
+    hid_ref,
+    reset_ref,
+    embt_ref,
+    gate_ref,
+    cprev_ref,
+    cnew_ref,
+    low_ref,
+    hprev_ref,
+    stat_ref,
+    out_ref,
+    pre_ref,
+    state_ref,
+    part_ref,
+    sum_ref,
+    all_ref,
+    stage_ref,
+    part_send,
+    part_recv,
+    all_send,
+    all_recv,
+    out_sem,
+    out_send,
+    out_recv,
+):
+    step = pl.program_id(0)
+    half_rows = reset_ref.shape[1]
+    part = half_rows // 4
+    units = wpr_ref.shape[1]
+    blocks = units // UNIT_BLOCK
+    wide = 4 * UNIT_BLOCK
+    comm = RingExchange(part_ref, sum_ref, all_ref, (part_send, part_recv, all_send, all_recv))
+    near = comm.near
+
+    def time_of(at):
+        return at + near * (WIN - 1 - 2 * at)
+
+    def input_part(at):
+        emb = emb_ref[:, :, time_of(at)]
+        halves = [emb[:, way].reshape(half_rows, PROJ) for way in range(2)]
+        both = jnp.concatenate(halves, axis=0)
+        slot = lax.rem(at, 2)
+        for owner in range(2):
+            for block in range(blocks):
+                cols = slice(block * wide, (block + 1) * wide)
+                pre_ref[slot, owner, :, cols] = (
+                    jnp.dot(both, win_ref[owner, :, cols], preferred_element_type=jnp.float32)
+                    + bias_ref[owner, :, cols]
+                )
+
+    def out_copies(way, at, incoming):
+        slot = lax.rem(at, 2)
+        now = time_of(at)
+        src = stage_ref.at[way, slot]
+        other = WIN - 1 - now if incoming else now
+        return (
+            pltpu.make_async_copy(src, out_ref.at[near, now, :, way], out_sem.at[way, slot]),
+            pltpu.make_async_remote_copy(
+                src_ref=src,
+                dst_ref=out_ref.at[1 - near if incoming else near, other, :, way],
+                send_sem=out_send.at[way, slot],
+                recv_sem=out_recv.at[way, at],
+                device_id={"mp": 2 * comm.me + 1 - near},
+                device_id_type=pl.DeviceIdType.MESH,
+            ),
+        )
+
+    def emit_hidden(way):
+        at = step - 1
+
+        @pl.when(at >= 2)
+        def _():
+            local, remote = out_copies(way, at - 2, False)
+            local.wait()
+            remote.wait_send()
+
+        stage_ref[way, lax.rem(at, 2)] = all_ref[way]
+        for copy in out_copies(way, at, False):
+            copy.start()
+
+    def cell_step(way):
+        now = time_of(step)
+        keep = jnp.where(reset_ref[way] - near == now, 0.0, 1.0)
+        keep_low = jnp.concatenate([keep.astype(jnp.bfloat16)] * (PROJ // UNIT_BLOCK), axis=1)
+        hidden_prev = all_ref[way].reshape(half_rows, PROJ) * keep_low
+        hprev_ref[0, way] = hidden_prev
+        embt_ref[0, way] = emb_ref[:, way, now].reshape(half_rows, PROJ)
+        slot = lax.rem(step, 2)
+        rows = slice(way * half_rows, (way + 1) * half_rows)
+        partial = None
+        for owner in range(2):
+            for block in range(blocks):
+                cols = slice(block * wide, (block + 1) * wide)
+                unit = slice(block * UNIT_BLOCK, (block + 1) * UNIT_BLOCK)
+                spot = slice(
+                    owner * units + block * UNIT_BLOCK, owner * units + (block + 1) * UNIT_BLOCK
+                )
+                place = slice((owner * blocks + block) * wide, (owner * blocks + block + 1) * wide)
+                pre = pre_ref[slot, owner, rows, cols] + jnp.dot(
+                    hidden_prev, wst_ref[owner, :, cols], preferred_element_type=jnp.float32
+                )
+                gate_in = sigmoid_of(pre[:, :UNIT_BLOCK])
+                gate_forget = sigmoid_of(pre[:, UNIT_BLOCK : 2 * UNIT_BLOCK])
+                gate_cand = jnp.tanh(pre[:, 2 * UNIT_BLOCK : 3 * UNIT_BLOCK])
+                gate_out = sigmoid_of(pre[:, 3 * UNIT_BLOCK :])
+                cell_prev = state_ref[way, owner, :, unit] * keep
+                cell_new = CLIP * jnp.tanh(
+                    (gate_forget * cell_prev + gate_in * gate_cand) * (1.0 / CLIP)
+                )
+                gate_ref[0, way, :, place] = jnp.concatenate(
+                    [gate_in, gate_forget, gate_cand, gate_out], axis=1
+                )
+                cprev_ref[0, way, :, spot] = cell_prev
+                cnew_ref[0, way, :, spot] = cell_new
+                state_ref[way, owner, :, unit] = cell_new
+                low_ref[0, way, :, spot] = (gate_out * jnp.tanh(cell_new)).astype(jnp.bfloat16)
+            term = jnp.dot(
+                low_ref[0, way, :, owner * units : (owner + 1) * units],
+                wpr_ref[owner],
+                preferred_element_type=jnp.float32,
+            )
+            partial = term if partial is None else partial + term
+        part_ref[way] = partial.astype(jnp.bfloat16).reshape(4, part, PROJ)
+        comm.send_parts(way)
+
+    def close_step(way, at):
+        total = comm.take_sum(way)
+        stat_ref[way, at] = total
+        comm.send_all(way, (CLIP * jnp.tanh(total * (1.0 / CLIP))).astype(jnp.bfloat16))
+
+    @pl.when(step == 0)
+    def _():
+        for way in range(2):
+            all_ref[way] = hid_ref[way]
+            state_ref[way] = cell_ref[way]
+        input_part(jnp.int32(0))
+        mp_barrier(8)
+
+    @pl.when(step > 0)
+    def _():
+        comm.wait_all(0)
+        emit_hidden(0)
+
+    @pl.when(step < WIN)
+    def _():
+        cell_step(0)
+
+    @pl.when(step > 0)
+    def _():
+        close_step(1, step - 1)
+
+    @pl.when(step < WIN)
+    def _():
+        @pl.when(step < WIN - 1)
+        def _():
+            input_part(step + 1)
+
+        close_step(0, step)
+
+    @pl.when(step > 0)
+    def _():
+        comm.wait_all(1)
+        emit_hidden(1)
+
+    @pl.when(step < WIN)
+    def _():
+        cell_step(1)
+
+    @pl.when(step == WIN)
+    def _():
+        for way in range(2):
+            for at in (WIN - 2, WIN - 1):
+                local, remote = out_copies(way, jnp.int32(at), False)
+                local.wait()
+                remote.wait_send()
+
+            @pl.loop(0, WIN)
+            def _(at):
+                out_copies(way, at, True)[1].wait_recv()
+
+
+def ring_forward(emb, win, wst, wpr, bias, cell, hid, reset):
+    half_rows = reset.shape[1]
+    part = half_rows // 4
+    gates = 2 * win.shape[2]
+    units = 2 * wpr.shape[1]
+    last = WIN - 1
+    vmem = pl.BlockSpec(memory_space=pltpu.VMEM)
+    bf16, f32 = jnp.bfloat16, jnp.float32
+    dma = pltpu.SemaphoreType.DMA
+    widths = (
+        (PROJ, bf16),
+        (gates, f32),
+        (units, f32),
+        (units, f32),
+        (units, bf16),
+        (PROJ, bf16),
+    )
+    return pl.pallas_call(
+        ring_forward_kernel,
+        grid=(WIN + 1,),
+        in_specs=[vmem] * 8,
+        out_specs=[
+            pl.BlockSpec((1, 2, half_rows, width), lambda w: (jnp.minimum(w, last), 0, 0, 0))
+            for width, kind in widths
+        ]
+        + [vmem, pl.BlockSpec(memory_space=pl.ANY)],
+        out_shape=[
+            jax.ShapeDtypeStruct((WIN, 2, half_rows, width), kind) for width, kind in widths
+        ]
+        + [
+            jax.ShapeDtypeStruct((2, WIN, part, PROJ), f32),
+            jax.ShapeDtypeStruct((2, WIN, 4, 2, part, PROJ), bf16),
+        ],
+        scratch_shapes=[
+            pltpu.VMEM((2, 2, 2 * half_rows, gates // 2), f32),
+            pltpu.VMEM((2, 2, half_rows, units // 2), f32),
+            pltpu.VMEM((2, 4, part, PROJ), bf16),
+            pltpu.VMEM((2, 4, part, PROJ), bf16),
+            pltpu.VMEM((2, 4, part, PROJ), bf16),
+            pltpu.VMEM((2, 2, 4, part, PROJ), bf16),
+        ]
+        + [dma((2, 4))] * 4
+        + [dma((2, 2))] * 2
+        + [dma((2, WIN))],
+        compiler_params=pltpu.CompilerParams(
+            collective_id=5, has_side_effects=True, vmem_limit_bytes=56 * 2**20
+        ),
+    )(emb, win, wst, wpr, bias, cell, hid, reset)
+
+
+def ring_backward_kernel(
+    gate_ref,
+    cprev_ref,
+    cnew_ref,
+    cot_ref,
+    stat_ref,
+    win_ref,
+    wst_ref,
+    wpr_ref,
+    reset_ref,
+    da_ref,
+    ds_ref,
+    bias_ref,
+    de_ref,
+    cell_ref,
+    part_ref,
+    sum_ref,
+    all_ref,
+    part_send,
+    part_recv,
+    all_send,
+    all_recv,
+    embed_part_ref,
+    embed_got_ref,
+    embed_send,
+    embed_recv,
+):
+    step = pl.program_id(0)
+    half_rows = reset_ref.shape[1]
+    part = half_rows // 4
+    units = wpr_ref.shape[1]
+    blocks = units // UNIT_BLOCK
+    wide = 4 * UNIT_BLOCK
+    comm = RingExchange(part_ref, sum_ref, all_ref, (part_send, part_recv, all_send, all_recv))
+    near = comm.near
+    device = lax.axis_index("mp")
+
+    def scan_of(at):
+        return WIN - 1 - at
+
+    def time_of(at):
+        back = scan_of(at)
+        return back + near * (WIN - 1 - 2 * back)
+
+    def stat_step(way, at, total):
+        grad = cot_ref[way, time_of(at)].astype(jnp.float32)
+        if total is not None:
+            own = reset_ref[way, pl.ds(comm.me * part, part), :] - near
+            keep = jnp.where(own == time_of(at - 1), 0.0, 1.0)
+            grad = grad + total * jnp.concatenate([keep] * (PROJ // UNIT_BLOCK), axis=1)
+        slope = jnp.tanh(stat_ref[way, scan_of(at)] * (1.0 / CLIP))
+        comm.send_all(way, (grad * (1.0 - slope * slope)).astype(jnp.bfloat16))
+
+    def cell_step(way):
+        comm.wait_all(way)
+        keep = jnp.where(reset_ref[way] - near == time_of(step), 0.0, 1.0)
+        grad_stat = all_ref[way].reshape(half_rows, PROJ)
+        ds_ref[0, way] = grad_stat
+        for owner in range(2):
+            for block in range(blocks):
+                unit = slice(block * UNIT_BLOCK, (block + 1) * UNIT_BLOCK)
+                spot = slice(
+                    owner * units + block * UNIT_BLOCK, owner * units + (block + 1) * UNIT_BLOCK
+                )
+                place = slice((owner * blocks + block) * wide, (owner * blocks + block + 1) * wide)
+                grad_out = lax.dot_general(
+                    grad_stat,
+                    wpr_ref[owner, unit, :],
+                    (((1,), (1,)), ((), ())),
+                    preferred_element_type=jnp.float32,
+                )
+                gates = gate_ref[0, way, :, place]
+                gate_in = gates[:, :UNIT_BLOCK]
+                gate_forget = gates[:, UNIT_BLOCK : 2 * UNIT_BLOCK]
+                gate_cand = gates[:, 2 * UNIT_BLOCK : 3 * UNIT_BLOCK]
+                gate_out = gates[:, 3 * UNIT_BLOCK :]
+                cell_prev = cprev_ref[0, way, :, spot]
+                cell_new = cnew_ref[0, way, :, spot]
+                tanh_cell = jnp.tanh(cell_new)
+                grad_total = (
+                    grad_out * gate_out * (1.0 - tanh_cell * tanh_cell) + cell_ref[way, :, spot]
+                )
+                scaled = cell_new * (1.0 / CLIP)
+                grad_inner = grad_total * (1.0 - scaled * scaled)
+                cell_ref[way, :, spot] = grad_inner * gate_forget * keep
+                grad_pre = jnp.concatenate(
+                    [
+                        grad_inner * gate_cand * gate_in * (1.0 - gate_in),
+                        grad_inner * cell_prev * gate_forget * (1.0 - gate_forget),
+                        grad_inner * gate_in * (1.0 - gate_cand * gate_cand),
+                        grad_out * tanh_cell * gate_out * (1.0 - gate_out),
+                    ],
+                    axis=1,
+                ).astype(jnp.bfloat16)
+                da_ref[0, way, :, place] = grad_pre
+                bias_ref[:, place] += jnp.sum(
+                    grad_pre.astype(jnp.float32).reshape(half_rows // 8, 8, wide), axis=0
+                )
+
+        @pl.when(step < WIN - 1)
+        def _():
+            partial = None
+            for owner in range(2):
+                span = slice(owner * blocks * wide, (owner + 1) * blocks * wide)
+                term = lax.dot_general(
+                    da_ref[0, way, :, span],
+                    wst_ref[owner],
+                    (((1,), (1,)), ((), ())),
+                    preferred_element_type=jnp.float32,
+                )
+                partial = term if partial is None else partial + term
+            part_ref[way] = partial.astype(jnp.bfloat16).reshape(4, part, PROJ)
+            comm.send_parts(way)
+
+    def embed_copy(src, dst, offset):
+        return pltpu.make_async_remote_copy(
+            src_ref=src,
+            dst_ref=dst,
+            send_sem=embed_send.at[offset],
+            recv_sem=embed_recv.at[offset],
+            device_id={"mp": lax.rem(device + offset, 8)},
+            device_id_type=pl.DeviceIdType.MESH,
+        )
+
+    def embed_step():
+        now = time_of(step)
+        total = None
+        for owner in range(2):
+            span = slice(owner * blocks * wide, (owner + 1) * blocks * wide)
+            both = jnp.concatenate([da_ref[0, 0, :, span], da_ref[0, 1, :, span]], axis=0)
+            term = lax.dot_general(
+                both,
+                win_ref[owner],
+                (((1,), (1,)), ((), ())),
+                preferred_element_type=jnp.float32,
+            )
+            total = term if total is None else total + term
+        total = total.astype(jnp.bfloat16)
+        for way in range(2):
+            embed_part_ref[now, way] = total[way * half_rows : (way + 1) * half_rows].reshape(
+                4, part, PROJ
+            )
+        for offset in range(1, 8):
+            peer = lax.rem(device + offset, 8)
+            embed_copy(
+                embed_part_ref.at[now, lax.rem(peer, 2), peer // 2],
+                embed_got_ref.at[device, now],
+                offset,
+            ).start()
+
+    def embed_finish():
+        total = embed_part_ref[:, near, comm.me].astype(jnp.float32)
+        for offset in range(1, 8):
+            peer = lax.rem(device + 8 - offset, 8)
+            embed_copy(embed_got_ref.at[peer], embed_got_ref.at[peer], offset).wait_recv()
+            total = total + embed_got_ref[peer].astype(jnp.float32)
+        de_ref[...] = total.astype(jnp.bfloat16)
+        for offset in range(1, 8):
+            embed_copy(embed_got_ref.at[device], embed_got_ref.at[device], offset).wait_send()
+
+    @pl.when(step == 0)
+    def _():
+        cell_ref[...] = jnp.zeros(cell_ref.shape, jnp.float32)
+        bias_ref[...] = jnp.zeros(bias_ref.shape, jnp.float32)
+        mp_barrier(8)
+        for way in range(2):
+            stat_step(way, 0, None)
+
+    cell_step(0)
+
+    @pl.when(step > 0)
+    def _():
+        stat_step(1, step, comm.take_sum(1))
+
+    @pl.when(step < WIN - 1)
+    def _():
+        stat_step(0, step + 1, comm.take_sum(0))
+
+    cell_step(1)
+    embed_step()
+
+    @pl.when(step == WIN - 1)
+    def _():
+        embed_finish()
+
+
+def ring_backward(gates, cprevs, cnews, cots, stats, win, wst, wpr, reset):
+    half_rows = reset.shape[1]
+    part = half_rows // 4
+    width = 2 * win.shape[2]
+    units = 2 * wpr.shape[1]
+    last = WIN - 1
+    vmem = pl.BlockSpec(memory_space=pltpu.VMEM)
+    bf16, f32 = jnp.bfloat16, jnp.float32
+    dma = pltpu.SemaphoreType.DMA
+
+    def block(size):
+        return pl.BlockSpec((1, 2, half_rows, size), lambda w: (last - w, 0, 0, 0))
+
+    return pl.pallas_call(
+        ring_backward_kernel,
+        grid=(WIN,),
+        in_specs=[block(width), block(units), block(units)] + [vmem] * 6,
+        out_specs=[block(width), block(PROJ), vmem, vmem],
+        out_shape=[
+            jax.ShapeDtypeStruct((WIN, 2, half_rows, width), bf16),
+            jax.ShapeDtypeStruct((WIN, 2, half_rows, PROJ), bf16),
+            jax.ShapeDtypeStruct((8, width), f32),
+            jax.ShapeDtypeStruct((WIN, part, PROJ), bf16),
+        ],
+        scratch_shapes=[
+            pltpu.VMEM((2, half_rows, units), f32),
+            pltpu.VMEM((2, 4, part, PROJ), bf16),
+            pltpu.VMEM((2, 4, part, PROJ), bf16),
+            pltpu.VMEM((2, 4, part, PROJ), bf16),
+        ]
+        + [dma((2, 4))] * 4
+        + [
+            pltpu.VMEM((WIN, 2, 4, part, PROJ), bf16),
+            pltpu.VMEM((8, WIN, part, PROJ), bf16),
+        ]
+        + [dma((8,))] * 2,
+        compiler_params=pltpu.CompilerParams(
+            collective_id=6, has_side_effects=True, vmem_limit_bytes=56 * 2**20
+        ),
+    )(gates, cprevs, cnews, cots, stats, win, wst, wpr, reset)
+
+
 SHIFTS = 8
 GROUP = SHIFTS * CDIM
 FBLOCK = 256
@@ -835,7 +1330,8 @@
     part0_ref,
     part2_ref,
     small_ref,
-    sum_ref,
+    high_sum_ref,
+    proj_sum_ref,
     conv_ref,
     table_ref,
     grad_ref,
@@ -956,7 +1452,19 @@
 
     def store(chunk):
         slot = lax.rem(chunk, 2)
-        return pltpu.make_async_copy(wide_ref.at[slot], sum_ref.at[chunk], store_sem.at[slot])
+        return wide_ref.at[slot], store_sem.at[slot]
+
+    def store_act(chunk, act):
+        src, sem = store(chunk)
+        layer, row = chunk // per_layer, lax.rem(chunk, per_layer)
+
+        @pl.when(layer < 2)
+        def _():
+            getattr(pltpu.make_async_copy(src, high_sum_ref.at[1 - layer, row], sem), act)()
+
+        @pl.when(layer == 2)
+        def _():
+            getattr(pltpu.make_async_copy(src, proj_sum_ref.at[row], sem), act)()
 
     def when_chunk(chunk, body):
         @pl.when(jnp.logical_and(chunk >= 0, chunk < chunks))
@@ -1009,12 +1517,12 @@
 
         @pl.when(chunk >= 2)
         def _():
-            store(chunk - 2).wait()
+            store_act(chunk - 2, "wait")
 
         slot = lax.rem(chunk, 2)
         wide_ref[slot, near] = all_z_ref[chunk]
         wide_ref[slot, 1 - near] = all_x_ref[chunk]
-        store(chunk).start()
+        store_act(chunk, "start")
 
     def small_copies(stage):
         if stage == 0:
@@ -1145,7 +1653,7 @@
     @pl.when(tick == pl.num_programs(0) - 1)
     def _():
         for chunk in (chunks - 2, chunks - 1):
-            store(jnp.int32(chunk)).wait()
+            store_act(jnp.int32(chunk), "wait")
 
         @pl.loop(0, chunks)
         def _(chunk):
@@ -1170,7 +1678,7 @@
     bf16, f32 = jnp.bfloat16, jnp.float32
     dma = pltpu.SemaphoreType.DMA
     last = SHIFTS - 1
-    sums, grad, table = pl.pallas_call(
+    high_sum, proj_sum, grad, table = pl.pallas_call(
         functools.partial(tail_kernel, chunks),
         grid=(-(-(chunks + 4 * SLACK) // BEATS),),
         in_specs=[pl.BlockSpec(memory_space=pltpu.VMEM)] * 6
@@ -1179,11 +1687,13 @@
         + [pl.BlockSpec(memory_space=pltpu.VMEM)],
         out_specs=[
             pl.BlockSpec(memory_space=pl.ANY),
+            pl.BlockSpec(memory_space=pl.ANY),
             pl.BlockSpec(memory_space=pltpu.VMEM),
             pl.BlockSpec(memory_space=pltpu.VMEM),
         ],
         out_shape=[
-            jax.ShapeDtypeStruct((chunks, 2, CHUNK_ROWS, width), bf16),
+            jax.ShapeDtypeStruct((2,) + parts[0].shape[1:], bf16),
+            jax.ShapeDtypeStruct(parts[2].shape[1:], bf16),
             jax.ShapeDtypeStruct((conv_rows, span), f32),
             jax.ShapeDtypeStruct((table_rows, GROUP), f32),
         ],
@@ -1226,16 +1736,11 @@
     )(*conv_operands(ids, vectors), ratio, weights, *parts, small)
     rest = table[vocab:]
     table = table[:vocab].reshape(vocab, SHIFTS, CDIM).sum(axis=1)[:VOCAB]
-    found = []
-    start = 0
-    for part in parts:
-        found.append(sums[start : start + part.shape[1]].reshape(-1, width))
-        start += part.shape[1]
-    return found, grad, table, rest
+    return high_sum.reshape(2, -1, width), proj_sum, grad, table, rest
 
 
 GROUPS = tuple(("high", layer, part) for layer in range(2) for part in range(2)) + (("proj", 0, 0),)
-LOCAL = tuple((item, side) for item in range(3) for side in range(2))
+LOCAL = tuple((item, other) for other in range(2) for item in range(3))
 START_STEPS = len(LOCAL) + 4
 
 
@@ -1251,7 +1756,8 @@
     total_ref,
     vec_ref,
     weight_ref,
-    high_all,
+    high_one,
+    high_two,
     proj_all,
     win_all,
     wst_all,
@@ -1274,6 +1780,8 @@
     ly_recv,
     lc_send,
     lc_recv,
+    lx_send,
+    lx_recv,
 ):
     step = pl.program_id(0)
     dp = lax.axis_index("dp")
@@ -1300,7 +1808,7 @@
     def in_full(index, place, quarter):
         kind, layer, part = GROUPS[index]
         if kind == "high":
-            return high_all.at[layer, quarter, 4 * part + place]
+            return (high_one, high_two)[layer].at[quarter, 4 * part + place]
         return proj_all.at[quarter, place]
 
     def local_full(item, side, quarter):
@@ -1309,13 +1817,30 @@
             return wpr_all.at[side, :, cols]
         return (win_all, wst_all)[item].at[side, quarter]
 
+    def side_of(index):
+        return 1 - near if LOCAL[index][1] else near
+
+    def local_source(index):
+        item, other = LOCAL[index]
+        if other:
+            return local_full(item, 1 - near, dp)
+        return (win_ref, wst_ref, wpr_ref)[item].at[near]
+
+    def lx_copy(item):
+        return remote(
+            (win_ref, wst_ref, wpr_ref)[item].at[1 - near],
+            local_full(item, near, dp),
+            lx_send.at[item],
+            lx_recv.at[item],
+            near_peer,
+        )
+
     def own_pair(index):
         if index < 2:
-            return high_ref.at[index], high_all.at[index, dp]
+            return high_ref.at[index], (high_one, high_two)[index].at[dp]
         if index == 2:
             return proj_ref, proj_all.at[dp]
-        item, side = LOCAL[index - 3]
-        return (win_ref, wst_ref, wpr_ref)[item].at[side], local_full(item, side, dp)
+        return local_source(index - 3), local_full(LOCAL[index - 3][0], side_of(index - 3), dp)
 
     owned = 3 + len(LOCAL)
 
@@ -1356,18 +1881,16 @@
         return remote(ref, ref, c_send.at[index, place], c_recv.at[index, place], core_peer)
 
     def ly_copy(index):
-        item, side = LOCAL[index]
         return remote(
-            (win_ref, wst_ref, wpr_ref)[item].at[side],
-            local_full(item, side, dp),
+            local_source(index),
+            local_full(LOCAL[index][0], side_of(index), dp),
             ly_send.at[index],
             ly_recv.at[index],
             high_peer,
         )
 
     def lc_copy(index):
-        item, side = LOCAL[index]
-        ref = local_full(item, side, across)
+        ref = local_full(LOCAL[index][0], side_of(index), across)
         return remote(ref, ref, lc_send.at[index], lc_recv.at[index], core_peer)
 
     conv_peers = (core_peer, high_peer, both_peer)
@@ -1388,6 +1911,8 @@
         y_copy(0).start()
         y_copy(1).start()
         ly_copy(0).start()
+        for item in range(3):
+            lx_copy(item).start()
         for index in range(2):
             core_copy(index).start()
             own_copy(index).start()
@@ -1437,12 +1962,15 @@
 
             @pl.when(step == index)
             def _():
+                if LOCAL[index][1]:
+                    lx_copy(LOCAL[index][0]).wait_recv()
                 ly_copy(index).start()
 
         @pl.when(step == index + 1)
         def _():
             core_copy(index + 3).start()
-            own_copy(index + 3).start()
+            if not LOCAL[index][1]:
+                own_copy(index + 3).start()
 
         @pl.when(step == index + 3)
         def _():
@@ -1464,8 +1992,11 @@
     @pl.when(step == START_STEPS - 1)
     def _():
         for index in range(owned):
-            own_copy(index).wait()
+            if index < owned - 3:
+                own_copy(index).wait()
             core_copy(index).wait()
+        for item in range(3):
+            lx_copy(item).wait_send()
         for index in range(len(GROUPS)):
             y_copy(index).wait_send()
             x_copy(index).wait_send()
@@ -1490,16 +2021,17 @@
     hbm = pl.BlockSpec(memory_space=pl.ANY)
     dma = pltpu.SemaphoreType.DMA
     count, local = len(GROUPS), len(LOCAL)
-    total, vec, weight, high, proj, win, wst, wpr = pl.pallas_call(
+    total, vec, weight, one, two, proj, win, wst, wpr = pl.pallas_call(
         start_kernel,
         grid=(START_STEPS,),
         in_specs=[vmem] * 8,
-        out_specs=[vmem] * 3 + [hbm] * 5,
+        out_specs=[vmem] * 3 + [hbm] * 6,
         out_shape=[
             jax.ShapeDtypeStruct((tokens, FILTERS), jnp.float32),
             jax.ShapeDtypeStruct((groups, tokens, GROUP), bf16),
             jax.ShapeDtypeStruct((SHIFTS, 2 * GROUP, FILTERS), bf16),
-            jax.ShapeDtypeStruct((2, 4) + highway.shape[1:], bf16),
+            jax.ShapeDtypeStruct((4,) + highway.shape[1:], bf16),
+            jax.ShapeDtypeStruct((4,) + highway.shape[1:], bf16),
             jax.ShapeDtypeStruct((4,) + proj.shape, bf16),
             jax.ShapeDtypeStruct((2, 4) + win.shape[1:], bf16),
             jax.ShapeDtypeStruct((2, 4) + wst.shape[1:], bf16),
@@ -1511,7 +2043,8 @@
         + [dma((count,))] * 4
         + [dma((count, 2))] * 2
         + [dma((count, 4))] * 2
-        + [dma((local,))] * 4,
+        + [dma((local,))] * 4
+        + [dma((3,))] * 2,
         compiler_params=pltpu.CompilerParams(
             collective_id=4, has_side_effects=True, vmem_limit_bytes=40 * 2**20
         ),
@@ -1520,7 +2053,7 @@
         total,
         vec,
         weight,
-        high.reshape(2, 4 * depth, wide),
+        [one.reshape(4 * depth, wide), two.reshape(4 * depth, wide)],
         proj.reshape(4 * rows, PROJ),
         win.reshape(2, PROJ, -1),
         wst.reshape(2, PROJ, -1),
@@ -1545,7 +2078,7 @@
         got = swap(pick(side, 1 - low), axis, 1)
         return (pick(side, low).astype(jnp.float32) + got.astype(jnp.float32)).astype(value.dtype)
 
-    return both(high), swap(both(1 - high), axis, 2)
+    return both(high), both(1 - high)
 
 
 def weight_part(left, right):
@@ -1705,39 +2238,96 @@
         jnp.where(window_doc[:, None] == doc_index[None, :], doc_lengths[None, :], 0), axis=1
     )
     reset_at = (chosen_len - window_offset).astype(jnp.int32)
-    reset_rows = pad_rows(reset_at[:, None], 0).reshape(rows, 1)
-    reset_wide = jnp.broadcast_to(reset_rows, (rows, UNIT_BLOCK))
-    cell_rows = pad_rows(init_cell, 1).reshape(2, rows, cell_local)
-    hidden_rows = pad_rows(init_hidden, 1)
-    kept = lstm_forward(
-        mp_size,
-        embed_all,
-        input_full,
-        state_full,
-        lproj_full,
-        lstm_bias[:, None, :],
-        cell_rows,
-        hidden_rows,
-        reset_wide,
-    )
-    embed_time = kept[0]
-    gates, cprevs, cnews, lows, hprevs, stats, outs = (
-        kept[1 + 2 * index : 3 + 2 * index] for index in range(7)
-    )
-    hidden = jnp.concatenate(
-        [jnp.transpose(drop_rows(value, 1), (1, 0, 2)) for value in outs], axis=-1
-    )
-    own_cot = lax.dynamic_slice_in_dim(cotangent, mp_index * rows_own, rows_own, 0)
-    own_cot = jnp.pad(
-        jnp.transpose(own_cot, (1, 0, 2)), ((0, 0), (0, part_rows - rows_own), (0, 0))
-    )
-    cots = (own_cot[:, :, :PROJ], own_cot[:, :, PROJ:])
-    back = lstm_backward(
-        mp_size, gates, cprevs, cnews, cots, stats, input_full, state_full, lproj_full, reset_wide
-    )
-    das, dss = back[0:2], back[2:4]
-    grad_bias = jnp.sum(back[4], axis=1)
-    grad_embed_local = back[5][:, :rows_own].reshape(tok_share, PROJ)
+    near, ring = mp_index % 2, mp_index // 2
+
+    def by_near(own, got):
+        return jnp.where(near == 0, jnp.stack([own, got]), jnp.stack([got, own]))
+
+    def take(value, index, dim=0):
+        size = value.shape[dim] // 2
+        return lax.dynamic_slice_in_dim(value, index * size, size, dim)
+
+    def to_owner(value):
+        return by_near(
+            take(value, near).reshape(value.shape[1:]),
+            swap(take(value, 1 - near), "mp", 1).reshape(value.shape[1:]),
+        )
+
+    def chains(value, axis):
+        shape = value.shape
+        split = value.reshape(shape[:axis] + (4, 2, rows_own) + shape[axis + 1 :])
+        widths = [(0, 0)] * split.ndim
+        widths[axis + 2] = (0, part_rows - rows_own)
+        split = jnp.moveaxis(jnp.pad(split, widths), axis + 1, 0)
+        return split.reshape((2,) + shape[:axis] + (4 * part_rows,) + shape[axis + 1 :])
+
+    if paired:
+        reset_wide = jnp.broadcast_to(
+            chains(reset_at, 0)[:, :, None], (2, 4 * part_rows, UNIT_BLOCK)
+        )
+        hidden_rows = chains(take(init_hidden, near)[0], 0).reshape(2, 4, part_rows, PROJ)
+        embed_time, gates, cprevs, cnews, lows, hprevs, stats, outs = ring_forward(
+            embed_all.reshape(4, 2, WIN, part_rows, PROJ),
+            input_full,
+            state_full,
+            lproj_full,
+            to_owner(lstm_bias)[:, None, :],
+            chains(to_owner(init_cell), 1),
+            hidden_rows,
+            reset_wide,
+        )
+        hidden = jnp.concatenate(
+            [
+                jnp.transpose(drop_rows(outs[way].reshape(WIN, rows, PROJ), 1), (1, 0, 2))
+                for way in range(2)
+            ],
+            axis=-1,
+        )
+        own_cot = lax.dynamic_slice(
+            cotangent, (ring * 2 * rows_own, 0, near * PROJ), (2 * rows_own, WIN, PROJ)
+        )
+        own_cot = jnp.transpose(own_cot.reshape(2, rows_own, WIN, PROJ), (0, 2, 1, 3))
+        own_cot = jnp.pad(own_cot, ((0, 0), (0, 0), (0, part_rows - rows_own), (0, 0)))
+        das, dss, bias_part, embed_back = ring_backward(
+            gates, cprevs, cnews, own_cot, stats, input_full, state_full, lproj_full, reset_wide
+        )
+        bias_part = jnp.sum(bias_part, axis=0).reshape(2, gate_local)
+        grad_bias = to_owner(bias_part)
+        grad_embed_local = embed_back[:, :rows_own].reshape(tok_share, PROJ)
+    else:
+        reset_rows = pad_rows(reset_at[:, None], 0).reshape(rows, 1)
+        reset_wide = jnp.broadcast_to(reset_rows, (rows, UNIT_BLOCK))
+        cell_rows = pad_rows(init_cell, 1).reshape(2, rows, cell_local)
+        hidden_rows = pad_rows(init_hidden, 1)
+        kept = lstm_forward(
+            mp_size,
+            embed_all,
+            input_full,
+            state_full,
+            lproj_full,
+            lstm_bias[:, None, :],
+            cell_rows,
+            hidden_rows,
+            reset_wide,
+        )
+        embed_time = kept[0]
+        gates, cprevs, cnews, lows, hprevs, stats, outs = (
+            kept[1 + 2 * index : 3 + 2 * index] for index in range(7)
+        )
+        hidden = jnp.concatenate(
+            [jnp.transpose(drop_rows(value, 1), (1, 0, 2)) for value in outs], axis=-1
+        )
+        own_cot = lax.dynamic_slice_in_dim(cotangent, mp_index * rows_own, rows_own, 0)
+        own_cot = jnp.pad(
+            jnp.transpose(own_cot, (1, 0, 2)), ((0, 0), (0, part_rows - rows_own), (0, 0))
+        )
+        cots = (own_cot[:, :, :PROJ], own_cot[:, :, PROJ:])
+        back = lstm_backward(
+            mp_size, gates, cprevs, cnews, cots, stats, input_full, state_full, lproj_full, reset_wide
+        )
+        das, dss = back[0:2], back[2:4]
+        grad_bias = jnp.sum(back[4], axis=1)
+        grad_embed_local = back[5][:, :rows_own].reshape(tok_share, PROJ)
 
     def outer(left, right):
         return jnp.dot(
@@ -1746,6 +2336,29 @@
             preferred_element_type=jnp.float32,
         ).astype(jnp.bfloat16)
 
+    if paired:
+        lstm_parts = [
+            (outer(embed_time, das), 0, 1),
+            (outer(hprevs, das), 0, 1),
+            (outer(lows, dss), 1, 0),
+        ]
+        outers, grad_embed_local = lax.optimization_barrier(
+            ([scatter_start(part, "dp", over) for part, over, _ in lstm_parts], grad_embed_local)
+        )
+        lstm_grads = []
+        for (own, other), (_, _, dim) in zip(outers, lstm_parts):
+            got = swap(other, "dp", 2)
+            sums = [
+                take(own, which, dim).astype(jnp.float32) + take(got, which, dim).astype(jnp.float32)
+                for which in (near, 1 - near)
+            ]
+            lstm_grads.append((sums[0], swap(sums[1].astype(jnp.bfloat16), "mp", 1)))
+    else:
+        lstm_parts = [
+            (outer(left[way], right[way]), dim)
+            for left, right, dim in (((embed_time,) * 2, das, 0), (hprevs, das, 0), (lows, dss, 1))
+            for way in range(2)
+        ]
     grad_pb = jnp.sum(grad_embed_local.astype(jnp.float32), axis=0)
     summed = []
     grad_hb = [None, None]
@@ -1774,12 +2387,6 @@
 
     ratio = jnp.pad(grad_pre_pool / exp_total[:tok_share], ((0, tok_pad), (0, 0)))
     low_mask = tap_mask[:, None, :].astype(jnp.float32)
-    das, dss, _ = lax.optimization_barrier((das, dss, ratio))
-    lstm_parts = [
-        (outer(left[way], right[way]), dim)
-        for left, right, dim in (((embed_time,) * 2, das, 0), (hprevs, das, 0), (lows, dss, 1))
-        for way in range(2)
-    ]
     shared = [grad_cb, jnp.stack(grad_hb), grad_pb]
 
     def flatten(values, unit):
@@ -1794,23 +2401,20 @@
         return pieces
 
     if paired:
-        lstm_parts = [scatter_start(part, "dp", dim) for part, dim in lstm_parts]
         pw_part = weight_part(top_low, grad_embed_local).reshape(2, -1, summed[0].shape[1])
         small = flatten(shared, 8 * UNIT_BLOCK)
         count = small.shape[0]
         small = jnp.concatenate([small, grad_bias.reshape(BIAS_ROWS, UNIT_BLOCK)])
-        (high_one, high_zero, pw_sum), grad_conv, grad_table, rest = conv_backward_and_sum(
+        high_sum, pw_sum, grad_conv, grad_table, rest = conv_backward_and_sum(
             ids_time, char_vecs, ratio, conv_shifted, summed + [pw_part], small
         )
-        lstm_parts, rest = lax.optimization_barrier((lstm_parts, rest))
-        lstm_parts = [
-            own.astype(jnp.float32) + got.astype(jnp.float32) for own, got in lstm_parts
-        ]
+        lstm_grads, rest = lax.optimization_barrier((lstm_grads, rest))
+        lstm_grads = [by_near(own, got.astype(jnp.float32)) for own, got in lstm_grads]
         own_mask = lax.dynamic_slice_in_dim(low_mask, dp_index * dp_width, dp_width, 2)
         grad_cw = grad_conv.reshape(TAPS, CDIM, dp_width) * own_mask
         grad_cb, grad_hbs, grad_pb = unflatten(rest[:count], shared)
         grad_lbias = rest[count:].reshape(grad_bias.shape)
-        grad_hws = jnp.stack([high_zero.astype(jnp.float32), high_one.astype(jnp.float32)])
+        grad_hws = high_sum.astype(jnp.float32)
         grad_pws = pw_sum.reshape(-1, PROJ).astype(jnp.float32)
     else:
         lstm_parts = [
@@ -1827,9 +2431,9 @@
         grad_table, grad_conv, grad_cb, grad_hbs, grad_pb = unflatten(flat, shared)
         grad_cw = lax.dynamic_slice_in_dim(grad_conv, dp_index * dp_width, dp_width, 2)
         grad_lbias = lax.psum(grad_bias, "dp")
-    grad_input, grad_state, grad_lproj = (
-        jnp.stack(lstm_parts[2 * index : 2 * index + 2]) for index in range(3)
-    )
+    if not paired:
+        lstm_grads = [jnp.stack(lstm_parts[2 * index : 2 * index + 2]) for index in range(3)]
+    grad_input, grad_state, grad_lproj = lstm_grads
     return (
         hidden,
         grad_table,

time: 1310 us -> 1150 us (0.88)
  Pallas kernels: 962 us -> 831 us
  local copies, waits for them, and re-layouts: 99.7 us -> 62.1 us
    pallas_call x2, Pallas kernels: 558 us -> 430 us  [the longest x1 227 us: ring_backward(): pl.pallas_call(ring_backward_kernel, grid=(WIN,), in_specs=[block(width),...]
    slice x6 -> x1, local copies, waits for them, and re-layouts: 34.7 us -> 4.88 us  [shards(): outs[way].reshape(WIN, rows, PROJ)]
    convert_element_type x1 -> x4, other arithmetic: 1.16 us -> 19.4 us  [the longest x1 11.8 us: shards(): grad_hws = high_sum.astype(jnp.float32)]
    another operation x9 -> x3, other arithmetic: 18.4 us -> 2.99 us  [by_near(): return jnp.where(near == 0, jnp.stack([own, got]), jnp.stack([got, own]))]
    dot_general x6 -> x3, matrix products: 30.2 us -> 36.9 us  [outer(): jnp.dot(left.reshape(WIN * rows, -1).T, right.reshape(WIN * rows, -1), pr...]
  transfers between devices with their start and end apart: 25 -> 22, of which waited for: 1 -> 2; matrix products, arithmetic and copies ran while one was open for 14% -> 15% of each run, Pallas kernels for 64% -> 23%
where the time goes in v4:
time: 1150 us; the launch traced here: 1130 us
  Pallas kernels  831 us (72%)
  matrix products  119 us (10%)
  other arithmetic  69.6 us (6%)
  local copies, waits for them, and re-layouts  62.1 us (5%)
  waiting for transfers between devices  24.9 us (2%)
  between operations  15.3 us (1%)
  starting transfers between devices  12 us (1%)
    pallas_call x1, Pallas kernels, conv_backward_and_sum(): pl.pallas_call(functools.partial(tail_kernel, chunks), grid=(-(-(chunks +...  263 us
    pallas_call x1, Pallas kernels, ring_backward(): pl.pallas_call(ring_backward_kernel, grid=(WIN,), in_specs=[block(width),...  227 us
    pallas_call x1, Pallas kernels, ring_forward(): pl.pallas_call(ring_forward_kernel, grid=(WIN + 1,), in_specs=[vmem] * 8,...  202 us
    pallas_call x1, Pallas kernels, start_gather(): pl.pallas_call(start_kernel, grid=(START_STEPS,), in_specs=[vmem] * 8, ou...  139 us
    dot_general x3, matrix products, outer(): jnp.dot(left.reshape(WIN * rows, -1).T, right.reshape(WIN * rows, -1), pr...  36.9 us
    dot_general x3, matrix products, weight_part(): jnp.dot(left_all.T, right_all, preferred_element_type=jnp.float32)  32 us
    dot_general x2, matrix products, shards(): jnp.dot(grad_mixed, high_full[layer_index].T, preferred_element_type=jnp....  25.5 us
    all_gather x1, waiting for transfers between devices, shards(): embed_all = lax.all_gather(embed_own, 'mp', axis=0)  24.8 us
  transfers between devices with their start and end apart: 22, of which 2 were waited for; matrix products, arithmetic and copies ran while one was open for 15% of the time, Pallas kernels for 23%

profile of v4, /device:TPU:0, one launch (start us, length us, event | category | flops | bytes accessed | tf_op | source)
XLA Modules:
  0.0 1134.4 jit_solution(9731733130948806677)
XLA Ops:
  10.3 9.1 convert_element_type.298
  22.5 138.9 %shard_map.265 = (f32[288,2048]{1,0:T(8,128)S(1)}, bf16[7,288,128]{2,1,0:T(8,128)(2,1)S(1)}, bf16[8,256,2048]{2,1,0:T(8,128)(2,1)}, bf16[4,8,64,4096]{3,2,1,0:T(...) custom-call(s32[288,50]{1,0:T(8,128)S(1)} %pad.64.clone.ids_ref, ...), custom_call_target="tpu_custom_call" | custom-call | tf_op jit(solution)/shard_map/pallas_call | solution.py:2024
  162.5 11.2 convolution_add_fusion.1
  176.0 9.4 convolution_add_fusion
  219.2 24.8 %all-gather.3.cloned.1.call-done = bf16[160,16,512]{2,1,0:T(8,128)(2,1)} async-done(((bf16[20,16,512]{2,1,0:T(8,128)(2,1)}), bf16[160,16,512]{2,1,0:T(8,128)(2,1)}) %all-gather.3.cloned.1.call-update) | async-done | bytes 2621456 | tf_op jit(solution)/shard_map/all_gather | solution.py:2235
  244.7 202.2 %shard_map.266 = (bf16[20,2,64,512]{3,2,1,0:T(8,128)(2,1)}, f32[20,2,64,4096]{3,2,1,0:T(8,128)}, f32[20,2,64,1024]{3,2,1,0:T(8,128)}, f32[20,2,64,1024]{3,2,1,0:...) custom-call(bf16[4,2,20,16,512]{4,3,2,1,0:T(8,128)(2,1)} %bitcast.15, ...), custom_call_target="tpu_custom_call" | custom-call | tf_op jit(solution)/shard_map/pallas_call | solution.py:771
  446.9 227.5 %shard_map.267 = (bf16[20,2,64,4096]{3,2,1,0:T(8,128)(2,1)}, bf16[20,2,64,512]{3,2,1,0:T(8,128)(2,1)}, f32[8,4096]{1,0:T(8,128)}, bf16[20,16,512]{2,1,0:T(8,128)(2,1)}) custom-call(f32[20,2,64,4096]{3,2,1,0:T(8,128)} %get-tuple-element.61.gate_ref, f32[20,2,64,1024]{3,2,1,0:T(8,128)} %get-tuple-element.62.cprev_ref, ...), custom_call_target="tpu_custom_call" | custom-call | tf_op jit(solution)/shard_map/pallas_call | solution.py:1003
  674.4 4.8 bitcast_convert_fusion.3
  680.2 15.5 %bitcast_convert_fusion.1 = bf16[512,4096]{1,0:T(8,128)(2,1)S(1)} fusion(bf16[20,2,64,512]{3,2,1,0:T(8,128)(2,1)S(1)} %copy-done.50, bf16[20,2,64,4096]{3,2,1,0:T(8,128)(2,1)} %get-tuple-element.65), kind=kOutput, calls=%fused_computation.1 | convolution fusion | flops 10739515392 | bytes 27787264 | tf_op jit(solution)/shard_map/dot_general | solution.py:2333
  699.4 16.6 %bitcast_convert_fusion.2 = bf16[512,4096]{1,0:T(8,128)(2,1)} fusion(bf16[20,2,64,512]{3,2,1,0:T(8,128)(2,1)S(1)} %copy-done.49, bf16[20,2,64,4096]{3,2,1,0:T(8,128)(2,1)} %get-tuple-element.65), kind=kOutput, calls=%fused_computation.2 | convolution fusion | flops 10739515392 | bytes 27787264 | tf_op jit(solution)/shard_map/dot_general | solution.py:2333
  716.8 4.9 fusion.46
  721.7 4.8 reshape.279
  731.7 4.5 pad_maximum_fusion
  738.7 4.5 add_convert_fusion.1
  748.0 3.3 multiply_convert_fusion.3
  754.6 14.5 %multiply_convert_fusion.1 = (bf16[280,2048]{1,0:T(8,128)(2,1)}, bf16[280,2048]{1,0:T(8,128)(2,1)}, f32[280,2048]{1,0:T(8,128)}) fusion(f32[280,4096]{1,0:T(8,128)} %copy-done.12, f32[2048]{0:T(1024)S(1)} %copy-done.45, f32[2048]{0:T(1024)S(1)} %subtract_convert_fusion, f32[288,2048]{1,0:T(8,128)S(1)} %copy-done.4, bf16[2048,4096]{1,0:T(8,128)(2,1)} %bitcast.171, ...), kind=kOutput, calls=%fused_computation.34 | convolution fusion | flops 4719984640 | bytes 35143680 | tf_op jit(solution)/shard_map/dot_general | solution.py:2382
  769.1 3.4 pad_maximum_fusion.2
  772.5 11.1 fusion.47
  790.9 3.1 convolution_convert_fusion.2
  805.8 16.4 %convolution_convert_fusion = bf16[1024,4096]{1,0:T(8,128)(2,1)} fusion(bf16[280,4096]{1,0:T(8,128)(2,1)} %collective-permute-done.11, bf16[280,2048]{1,0:T(8,128)(2,1)S(1)} %copy-done.20, bf16[280,2048]{1,0:T(8,128)(2,1)S(1)} %copy-done.18, bf16[280,1024]{1,0:T(8,128)(2,1)} %collective-permute-done.10, bf16[280,512]{1,0:T(8,128)(2,1)S(1)} %copy-done.39, ...), kind=kOutput, calls=%fused_computation.3 | convolution fusion | flops 4719017984 | bytes 14123008 | tf_op jit(solution)/shard_map/dot_general | solution.py:2101
  822.3 12.5 %convolution_convert_fusion.1 = bf16[1024,4096]{1,0:T(8,128)(2,1)} fusion(bf16[280,4096]{1,0:T(8,128)(2,1)} %collective-permute-done.9, bf16[280,2048]{1,0:T(8,128)(2,1)S(1)} %copy-done.16, bf16[280,2048]{1,0:T(8,128)(2,1)S(1)} %copy-done.14, bf16[280,1024]{1,0:T(8,128)(2,1)S(1)} %collective-permute-done.8, bf16[280,512]{1,0:T(8,128)(2,1)S(1)} %copy-done.37, ...), kind=kOutput, calls=%fused_computation.4 | convolution fusion | flops 4719017984 | bytes 14123008 | tf_op jit(solution)/shard_map/dot_general | solution.py:2101
  834.8 262.7 %shard_map.268 = (bf16[2,16,2,16,4096]{4,3,2,1,0:T(8,128)(2,1)}, bf16[2,2,16,4096]{3,2,1,0:T(8,128)(2,1)}, f32[112,512]{1,0:T(8,128)}, f32[384,128]{1,0:T(8,128)}) custom-call(s32[8,1728]{1,0:T(8,128)} %reshape.282.hot_ref, s32[2,288]{1,0:T(2,128)} %slice.121.hot_extra_ref, bf16[7,288,128]{2,1,0:T(8,128)(2,1)} %copy-done.6, ...), custom_call_target="tpu_custom_call" | custom-call | tf_op jit(solution)/shard_map/pallas_call | solution.py:1681
  1103.4 11.8 %bitcast_convert_fusion = f32[2,512,4096]{2,1,0:T(8,128)} fusion(bf16[2,16,2,16,4096]{4,3,2,1,0:T(8,128)(2,1)} %get-tuple-element.82), kind=kLoop, calls=%fused_computation | loop fusion | flops 4194304 | bytes 25165824 | tf_op jit(solution)/shard_map/convert_element_type | solution.py:2417
  1123.3 4.1 maximum_select_fusion
  (273 shorter events, 97.6 us)
Async XLA Ops:
  7.2 186.0 %copy-start = (bf16[2,112,512]{2,1,0:T(8,128)(2,1)S(1)}, bf16[2,112,512]{2,1,0:T(8,128)(2,1)}, u32[]{:S(2)}) copy-start(bf16[2,112,512]{2,1,0:T(8,128)(2,1)} %param.34) | copy-start | bytes 688132
  7.2 236.8 %all-gather.3.cloned.1.call-start = ((), (), s32[]{:S(2)}) async-start(), calls=%async_computation | async-start | bytes 2949120 | tf_op jit(solution)/shard_map/all_gather | solution.py:2235
  191.0 25.3 %collective-permute-start.1 = (f32[1,112,512]{2,1,0:T(8,128)}, f32[1,112,512]{2,1,0:T(8,128)}, u32[]{:S(2)}, u32[]{:S(2)}) collective-permute-start(f32[1,112,512]{2,1,0:T(8,128)} %get-tuple-element.133), channel_id=1, source_target_pairs={{0,1},{1,0},{2,3},{3,2},{4,5},{5,4},{6,7},{7,6},{8,9},{9,8},{10,11... | collective-permute-start | bytes 688136 | tf_op jit(solution)/shard_map/ppermute | solution.py:2066
  191.8 23.9 %collective-permute-start = (f32[1,2048]{1,0:T(1,128)S(1)}, f32[1,2048]{1,0:T(1,128)S(1)}, u32[]{:S(2)}, u32[]{:S(2)}) collective-permute-start(f32[1,2048]{1,0:T(1,128)S(1)} %get-tuple-element.139), channel_id=1, source_target_pairs={{0,1},{1,0},{2,3},{3,2},{4,5},{5,4},{6,7},{7,6},{8,9},{9,8},{10,11... | collective-permute-start | bytes 24584 | tf_op jit(solution)/shard_map/ppermute | solution.py:2066
  446.9 227.5 %copy-start.48 = (bf16[20,2,64,1024]{3,2,1,0:T(8,128)(2,1)S(1)}, bf16[20,2,64,1024]{3,2,1,0:T(8,128)(2,1)}, u32[]{:S(2)}) copy-start(bf16[20,2,64,1024]{3,2,1,0:T(8,128)(2,1)} %get-tuple-element.67) | copy-start | bytes 15728644
  679.3 57.2 %collective-permute-start.6 = (bf16[1024,128]{1,0:T(8,128)(2,1)S(1)}, bf16[1024,128]{1,0:T(8,128)(2,1)}, u32[]{:S(2)}, u32[]{:S(2)}) collective-permute-start(bf16[1024,128]{1,0:T(8,128)(2,1)S(1)} %get-tuple-element.127), channel_id=1, source_target_pairs={{0,8},{8,0},{16,24},{24,16},{1,9},{9,1},{17,25},{25,17},{2,10},{10... | collective-permute-start | bytes 786440 | tf_op jit(solution)/shard_map/ppermute | solution.py:2066
  679.4 57.6 %collective-permute-start.7 = (bf16[1024,128]{1,0:T(8,128)(2,1)S(1)}, bf16[1024,128]{1,0:T(8,128)(2,1)}, u32[]{:S(2)}, u32[]{:S(2)}) collective-permute-start(bf16[1024,128]{1,0:T(8,128)(2,1)S(1)} %get-tuple-element.126), channel_id=1, source_target_pairs={{0,8},{8,0},{16,24},{24,16},{1,9},{9,1},{17,25},{25,17},{2,10},{10... | collective-permute-start | bytes 786440 | tf_op jit(solution)/shard_map/ppermute | solution.py:2066
  697.2 41.4 %collective-permute-start.4 = (bf16[128,4096]{1,0:T(8,128)(2,1)}, bf16[128,4096]{1,0:T(8,128)(2,1)}, u32[]{:S(2)}, u32[]{:S(2)}) collective-permute-start(bf16[128,4096]{1,0:T(8,128)(2,1)} %get-tuple-element.101), channel_id=1, source_target_pairs={{0,8},{8,0},{16,24},{24,16},{1,9},{9,1},{17,25},{25,17},{2,10},{10... | collective-permute-start | bytes 3145736 | tf_op jit(solution)/shard_map/ppermute | solution.py:2066
  697.2 41.4 %collective-permute-start.5 = (bf16[128,4096]{1,0:T(8,128)(2,1)}, bf16[128,4096]{1,0:T(8,128)(2,1)}, u32[]{:S(2)}, u32[]{:S(2)}) collective-permute-start(bf16[128,4096]{1,0:T(8,128)(2,1)} %get-tuple-element.100), channel_id=1, source_target_pairs={{0,8},{8,0},{16,24},{24,16},{1,9},{9,1},{17,25},{25,17},{2,10},{10... | collective-permute-start | bytes 3145736 | tf_op jit(solution)/shard_map/ppermute | solution.py:2066
  716.1 20.2 %collective-permute-start.14 = (f32[1,2048]{1,0:T(1,128)S(1)}, f32[1,2048]{1,0:T(1,128)S(1)}, u32[]{:S(2)}, u32[]{:S(2)}) collective-permute-start(f32[1,2048]{1,0:T(1,128)S(1)} %get-tuple-element.137), channel_id=1, source_target_pairs={{0,1},{1,0},{2,3},{3,2},{4,5},{5,4},{6,7},{7,6},{8,9},{9,8},{10,11... | collective-permute-start | bytes 24584 | tf_op jit(solution)/shard_map/ppermute | solution.py:2066
  736.3 49.2 %collective-permute-start.12 = (bf16[280,1024]{1,0:T(8,128)(2,1)}, bf16[280,1024]{1,0:T(8,128)(2,1)}, u32[]{:S(2)}, u32[]{:S(2)}) collective-permute-start(bf16[280,1024]{1,0:T(8,128)(2,1)} %pad_maximum_fusion.6), channel_id=1, source_target_pairs={{0,8},{8,0},{16,24},{24,16},{1,9},{9,1},{17,25},{25,17},{2,10},{10... | collective-permute-start | bytes 1720328 | tf_op jit(solution)/shard_map/ppermute | solution.py:2066
  736.5 6.7 collective-permute-start.2
  737.1 6.1 collective-permute-start.3
  745.3 40.9 %collective-permute-start.19 = (bf16[1024,128]{1,0:T(8,128)(2,1)S(1)}, bf16[1024,128]{1,0:T(8,128)(2,1)}, u32[]{:S(2)}, u32[]{:S(2)}) collective-permute-start(bf16[1024,128]{1,0:T(8,128)(2,1)S(1)} %get-tuple-element.80), channel_id=1, source_target_pairs={{0,16},{8,24},{16,0},{24,8},{1,17},{9,25},{17,1},{25,9},{2,18},{10... | collective-permute-start | bytes 786440 | tf_op jit(solution)/shard_map/ppermute | solution.py:2066
  745.9 50.4 %collective-permute-start.17 = (bf16[128,4096]{1,0:T(8,128)(2,1)}, bf16[128,4096]{1,0:T(8,128)(2,1)}, u32[]{:S(2)}, u32[]{:S(2)}) collective-permute-start(bf16[128,4096]{1,0:T(8,128)(2,1)} %get-tuple-element.78), channel_id=1, source_target_pairs={{0,16},{8,24},{16,0},{24,8},{1,17},{9,25},{17,1},{25,9},{2,18},{10... | collective-permute-start | bytes 3145736 | tf_op jit(solution)/shard_map/ppermute | solution.py:2066
  747.3 52.3 %collective-permute-start.15 = (bf16[128,4096]{1,0:T(8,128)(2,1)}, bf16[128,4096]{1,0:T(8,128)(2,1)}, u32[]{:S(2)}, u32[]{:S(2)}) collective-permute-start(bf16[128,4096]{1,0:T(8,128)(2,1)} %get-tuple-element.76), channel_id=1, source_target_pairs={{0,16},{8,24},{16,0},{24,8},{1,17},{9,25},{17,1},{25,9},{2,18},{10... | collective-permute-start | bytes 3145736 | tf_op jit(solution)/shard_map/ppermute | solution.py:2066
  772.5 32.1 %collective-permute-start.11 = (bf16[280,4096]{1,0:T(8,128)(2,1)}, bf16[280,4096]{1,0:T(8,128)(2,1)}, u32[]{:S(2)}, u32[]{:S(2)}) collective-permute-start(bf16[280,4096]{1,0:T(8,128)(2,1)} %pad_maximum_fusion.2), channel_id=1, source_target_pairs={{0,8},{8,0},{16,24},{24,16},{1,9},{9,1},{17,25},{25,17},{2,10},{10... | collective-permute-start | bytes 6881288 | tf_op jit(solution)/shard_map/ppermute | solution.py:2066
  785.6 36.7 %collective-permute-start.9 = (bf16[280,4096]{1,0:T(8,128)(2,1)}, bf16[280,4096]{1,0:T(8,128)(2,1)}, u32[]{:S(2)}, u32[]{:S(2)}) collective-permute-start(bf16[280,4096]{1,0:T(8,128)(2,1)} %pad_maximum_fusion.1), channel_id=1, source_target_pairs={{0,8},{8,0},{16,24},{24,16},{1,9},{9,1},{17,25},{25,17},{2,10},{10... | collective-permute-start | bytes 6881288 | tf_op jit(solution)/shard_map/ppermute | solution.py:2066
  786.3 4.2 collective-permute-start.13
  790.5 13.3 %collective-permute-start.10 = (bf16[280,1024]{1,0:T(8,128)(2,1)}, bf16[280,1024]{1,0:T(8,128)(2,1)}, u32[]{:S(2)}, u32[]{:S(2)}) collective-permute-start(bf16[280,1024]{1,0:T(8,128)(2,1)} %pad_maximum_fusion.5), channel_id=1, source_target_pairs={{0,8},{8,0},{16,24},{24,16},{1,9},{9,1},{17,25},{25,17},{2,10},{10... | collective-permute-start | bytes 1720328 | tf_op jit(solution)/shard_map/ppermute | solution.py:2066
  796.3 25.9 %collective-permute-start.8 = (bf16[280,1024]{1,0:T(8,128)(2,1)S(1)}, bf16[280,1024]{1,0:T(8,128)(2,1)S(1)}, u32[]{:S(2)}, u32[]{:S(2)}) collective-permute-start(bf16[280,1024]{1,0:T(8,128)(2,1)S(1)} %copy-done.32), channel_id=1, source_target_pairs={{0,8},{8,0},{16,24},{24,16},{1,9},{9,1},{17,25},{25,17},{2,10},{10... | collective-permute-start | bytes 1720328 | tf_op jit(solution)/shard_map/ppermute | solution.py:2066
  799.7 298.6 %collective-permute-start.20 = (bf16[512,128]{1,0:T(8,128)(2,1)}, bf16[512,128]{1,0:T(8,128)(2,1)S(1)}, u32[]{:S(2)}, u32[]{:S(2)}) collective-permute-start(bf16[512,128]{1,0:T(8,128)(2,1)} %get-tuple-element.130), channel_id=1, source_target_pairs={{0,1},{1,0},{2,3},{3,2},{4,5},{5,4},{6,7},{7,6},{8,9},{9,8},{10,11... | collective-permute-start | bytes 393224 | tf_op jit(solution)/shard_map/ppermute | solution.py:2066
  803.8 294.5 %collective-permute-start.18 = (bf16[128,2048]{1,0:T(8,128)(2,1)}, bf16[128,2048]{1,0:T(8,128)(2,1)}, u32[]{:S(2)}, u32[]{:S(2)}) collective-permute-start(bf16[128,2048]{1,0:T(8,128)(2,1)} %get-tuple-element.108), channel_id=1, source_target_pairs={{0,1},{1,0},{2,3},{3,2},{4,5},{5,4},{6,7},{7,6},{8,9},{9,8},{10,11... | collective-permute-start | bytes 1572872 | tf_op jit(solution)/shard_map/ppermute | solution.py:2066
  804.5 293.8 %collective-permute-start.16 = (bf16[128,2048]{1,0:T(8,128)(2,1)}, bf16[128,2048]{1,0:T(8,128)(2,1)}, u32[]{:S(2)}, u32[]{:S(2)}) collective-permute-start(bf16[128,2048]{1,0:T(8,128)(2,1)} %get-tuple-element.110), channel_id=1, source_target_pairs={{0,1},{1,0},{2,3},{3,2},{4,5},{5,4},{6,7},{7,6},{8,9},{9,8},{10,11... | collective-permute-start | bytes 1572872 | tf_op jit(solution)/shard_map/ppermute | solution.py:2066
  (55 other events, 503.5 us)
Sparse Core Ops, SparseCore 0:
  190.4 53.5 all-gather.2

commit v5 on v4

--- a/solution.py
+++ b/solution.py
@@ -1909,8 +1909,6 @@
         for index in range(3):
             conv_copy(index).start()
         y_copy(0).start()
-        y_copy(1).start()
-        ly_copy(0).start()
         for item in range(3):
             lx_copy(item).start()
         for index in range(2):
@@ -1934,13 +1932,13 @@
                     quarter * span : (quarter + 1) * span,
                 ] = part
 
-    for index in range(len(GROUPS)):
+    for index in reversed(range(len(GROUPS))):
 
         @pl.when(step == index + 1)
         def _():
             y_copy(index).wait_recv()
-            if index + 2 < len(GROUPS):
-                y_copy(index + 2).start()
+            if index + 1 < len(GROUPS):
+                y_copy(index + 1).start()
             x_copy(index).start()
             z_copy(index, near).start()
             c_copy(index, mine).start()
@@ -1958,16 +1956,11 @@
                 c_copy(index, beyond + which).start()
 
     for index in range(len(LOCAL)):
-        if index:
-
-            @pl.when(step == index)
-            def _():
-                if LOCAL[index][1]:
-                    lx_copy(LOCAL[index][0]).wait_recv()
-                ly_copy(index).start()
-
         @pl.when(step == index + 1)
         def _():
+            if LOCAL[index][1]:
+                lx_copy(LOCAL[index][0]).wait_recv()
+            ly_copy(index).start()
             core_copy(index + 3).start()
             if not LOCAL[index][1]:
                 own_copy(index + 3).start()

time: 1150 us -> 1140 us (level)
  no operation moved by 1% of the time
where the time goes in v5:
time: 1140 us; the launch traced here: 1130 us
  Pallas kernels  820 us (72%)
  matrix products  119 us (10%)
  other arithmetic  69.8 us (6%)
  local copies, waits for them, and re-layouts  62.1 us (5%)
  waiting for transfers between devices  26.5 us (2%)
  between operations  15.3 us (1%)
  starting transfers between devices  14.3 us (1%)
    pallas_call x1, Pallas kernels, conv_backward_and_sum(): pl.pallas_call(functools.partial(tail_kernel, chunks), grid=(-(-(chunks +...  263 us
    pallas_call x1, Pallas kernels, ring_backward(): pl.pallas_call(ring_backward_kernel, grid=(WIN,), in_specs=[block(width),...  226 us
    pallas_call x1, Pallas kernels, ring_forward(): pl.pallas_call(ring_forward_kernel, grid=(WIN + 1,), in_specs=[vmem] * 8,...  201 us
    pallas_call x1, Pallas kernels, start_gather(): pl.pallas_call(start_kernel, grid=(START_STEPS,), in_specs=[vmem] * 8, ou...  131 us
    dot_general x3, matrix products, outer(): jnp.dot(left.reshape(WIN * rows, -1).T, right.reshape(WIN * rows, -1), pr...  36.9 us
    dot_general x3, matrix products, weight_part(): jnp.dot(left_all.T, right_all, preferred_element_type=jnp.float32)  32 us
    all_gather x1, waiting for transfers between devices, shards(): embed_all = lax.all_gather(embed_own, 'mp', axis=0)  26.4 us
    dot_general x2, matrix products, shards(): jnp.dot(grad_mixed, high_full[layer_index].T, preferred_element_type=jnp....  25.5 us
  transfers between devices with their start and end apart: 22, of which 2 were waited for; matrix products, arithmetic and copies ran while one was open for 15% of the time, Pallas kernels for 23%

profile of v5, /device:TPU:0, one launch (start us, length us, event | category | flops | bytes accessed | tf_op | source)
XLA Modules:
  0.0 1127.5 jit_solution(12183261098499309653)
XLA Ops:
  10.3 9.1 convert_element_type.298
  22.5 130.8 %shard_map.265 = (f32[288,2048]{1,0:T(8,128)S(1)}, bf16[7,288,128]{2,1,0:T(8,128)(2,1)S(1)}, bf16[8,256,2048]{2,1,0:T(8,128)(2,1)}, bf16[4,8,64,4096]{3,2,1,0:T(...) custom-call(s32[288,50]{1,0:T(8,128)S(1)} %pad.64.clone.ids_ref, ...), custom_call_target="tpu_custom_call" | custom-call | tf_op jit(solution)/shard_map/pallas_call | solution.py:2017
  154.3 11.2 convolution_add_fusion.1
  167.9 9.4 convolution_add_fusion
  211.3 26.4 %all-gather.3.cloned.1.call-done = bf16[160,16,512]{2,1,0:T(8,128)(2,1)} async-done(((bf16[20,16,512]{2,1,0:T(8,128)(2,1)}), bf16[160,16,512]{2,1,0:T(8,128)(2,1)}) %all-gather.3.cloned.1.call-update) | async-done | bytes 2621456 | tf_op jit(solution)/shard_map/all_gather | solution.py:2228
  238.4 200.9 %shard_map.266 = (bf16[20,2,64,512]{3,2,1,0:T(8,128)(2,1)}, f32[20,2,64,4096]{3,2,1,0:T(8,128)}, f32[20,2,64,1024]{3,2,1,0:T(8,128)}, f32[20,2,64,1024]{3,2,1,0:...) custom-call(bf16[4,2,20,16,512]{4,3,2,1,0:T(8,128)(2,1)} %bitcast.15, ...), custom_call_target="tpu_custom_call" | custom-call | tf_op jit(solution)/shard_map/pallas_call | solution.py:771
  439.3 225.9 %shard_map.267 = (bf16[20,2,64,4096]{3,2,1,0:T(8,128)(2,1)}, bf16[20,2,64,512]{3,2,1,0:T(8,128)(2,1)}, f32[8,4096]{1,0:T(8,128)}, bf16[20,16,512]{2,1,0:T(8,128)(2,1)}) custom-call(f32[20,2,64,4096]{3,2,1,0:T(8,128)} %get-tuple-element.61.gate_ref, f32[20,2,64,1024]{3,2,1,0:T(8,128)} %get-tuple-element.62.cprev_ref, ...), custom_call_target="tpu_custom_call" | custom-call | tf_op jit(solution)/shard_map/pallas_call | solution.py:1003
  665.3 4.8 bitcast_convert_fusion.3
  671.1 15.5 %bitcast_convert_fusion.1 = bf16[512,4096]{1,0:T(8,128)(2,1)S(1)} fusion(bf16[20,2,64,512]{3,2,1,0:T(8,128)(2,1)S(1)} %copy-done.50, bf16[20,2,64,4096]{3,2,1,0:T(8,128)(2,1)} %get-tuple-element.65), kind=kOutput, calls=%fused_computation.1 | convolution fusion | flops 10739515392 | bytes 27787264 | tf_op jit(solution)/shard_map/dot_general | solution.py:2326
  690.2 16.6 %bitcast_convert_fusion.2 = bf16[512,4096]{1,0:T(8,128)(2,1)} fusion(bf16[20,2,64,512]{3,2,1,0:T(8,128)(2,1)S(1)} %copy-done.49, bf16[20,2,64,4096]{3,2,1,0:T(8,128)(2,1)} %get-tuple-element.65), kind=kOutput, calls=%fused_computation.2 | convolution fusion | flops 10739515392 | bytes 27787264 | tf_op jit(solution)/shard_map/dot_general | solution.py:2326
  708.6 4.9 fusion.46
  713.4 4.8 reshape.279
  723.5 4.5 pad_maximum_fusion
  730.4 4.5 add_convert_fusion.1
  741.8 3.3 multiply_convert_fusion.3
  748.5 14.5 %multiply_convert_fusion.1 = (bf16[280,2048]{1,0:T(8,128)(2,1)}, bf16[280,2048]{1,0:T(8,128)(2,1)}, f32[280,2048]{1,0:T(8,128)}) fusion(f32[280,4096]{1,0:T(8,128)} %copy-done.12, f32[2048]{0:T(1024)S(1)} %copy-done.45, f32[2048]{0:T(1024)S(1)} %subtract_convert_fusion, f32[288,2048]{1,0:T(8,128)S(1)} %copy-done.4, bf16[2048,4096]{1,0:T(8,128)(2,1)} %bitcast.171, ...), kind=kOutput, calls=%fused_computation.34 | convolution fusion | flops 4719984640 | bytes 35143680 | tf_op jit(solution)/shard_map/dot_general | solution.py:2375
  763.0 3.4 pad_maximum_fusion.2
  766.3 11.1 fusion.47
  784.7 3.1 convolution_convert_fusion.2
  799.1 16.4 %convolution_convert_fusion = bf16[1024,4096]{1,0:T(8,128)(2,1)} fusion(bf16[280,4096]{1,0:T(8,128)(2,1)} %collective-permute-done.11, bf16[280,2048]{1,0:T(8,128)(2,1)S(1)} %copy-done.20, bf16[280,2048]{1,0:T(8,128)(2,1)S(1)} %copy-done.18, bf16[280,1024]{1,0:T(8,128)(2,1)} %collective-permute-done.10, bf16[280,512]{1,0:T(8,128)(2,1)S(1)} %copy-done.39, ...), kind=kOutput, calls=%fused_computation.3 | convolution fusion | flops 4719017984 | bytes 14123008 | tf_op jit(solution)/shard_map/dot_general | solution.py:2094
  815.5 12.5 %convolution_convert_fusion.1 = bf16[1024,4096]{1,0:T(8,128)(2,1)} fusion(bf16[280,4096]{1,0:T(8,128)(2,1)} %collective-permute-done.9, bf16[280,2048]{1,0:T(8,128)(2,1)S(1)} %copy-done.16, bf16[280,2048]{1,0:T(8,128)(2,1)S(1)} %copy-done.14, bf16[280,1024]{1,0:T(8,128)(2,1)S(1)} %collective-permute-done.8, bf16[280,512]{1,0:T(8,128)(2,1)S(1)} %copy-done.37, ...), kind=kOutput, calls=%fused_computation.4 | convolution fusion | flops 4719017984 | bytes 14123008 | tf_op jit(solution)/shard_map/dot_general | solution.py:2094
  828.0 262.6 %shard_map.268 = (bf16[2,16,2,16,4096]{4,3,2,1,0:T(8,128)(2,1)}, bf16[2,2,16,4096]{3,2,1,0:T(8,128)(2,1)}, f32[112,512]{1,0:T(8,128)}, f32[384,128]{1,0:T(8,128)}) custom-call(s32[8,1728]{1,0:T(8,128)} %reshape.282.hot_ref, s32[2,288]{1,0:T(2,128)} %slice.121.hot_extra_ref, bf16[7,288,128]{2,1,0:T(8,128)(2,1)} %copy-done.6, ...), custom_call_target="tpu_custom_call" | custom-call | tf_op jit(solution)/shard_map/pallas_call | solution.py:1681
  1096.6 11.8 %bitcast_convert_fusion = f32[2,512,4096]{2,1,0:T(8,128)} fusion(bf16[2,16,2,16,4096]{4,3,2,1,0:T(8,128)(2,1)} %get-tuple-element.82), kind=kLoop, calls=%fused_computation | loop fusion | flops 4194304 | bytes 25165824 | tf_op jit(solution)/shard_map/convert_element_type | solution.py:2410
  1116.4 4.1 maximum_select_fusion
  (273 shorter events, 100.2 us)
Async XLA Ops:
  7.2 178.1 %copy-start = (bf16[2,112,512]{2,1,0:T(8,128)(2,1)S(1)}, bf16[2,112,512]{2,1,0:T(8,128)(2,1)}, u32[]{:S(2)}) copy-start(bf16[2,112,512]{2,1,0:T(8,128)(2,1)} %param.34) | copy-start | bytes 688132
  7.2 230.5 %all-gather.3.cloned.1.call-start = ((), (), s32[]{:S(2)}) async-start(), calls=%async_computation | async-start | bytes 2949120 | tf_op jit(solution)/shard_map/all_gather | solution.py:2228
  182.9 25.6 %collective-permute-start.1 = (f32[1,112,512]{2,1,0:T(8,128)}, f32[1,112,512]{2,1,0:T(8,128)}, u32[]{:S(2)}, u32[]{:S(2)}) collective-permute-start(f32[1,112,512]{2,1,0:T(8,128)} %get-tuple-element.133), channel_id=1, source_target_pairs={{0,1},{1,0},{2,3},{3,2},{4,5},{5,4},{6,7},{7,6},{8,9},{9,8},{10,11... | collective-permute-start | bytes 688136 | tf_op jit(solution)/shard_map/ppermute | solution.py:2059
  185.2 22.7 %collective-permute-start = (f32[1,2048]{1,0:T(1,128)S(1)}, f32[1,2048]{1,0:T(1,128)S(1)}, u32[]{:S(2)}, u32[]{:S(2)}) collective-permute-start(f32[1,2048]{1,0:T(1,128)S(1)} %get-tuple-element.139), channel_id=1, source_target_pairs={{0,1},{1,0},{2,3},{3,2},{4,5},{5,4},{6,7},{7,6},{8,9},{9,8},{10,11... | collective-permute-start | bytes 24584 | tf_op jit(solution)/shard_map/ppermute | solution.py:2059
  439.3 225.9 %copy-start.48 = (bf16[20,2,64,1024]{3,2,1,0:T(8,128)(2,1)S(1)}, bf16[20,2,64,1024]{3,2,1,0:T(8,128)(2,1)}, u32[]{:S(2)}) copy-start(bf16[20,2,64,1024]{3,2,1,0:T(8,128)(2,1)} %get-tuple-element.67) | copy-start | bytes 15728644
  670.2 58.1 %collective-permute-start.6 = (bf16[1024,128]{1,0:T(8,128)(2,1)S(1)}, bf16[1024,128]{1,0:T(8,128)(2,1)}, u32[]{:S(2)}, u32[]{:S(2)}) collective-permute-start(bf16[1024,128]{1,0:T(8,128)(2,1)S(1)} %get-tuple-element.127), channel_id=1, source_target_pairs={{0,8},{8,0},{16,24},{24,16},{1,9},{9,1},{17,25},{25,17},{2,10},{10... | collective-permute-start | bytes 786440 | tf_op jit(solution)/shard_map/ppermute | solution.py:2059
  670.3 58.5 %collective-permute-start.7 = (bf16[1024,128]{1,0:T(8,128)(2,1)S(1)}, bf16[1024,128]{1,0:T(8,128)(2,1)}, u32[]{:S(2)}, u32[]{:S(2)}) collective-permute-start(bf16[1024,128]{1,0:T(8,128)(2,1)S(1)} %get-tuple-element.126), channel_id=1, source_target_pairs={{0,8},{8,0},{16,24},{24,16},{1,9},{9,1},{17,25},{25,17},{2,10},{10... | collective-permute-start | bytes 786440 | tf_op jit(solution)/shard_map/ppermute | solution.py:2059
  688.1 42.3 %collective-permute-start.4 = (bf16[128,4096]{1,0:T(8,128)(2,1)}, bf16[128,4096]{1,0:T(8,128)(2,1)}, u32[]{:S(2)}, u32[]{:S(2)}) collective-permute-start(bf16[128,4096]{1,0:T(8,128)(2,1)} %get-tuple-element.101), channel_id=1, source_target_pairs={{0,8},{8,0},{16,24},{24,16},{1,9},{9,1},{17,25},{25,17},{2,10},{10... | collective-permute-start | bytes 3145736 | tf_op jit(solution)/shard_map/ppermute | solution.py:2059
  688.1 42.3 %collective-permute-start.5 = (bf16[128,4096]{1,0:T(8,128)(2,1)}, bf16[128,4096]{1,0:T(8,128)(2,1)}, u32[]{:S(2)}, u32[]{:S(2)}) collective-permute-start(bf16[128,4096]{1,0:T(8,128)(2,1)} %get-tuple-element.100), channel_id=1, source_target_pairs={{0,8},{8,0},{16,24},{24,16},{1,9},{9,1},{17,25},{25,17},{2,10},{10... | collective-permute-start | bytes 3145736 | tf_op jit(solution)/shard_map/ppermute | solution.py:2059
  707.0 21.1 %collective-permute-start.14 = (f32[1,2048]{1,0:T(1,128)S(1)}, f32[1,2048]{1,0:T(1,128)S(1)}, u32[]{:S(2)}, u32[]{:S(2)}) collective-permute-start(f32[1,2048]{1,0:T(1,128)S(1)} %get-tuple-element.137), channel_id=1, source_target_pairs={{0,1},{1,0},{2,3},{3,2},{4,5},{5,4},{6,7},{7,6},{8,9},{9,8},{10,11... | collective-permute-start | bytes 24584 | tf_op jit(solution)/shard_map/ppermute | solution.py:2059
  728.1 51.3 %collective-permute-start.12 = (bf16[280,1024]{1,0:T(8,128)(2,1)}, bf16[280,1024]{1,0:T(8,128)(2,1)}, u32[]{:S(2)}, u32[]{:S(2)}) collective-permute-start(bf16[280,1024]{1,0:T(8,128)(2,1)} %pad_maximum_fusion.6), channel_id=1, source_target_pairs={{0,8},{8,0},{16,24},{24,16},{1,9},{9,1},{17,25},{25,17},{2,10},{10... | collective-permute-start | bytes 1720328 | tf_op jit(solution)/shard_map/ppermute | solution.py:2059
  728.2 6.7 collective-permute-start.2
  728.8 6.1 collective-permute-start.3
  737.0 43.1 %collective-permute-start.19 = (bf16[1024,128]{1,0:T(8,128)(2,1)S(1)}, bf16[1024,128]{1,0:T(8,128)(2,1)}, u32[]{:S(2)}, u32[]{:S(2)}) collective-permute-start(bf16[1024,128]{1,0:T(8,128)(2,1)S(1)} %get-tuple-element.80), channel_id=1, source_target_pairs={{0,16},{8,24},{16,0},{24,8},{1,17},{9,25},{17,1},{25,9},{2,18},{10... | collective-permute-start | bytes 786440 | tf_op jit(solution)/shard_map/ppermute | solution.py:2059
  739.8 50.4 %collective-permute-start.17 = (bf16[128,4096]{1,0:T(8,128)(2,1)}, bf16[128,4096]{1,0:T(8,128)(2,1)}, u32[]{:S(2)}, u32[]{:S(2)}) collective-permute-start(bf16[128,4096]{1,0:T(8,128)(2,1)} %get-tuple-element.78), channel_id=1, source_target_pairs={{0,16},{8,24},{16,0},{24,8},{1,17},{9,25},{17,1},{25,9},{2,18},{10... | collective-permute-start | bytes 3145736 | tf_op jit(solution)/shard_map/ppermute | solution.py:2059
  739.8 53.7 %collective-permute-start.15 = (bf16[128,4096]{1,0:T(8,128)(2,1)}, bf16[128,4096]{1,0:T(8,128)(2,1)}, u32[]{:S(2)}, u32[]{:S(2)}) collective-permute-start(bf16[128,4096]{1,0:T(8,128)(2,1)} %get-tuple-element.76), channel_id=1, source_target_pairs={{0,16},{8,24},{16,0},{24,8},{1,17},{9,25},{17,1},{25,9},{2,18},{10... | collective-permute-start | bytes 3145736 | tf_op jit(solution)/shard_map/ppermute | solution.py:2059
  766.3 31.9 %collective-permute-start.11 = (bf16[280,4096]{1,0:T(8,128)(2,1)}, bf16[280,4096]{1,0:T(8,128)(2,1)}, u32[]{:S(2)}, u32[]{:S(2)}) collective-permute-start(bf16[280,4096]{1,0:T(8,128)(2,1)} %pad_maximum_fusion.2), channel_id=1, source_target_pairs={{0,8},{8,0},{16,24},{24,16},{1,9},{9,1},{17,25},{25,17},{2,10},{10... | collective-permute-start | bytes 6881288 | tf_op jit(solution)/shard_map/ppermute | solution.py:2059
  779.4 36.1 %collective-permute-start.9 = (bf16[280,4096]{1,0:T(8,128)(2,1)}, bf16[280,4096]{1,0:T(8,128)(2,1)}, u32[]{:S(2)}, u32[]{:S(2)}) collective-permute-start(bf16[280,4096]{1,0:T(8,128)(2,1)} %pad_maximum_fusion.1), channel_id=1, source_target_pairs={{0,8},{8,0},{16,24},{24,16},{1,9},{9,1},{17,25},{25,17},{2,10},{10... | collective-permute-start | bytes 6881288 | tf_op jit(solution)/shard_map/ppermute | solution.py:2059
  780.1 4.2 collective-permute-start.13
  784.3 12.7 %collective-permute-start.10 = (bf16[280,1024]{1,0:T(8,128)(2,1)}, bf16[280,1024]{1,0:T(8,128)(2,1)}, u32[]{:S(2)}, u32[]{:S(2)}) collective-permute-start(bf16[280,1024]{1,0:T(8,128)(2,1)} %pad_maximum_fusion.5), channel_id=1, source_target_pairs={{0,8},{8,0},{16,24},{24,16},{1,9},{9,1},{17,25},{25,17},{2,10},{10... | collective-permute-start | bytes 1720328 | tf_op jit(solution)/shard_map/ppermute | solution.py:2059
  790.2 25.3 %collective-permute-start.8 = (bf16[280,1024]{1,0:T(8,128)(2,1)S(1)}, bf16[280,1024]{1,0:T(8,128)(2,1)S(1)}, u32[]{:S(2)}, u32[]{:S(2)}) collective-permute-start(bf16[280,1024]{1,0:T(8,128)(2,1)S(1)} %copy-done.32), channel_id=1, source_target_pairs={{0,8},{8,0},{16,24},{24,16},{1,9},{9,1},{17,25},{25,17},{2,10},{10... | collective-permute-start | bytes 1720328 | tf_op jit(solution)/shard_map/ppermute | solution.py:2059
  793.5 297.9 %collective-permute-start.20 = (bf16[512,128]{1,0:T(8,128)(2,1)}, bf16[512,128]{1,0:T(8,128)(2,1)S(1)}, u32[]{:S(2)}, u32[]{:S(2)}) collective-permute-start(bf16[512,128]{1,0:T(8,128)(2,1)} %get-tuple-element.130), channel_id=1, source_target_pairs={{0,1},{1,0},{2,3},{3,2},{4,5},{5,4},{6,7},{7,6},{8,9},{9,8},{10,11... | collective-permute-start | bytes 393224 | tf_op jit(solution)/shard_map/ppermute | solution.py:2059
  797.0 294.4 %collective-permute-start.18 = (bf16[128,2048]{1,0:T(8,128)(2,1)}, bf16[128,2048]{1,0:T(8,128)(2,1)}, u32[]{:S(2)}, u32[]{:S(2)}) collective-permute-start(bf16[128,2048]{1,0:T(8,128)(2,1)} %get-tuple-element.108), channel_id=1, source_target_pairs={{0,1},{1,0},{2,3},{3,2},{4,5},{5,4},{6,7},{7,6},{8,9},{9,8},{10,11... | collective-permute-start | bytes 1572872 | tf_op jit(solution)/shard_map/ppermute | solution.py:2059
  798.3 293.2 %collective-permute-start.16 = (bf16[128,2048]{1,0:T(8,128)(2,1)}, bf16[128,2048]{1,0:T(8,128)(2,1)}, u32[]{:S(2)}, u32[]{:S(2)}) collective-permute-start(bf16[128,2048]{1,0:T(8,128)(2,1)} %get-tuple-element.110), channel_id=1, source_target_pairs={{0,1},{1,0},{2,3},{3,2},{4,5},{5,4},{6,7},{7,6},{8,9},{9,8},{10,11... | collective-permute-start | bytes 1572872 | tf_op jit(solution)/shard_map/ppermute | solution.py:2059
  (55 other events, 503.1 us)
Sparse Core Ops, SparseCore 0:
  182.2 55.4 all-gather.2
